TPU v7x, 32 devices: a whole 2x2x4 slice. The times are simulated.
32 devices in a mesh: grp: 4 (over z), dev: 8 (over y, x, core).
Axes of the slice: x: 2, y: 2, z: 4, core: 2. Of those that a mesh axis runs over, the one named last changes fastest.
Arguments:
- omega: float32 [4, 32, 256, 128], P('grp', 'dev'), may hold values from -6 to 6
- u_factor: float32 [4, 32, 80, 256, 32], P('grp', 'dev'), may hold values from -0.0625 to 0.0625
- v_factor: float32 [4, 32, 80, 256, 32], P('grp', 'dev'), may hold values from -0.375 to 0.375
- columns: int32 [4, 32, 80, 1], P('grp', 'dev'), may hold values from 0 to 31; in each aligned block of 320 rows (0 to 319, 320 to 639, ..., all dimensions but the last counted through in order) at most 11 rows name the same one
- ranks: int32 [4, 32, 80], P('grp', 'dev'), may hold values from 8 to 32
Outputs:
- leaf_basis: float32 [32, 256, 128], P('dev', 'grp')
- transfer: float32 [32, 256, 128], P('dev')
Inputs may be any that keep to these rules, and one draw needn't show every extreme that they name: `columns`: within the 320 blocks of one device's row clusters in one group, at most 11 name any one column cluster, and some column cluster is named by exactly 11.
All inputs are finite; a program needn't handle non-finite values.
Results may differ from a plain program's by a relative error of at most 0.0003.
Values sent between devices are 32-bit elements; how exact they have to be, the bound alone decides.
No kernel may reach another device: no remote copies, remote signals or barrier semaphores. Data moves between devices by JAX's collectives and lax.ppermute only.
A program may use at most 192 MiB of HBM per device.

v0:
```python
import jax
import jax.numpy as jnp
from jax import lax
from jax.sharding import PartitionSpec as P

precise = lax.Precision.HIGHEST


def swapped(value, axis, apart):
    mask = 2**apart
    pairs = [(source, source ^ mask) for source in range(lax.axis_size(axis))]
    return lax.ppermute(value, axis, pairs)


def on_device(omega, u_factor, v_factor, columns, ranks):
    n_local = u_factor.shape[1]
    n_blocks = u_factor.shape[2]
    leaf_rows = u_factor.shape[3]
    rank_width = u_factor.shape[4]
    probe_count = omega.shape[3]
    dev_count = lax.axis_size("dev")
    grp_count = lax.axis_size("grp")
    col_flat = columns[0, :, :, 0].reshape(n_local * n_blocks)
    v_flat = v_factor[0].reshape(n_local * n_blocks, leaf_rows, rank_width)
    whole_probe = lax.all_gather(omega, "dev", axis=1, tiled=True)[0]
    coeff = jnp.einsum("bik,bip->bkp", v_flat, whole_probe[col_flat], precision=precise)
    rank_mask = (
        jnp.arange(rank_width, dtype=jnp.int32)[None, None, :] < ranks[0][:, :, None]
    ).astype(jnp.float32)
    masked_rows = u_factor[0] * rank_mask[:, :, None, :]
    partial_sketch = jnp.einsum(
        "cbik,cbkp->cip",
        masked_rows,
        coeff.reshape(n_local, n_blocks, rank_width, probe_count),
        precision=precise,
    )
    quarter = leaf_rows // grp_count
    total_sketch = lax.psum(partial_sketch, "grp")
    gram_matrix = jnp.einsum("cip,ciq->cpq", total_sketch, total_sketch, precision=precise)
    own_rows = lax.dynamic_slice_in_dim(total_sketch, lax.axis_index("grp") * quarter, quarter, 1)
    pair_gram = gram_matrix[0::2] + gram_matrix[1::2]
    top_gram = pair_gram[0] + pair_gram[1]
    device_index = lax.axis_index("dev")
    tree_bits = dev_count.bit_length() - 1
    identity = jnp.eye(probe_count, dtype=jnp.float32)
    keep_left = identity
    keep_right = identity
    owned = device_index < 0
    current = top_gram
    for depth_step in range(tree_bits):
        sibling = swapped(current, "dev", depth_step)
        is_left = device_index // 2**depth_step % 2 == 0
        left_gram = jnp.where(is_left, current, sibling)
        right_gram = jnp.where(is_left, sibling, current)
        owner = device_index % 2 ** (depth_step + 1) == 2**depth_step - 1
        keep_left = jnp.where(owner, left_gram, keep_left)
        keep_right = jnp.where(owner, right_gram, keep_right)
        owned = jnp.logical_or(owned, owner)
        current = left_gram + right_gram
    all_grams = jnp.concatenate(
        [
            gram_matrix,
            pair_gram,
            top_gram[None],
            keep_left[None],
            keep_right[None],
            (keep_left + keep_right)[None],
        ],
        axis=0,
    )
    all_lower = jnp.linalg.cholesky(all_grams)
    all_upper = jnp.swapaxes(all_lower, 1, 2)
    leaf_basis = lax.linalg.triangular_solve(
        all_lower[0:4], own_rows, left_side=False, lower=True, transpose_a=True
    )
    left_parts = jnp.stack([all_upper[0], all_upper[2], all_upper[4], all_upper[7]], axis=0)
    right_parts = jnp.stack([all_upper[1], all_upper[3], all_upper[5], all_upper[8]], axis=0)
    parent_lower = jnp.stack([all_lower[4], all_lower[5], all_lower[6], all_lower[9]], axis=0)
    stacked_rows = jnp.concatenate([left_parts, right_parts], axis=1)
    node_transfer = lax.linalg.triangular_solve(
        parent_lower, stacked_rows, left_side=False, lower=True, transpose_a=True
    )
    kept = jnp.where(owned, node_transfer[3], jnp.zeros_like(node_transfer[3]))
    transfer = jnp.stack([node_transfer[0], node_transfer[1], node_transfer[2], kept], axis=0)
    return (leaf_basis, transfer)


def solution(mesh):
    placed = (
        P("grp", "dev", None, None),
        P("grp", "dev", None, None, None),
        P("grp", "dev", None, None, None),
        P("grp", "dev", None, None),
        P("grp", "dev", None),
    )
    return jax.shard_map(
        on_device,
        mesh=mesh,
        in_specs=placed,
        out_specs=(P("dev", "grp", None), P("dev", None, None)),
        check_vma=False,
    )
```

profile of v0, /device:TPU:0, one launch (start us, length us, event | category | flops | bytes accessed | tf_op | source)
XLA Modules:
  0.0 378.6 jit_solution(2373997758977308243)
XLA Ops:
  7.2 0.7 all-gather.2.cloned.1.call-update
  7.9 0.5 broadcast.113
  8.5 1.3 reduce.11
  9.9 0.8 fusion.24
  10.7 38.5 %all-gather.2.cloned.1.call-done = f32[1,32,256,128]{3,2,0,1:T(8,128)} async-done(((f32[1,4,256,128]{3,2,0,1:T(8,128)}), f32[1,32,256,128]{3,2,0,1:T(8,128)}) %all-gather.2.cloned.1.call-update) | async-done | bytes 4194320 | tf_op jit(solution)/shard_map/all_gather | solution.py:25
  49.2 19.8 %gather_fusion = f32[320,256,128]{2,1,0:T(8,128)} fusion(f32[32,256,128]{2,1,0:T(8,128)} %bitcast.51, s32[1024]{0:T(1024)S(1)} %pad_clamp_fusion), kind=kCustom, calls=%fused_computation | custom fusion | bytes 83887360 | tf_op jit(solution)/shard_map/gather | solution.py:26
  69.0 31.4 %fusion.40 = f32[320,128,32]{1,2,0:T(8,128)S(1)} fusion(f32[320,256,128]{2,1,0:T(8,128)} %gather_fusion, f32[320,256,32]{1,2,0:T(8,128)} %bitcast.52), kind=kOutput, calls=%fused_computation.68 | convolution fusion | flops 4026531840 | bytes 57671680 | tf_op jit(solution)/shard_map/bik,bip->bkp/dot_general | solution.py:26
  100.4 18.9 %fusion.2 = f32[4,256,128]{2,1,0:T(8,128)} fusion(f32[4,80,32,128]{3,2,1,0:T(8,128)S(1)} %bitcast.53, f32[1,4,80,256,32]{3,4,2,1,0:T(8,128)S(1)} %copy-done, f32[4,80,32]{2,1,0:T(8,128)S(1)} %fusion.24), kind=kOutput, calls=%fused_computation.4 | convolution fusion | flops 4029153280 | bytes 16293888 | tf_op jit(solution)/shard_map/cbik,cbkp->cip/dot_general | solution.py:31
  119.4 38.7 %all-reduce.2.cloned.1.call-done = f32[4,256,128]{2,1,0:T(8,128)} async-done(((f32[4,256,128]{2,1,0:T(8,128)}), f32[4,256,128]{2,1,0:T(8,128)}) %all-reduce.2.cloned.1.call-update) | async-done | bytes 524304 | tf_op jit(solution)/shard_map/psum | solution.py:38
  158.0 2.2 constant_dynamic-update-slice_fusion.1
  160.5 1.2 collective-permute-done
  161.6 1.5 collective-permute-start.1
  163.3 2.6 collective-permute-done.1
  166.0 1.5 collective-permute-start.2
  167.5 2.8 collective-permute-done.2
  170.4 0.2 copy.40
  170.7 117.2 %custom-call.10 = f32[10,128,128]{2,1,0:T(8,128)S(1)} custom-call(f32[10,128,128]{2,1,0:T(8,128)S(1)} %fusion.3), custom_call_target="Cholesky" | custom-call | tf_op jit(solution)/shard_map/jit(cholesky)/cholesky | solution.py:71
  288.1 0.1 select_select_fusion
  288.3 0.1 fusion.46
  288.5 39.6 %custom-call.11 = f32[4,1,128,128]{2,3,1,0:T(8,128)S(1)} custom-call(f32[4,1,128,128]{3,2,1,0:T(8,128)S(1)} %fusion.20), custom_call_target="InvertDiagBlocksLowerTriangular" | custom-call | tf_op jit(solution)/shard_map/triangular_solve | solution.py:73
  328.1 39.3 %custom-call.12 = f32[4,1,128,128]{2,3,1,0:T(8,128)S(1)} custom-call(f32[4,1,128,128]{3,2,1,0:T(8,128)S(1)} %maximum_select_fusion), custom_call_target="InvertDiagBlocksLowerTriangular" | custom-call | tf_op jit(solution)/shard_map/triangular_solve | solution.py:80
  367.5 1.0 fusion.4
  368.6 0.8 pad_maximum_fusion
  369.4 1.9 fusion.22
  (29 shorter events, 1.0 us)
Async XLA Ops:
  7.2 42.0 %all-gather.2.cloned.1.call-start = ((), (), s32[]{:S(2)}) async-start(), calls=%async_computation | async-start | bytes 4718592 | tf_op jit(solution)/shard_map/all_gather | solution.py:25
  7.9 150.1 %all-reduce.2.cloned.1.call-start = ((), (), s32[]{:S(2)}) async-start(), calls=%async_computation.1 | async-start | bytes 1048576 | tf_op jit(solution)/shard_map/psum | solution.py:38
  69.0 31.4 %copy-start = (f32[1,4,80,256,32]{3,4,2,1,0:T(8,128)S(1)}, f32[1,4,80,256,32]{3,4,2,1,0:T(8,128)}, u32[]{:S(2)}) copy-start(f32[1,4,80,256,32]{3,4,2,1,0:T(8,128)} %param.6) | copy-start | bytes 31457284
  160.3 1.3 collective-permute-start
  161.6 4.3 %collective-permute-start.1 = (f32[128,128]{0,1:T(8,128)S(1)}, f32[128,128]{0,1:T(8,128)S(1)}, u32[]{:S(2)}, u32[]{:S(2)}) collective-permute-start(f32[128,128]{0,1:T(8,128)S(1)} %fusion.30), channel_id=1, source_target_pairs={{0,2},{1,3},{2,0},{3,1},{4,6},{5,7},{6,4},{7,5},{8,10},{9,11},{10,... | collective-permute-start | bytes 196616 | tf_op jit(solution)/shard_map/ppermute | solution.py:12
  166.0 4.3 %collective-permute-start.2 = (f32[128,128]{0,1:T(8,128)S(1)}, f32[128,128]{0,1:T(8,128)S(1)}, u32[]{:S(2)}, u32[]{:S(2)}) collective-permute-start(f32[128,128]{0,1:T(8,128)S(1)} %fusion.31), channel_id=1, source_target_pairs={{0,4},{1,5},{2,6},{3,7},{4,0},{5,1},{6,2},{7,3},{8,12},{9,13},{10,... | collective-permute-start | bytes 196616 | tf_op jit(solution)/shard_map/ppermute | solution.py:12
Sparse Core Ops, SparseCore 0:
  9.9 39.2 all-gather.1
  119.5 38.4 all-reduce.1
where the time goes:
time: 385 us; the launch traced here: 379 us
  other arithmetic  200 us (52%)
  waiting for transfers between devices  84.4 us (22%)
  matrix products  55.5 us (14%)
  local copies, waits for them, and re-layouts  20.8 us (5%)
  between operations  14.8 us (4%)
    another operation x4, other arithmetic, on_device(): all_lower = jnp.linalg.cholesky(all_grams)  117 us
    another operation x3, other arithmetic, on_device(): lax.linalg.triangular_solve(all_lower[0:4], own_rows, left_side=False, lo...  39.6 us
    another operation x2, other arithmetic, on_device(): lax.linalg.triangular_solve(parent_lower, stacked_rows, left_side=False,...  39.3 us
    psum x1, waiting for transfers between devices, on_device(): total_sketch = lax.psum(partial_sketch, 'grp')  38.7 us
    all_gather x1, waiting for transfers between devices, on_device(): whole_probe = lax.all_gather(omega, 'dev', axis=1, tiled=True)[0]  38.5 us
    dot_general x1, matrix products, on_device(): jnp.einsum('bik,bip->bkp', v_flat, whole_probe[col_flat], precision=precise)  31.4 us
    gather x1, local copies, waits for them, and re-layouts, on_device(): whole_probe[col_flat]  19.8 us
    dot_general x1, matrix products, on_device(): jnp.einsum('cbik,cbkp->cip', masked_rows, coeff.reshape(n_local, n_blocks...  18.9 us
  transfers between devices with their start and end apart: 5, of which 5 were waited for; matrix products, arithmetic and copies ran while one was open for 1% of the time, Pallas kernels for 0%

commit v1 on v0

v1 whole, which is shorter than its diff:
```python
import functools

import jax
import jax.numpy as jnp
from jax import lax
from jax.experimental import pallas as pl
from jax.experimental.pallas import tpu as pltpu
from jax.sharding import PartitionSpec as P


f32 = jnp.float32
bf16 = jnp.bfloat16
VM = pl.BlockSpec(memory_space=pltpu.VMEM)
SM = pl.BlockSpec(memory_space=pltpu.SMEM)


def swapped(value, axis, mask):
    pairs = [(source, source ^ mask) for source in range(lax.axis_size(axis))]
    return lax.ppermute(value, axis, pairs)


def split(x):
    high = x.astype(bf16)
    low = (x - high.astype(f32)).astype(bf16)
    return high, low


def dot_full(x, y, dims):
    return lax.dot_general(
        x, y, (dims, ((), ())), precision=lax.Precision.HIGHEST, preferred_element_type=f32
    )


def table_kernel(order, unit, n_local, cols_ref, ranks_ref, slot_ref):
    n_leaf, _, n_blocks = cols_ref.shape
    depth, clusters = slot_ref.shape
    position = lax.broadcasted_iota(jnp.int32, (clusters, 1), 0)
    names = jnp.zeros((clusters, 1), jnp.int32)
    for at, cluster in enumerate(order):
        names = jnp.where(position == at, cluster, names)
    names = jnp.bitwise_xor(names, lax.axis_index("dev") * n_local)
    ones = jnp.ones((n_blocks, n_blocks), bf16)
    si = lax.broadcasted_iota(jnp.int32, (n_blocks, n_blocks), 0)
    li = lax.broadcasted_iota(jnp.int32, (n_blocks, n_blocks), 1)
    before = jnp.where(si < li, 1.0, 0.0).astype(bf16)
    number = lax.broadcasted_iota(jnp.int32, (depth, n_blocks), 1).astype(f32)
    level = lax.broadcasted_iota(jnp.int32, (depth, n_blocks), 0).astype(f32)
    offset = jnp.zeros((clusters, n_blocks), f32)
    index = jnp.zeros((depth, clusters), f32)
    rank = jnp.zeros((depth, clusters), f32)
    used = jnp.zeros((depth, clusters), f32)
    for c in range(n_leaf):
        named = jnp.where(cols_ref[c] == names, 1.0, 0.0)
        named_low = named.astype(bf16)

        def listed(x, named_low=named_low):
            return lax.dot_general(
                x.astype(bf16), named_low, (((1,), (1,)), ((), ())), preferred_element_type=f32
            )

        ahead = offset + jnp.dot(named_low, before, preferred_element_type=f32)
        place = jnp.sum(named * ahead, axis=0, keepdims=True)
        mark = jnp.where(place == level, 1.0, 0.0)
        here = listed(mark)
        index = index + listed(mark * number) + here * float(c * n_blocks)
        rank = rank + listed(mark * ranks_ref[c : c + 1, :].astype(f32))
        used = used + here
        offset = offset + jnp.dot(named_low, ones, preferred_element_type=f32)
    index = jnp.where(used > 0.5, index, float(n_leaf * n_blocks))
    slot_ref[...] = index.astype(jnp.int32) * unit + rank.astype(jnp.int32)


def slot_table(order, cols, ranks, depth, unit, n_local):
    return pl.pallas_call(
        functools.partial(table_kernel, order, unit, n_local),
        out_shape=jax.ShapeDtypeStruct((depth, len(order)), jnp.int32),
        in_specs=[VM, VM],
        out_specs=VM,
        compiler_params=pltpu.CompilerParams(vmem_limit_bytes=4 << 20),
        cost_estimate=pl.CostEstimate(flops=0, bytes_accessed=24 << 20, transcendentals=0),
        name="slots",
    )(cols, ranks)


def coeff_kernel(most, start, unit, n_pieces, *refs):
    slot_ref, v_ref = refs[:2]
    pieces = refs[2 : 2 + n_pieces]
    c_ref, w_ref = refs[-2:]
    p = pieces[0].shape[2]
    n_all, k, _ = v_ref.shape
    at = 0
    for piece in pieces:
        for q in range(piece.shape[0]):
            high, low = split(piece[q])
            w_ref[at, :, :p] = high
            w_ref[at, :, p:] = low
            at += 1
    sub = lax.broadcasted_iota(jnp.int32, (k, p), 0)

    def body(j, _):
        highs, lows, ids, kept = [], [], [], []
        for n in range(most):
            entry = slot_ref[n, start + j]
            b = entry // unit
            ids.append(b)
            kept.append(sub < entry % unit)
            high, low = split(v_ref[jnp.minimum(b, n_all - 1)])
            highs.append(high)
            lows.append(low)
        w = w_ref[j]
        both = jnp.dot(jnp.concatenate(highs, 0), w, preferred_element_type=f32)
        both = both + jnp.dot(jnp.concatenate(lows, 0), w, preferred_element_type=f32)
        total = both[:, :p] + both[:, p:]
        for n in range(most):
            c_ref[ids[n]] = jnp.where(kept[n], total[n * k : (n + 1) * k], 0.0)
        return 0

    lax.fori_loop(0, at, body, 0, unroll=2)


def coefficients(slots, v, pieces, start, most, unit, before):
    n_all, k, rows = v.shape
    p = pieces[0].shape[2]
    held = sum(piece.shape[0] for piece in pieces)
    chained = before is not None
    args = [slots, v, *pieces] + ([before] if chained else [])
    return pl.pallas_call(
        functools.partial(coeff_kernel, most, start, unit, len(pieces)),
        out_shape=jax.ShapeDtypeStruct((n_all + 1, k, p), f32),
        in_specs=[SM, VM] + [VM] * len(pieces) + [VM] * chained,
        out_specs=VM,
        scratch_shapes=[pltpu.VMEM((held, rows, 2 * p), bf16)],
        input_output_aliases={len(args) - 1: 0} if chained else {},
        compiler_params=pltpu.CompilerParams(vmem_limit_bytes=8 << 20),
        cost_estimate=pl.CostEstimate(
            flops=held * most * k * rows * p * 8, bytes_accessed=8 << 20, transcendentals=0
        ),
        name="coeff",
    )(*args)


def sketch_kernel(m, n_blocks, c_ref, u_ref, o_ref):
    p, rows = o_ref.shape
    k = u_ref.shape[1]
    step = rows // k
    leaf = jnp.bitwise_xor(lax.axis_index("grp"), m)
    total = jnp.zeros((p, rows), f32)
    for q in range(n_blocks // step):
        at = pl.ds(leaf * n_blocks + q * step, step)
        high, low = split(c_ref[at].reshape(rows, p).T)
        u_high, u_low = split(u_ref[at].reshape(rows, rows))
        total = total + jnp.dot(high, u_high, preferred_element_type=f32)
        total = total + jnp.dot(low, u_high, preferred_element_type=f32)
        total = total + jnp.dot(high, u_low, preferred_element_type=f32)
    o_ref[...] = total


def sketch(coeff, u, m, n_blocks):
    k, rows = u.shape[1:]
    p = coeff.shape[2]
    return pl.pallas_call(
        functools.partial(sketch_kernel, m, n_blocks),
        out_shape=jax.ShapeDtypeStruct((p, rows), f32),
        in_specs=[VM, VM],
        out_specs=VM,
        compiler_params=pltpu.CompilerParams(vmem_limit_bytes=8 << 20),
        cost_estimate=pl.CostEstimate(
            flops=n_blocks * k * rows * p * 6, bytes_accessed=1 << 20, transcendentals=0
        ),
        name="sketch",
    )(coeff, u)


def gram_kernel(n_terms, *refs):
    terms = refs[:n_terms]
    near_ref, far_ref, keep_ref, hold_ref = refs[n_terms:]
    total = terms[0][...]
    for term in terms[1:]:
        total = total + term[...]
    gram = dot_full(total, total, ((1,), (1,)))
    hold_ref[...] = total.T
    p = gram.shape[0]
    quarter = keep_ref.shape[0]

    def rows_of(m):
        at = pl.multiple_of(jnp.bitwise_xor(lax.axis_index("grp"), m) * quarter, quarter)
        return hold_ref[pl.ds(at, quarter), :]

    keep_ref[...] = rows_of(0)
    near_ref[:quarter] = rows_of(1)
    near_ref[quarter : quarter + p] = gram
    near_ref[quarter + p :] = rows_of(3)
    far_ref[:p] = gram
    far_ref[p:] = rows_of(2)


def gram_of(terms, n_grp):
    p, rows = terms[0].shape
    quarter = rows // n_grp
    return pl.pallas_call(
        functools.partial(gram_kernel, len(terms)),
        out_shape=(
            jax.ShapeDtypeStruct((p + 2 * quarter, p), f32),
            jax.ShapeDtypeStruct((p + quarter, p), f32),
            jax.ShapeDtypeStruct((quarter, p), f32),
        ),
        in_specs=[VM] * len(terms),
        out_specs=(VM, VM, VM),
        scratch_shapes=[pltpu.VMEM((rows, p), f32)],
        compiler_params=pltpu.CompilerParams(vmem_limit_bytes=8 << 20),
        name="gram",
    )(*terms)


def tree_kernel(panel, n_leaf, n_levels, *refs):
    grams = refs[:n_leaf]
    rows_in = refs[n_leaf : 2 * n_leaf]
    lefts = refs[2 * n_leaf : 2 * n_leaf + n_levels]
    rights = refs[2 * n_leaf + n_levels : 2 * n_leaf + 2 * n_levels]
    basis_ref, tr_ref, m_ref = refs[2 * n_leaf + 2 * n_levels :]
    count, p, _ = m_ref.shape
    own = lax.axis_index("grp")
    device = lax.axis_index("dev")
    ri = lax.broadcasted_iota(jnp.int32, (p, p), 0)
    ci = lax.broadcasted_iota(jnp.int32, (p, p), 1)
    for m in range(n_leaf):
        m_ref[jnp.bitwise_xor(own, m)] = grams[m][...]
    identity = jnp.where(ri == ci, 1.0, 0.0)
    m_ref[7] = identity
    m_ref[8] = identity
    for level in range(n_levels):

        @pl.when(device % 2 ** (level + 1) == 2**level - 1)
        def _(level=level):
            m_ref[7] = lefts[level][...]
            m_ref[8] = rights[level][...]

    m_ref[4] = m_ref[0] + m_ref[1]
    m_ref[5] = m_ref[2] + m_ref[3]
    m_ref[6] = m_ref[4] + m_ref[5]
    m_ref[9] = m_ref[7] + m_ref[8]
    lane = lax.broadcasted_iota(jnp.int32, (1, 1, p), 2)
    sub8 = lax.broadcasted_iota(jnp.int32, (1, 8, p), 1)
    n_panels = p // panel
    n_tiles = panel // 8
    for pn in range(n_panels):
        base = pn * panel
        x = [m_ref[:, base + 8 * i : base + 8 * i + 8, :] for i in range(n_tiles)]
        for t in range(panel):
            i0, ts = t // 8, t % 8
            k = base + t
            columns = [jnp.broadcast_to(x[i][:, :, k : k + 1], x[i].shape) for i in range(i0, n_tiles)]
            scale = lax.rsqrt(columns[0][:, ts : ts + 1, :])
            hit = lane == k
            row = jnp.where(hit, 1.0, x[i0][:, ts : ts + 1, :]) * scale
            for i in range(i0, n_tiles):
                new = jnp.where(hit, 0.0, x[i]) - (columns[i - i0] * scale) * row
                if i == i0:
                    new = jnp.where(sub8 < ts, x[i], jnp.where(sub8 == ts, row, new))
                x[i] = new
        for i in range(n_tiles):
            m_ref[:, base + 8 * i : base + 8 * i + 8, :] = x[i]
        if pn < n_panels - 1:
            after = base + panel
            for b in range(count):
                block = m_ref[b, base:after, :]
                si = lax.broadcasted_iota(jnp.int32, block.shape, 0)
                li = lax.broadcasted_iota(jnp.int32, block.shape, 1)
                right = jnp.where((li < after) & (li - base > si), 0.0, block)
                change = dot_full(block.T[after:, :], right, ((1,), (0,)))
                old = m_ref[b, after:, :]
                lj = lax.broadcasted_iota(jnp.int32, old.shape, 1)
                old = jnp.where((lj >= base) & (lj < after), 0.0, old)
                m_ref[b, after:, :] = old - change

    def inverse(b):
        return jnp.where(ci <= ri, m_ref[b], 0.0)

    def upper(b):
        whole = m_ref[b]
        return jnp.where(ci > ri, whole, jnp.where(ci == ri, 1.0 / whole, 0.0))

    for m in range(n_leaf):
        leaf = jnp.bitwise_xor(own, m)
        basis_ref[leaf] = dot_full(rows_in[m][...], inverse(leaf), ((1,), (1,)))
    keep = device != lax.axis_size("dev") - 1
    for q, (a, b, node) in enumerate(((0, 1, 4), (2, 3, 5), (4, 5, 6), (7, 8, 9))):
        solve = inverse(node)
        top = dot_full(upper(a), solve, ((1,), (1,)))
        bottom = dot_full(upper(b), solve, ((1,), (1,)))
        if q == 3:
            top = jnp.where(keep, top, 0.0)
            bottom = jnp.where(keep, bottom, 0.0)
        tr_ref[q, :p] = top
        tr_ref[q, p:] = bottom


def tree(grams, rows_in, lefts, rights, panel=32):
    quarter, p = rows_in[0].shape
    n_leaf = len(grams)
    arrays = [*grams, *rows_in, *lefts, *rights]
    return pl.pallas_call(
        functools.partial(tree_kernel, panel, n_leaf, len(lefts)),
        out_shape=(
            jax.ShapeDtypeStruct((n_leaf, quarter, p), f32),
            jax.ShapeDtypeStruct((4, 2 * p, p), f32),
        ),
        in_specs=[VM] * len(arrays),
        out_specs=(VM, VM),
        scratch_shapes=[pltpu.VMEM((10, p, p), f32)],
        compiler_params=pltpu.CompilerParams(vmem_limit_bytes=16 << 20),
        name="tree",
    )(*arrays)


def gathered(omega, dev_count):
    n_local = omega.shape[0]
    half = n_local // 2
    masks = [2**bit for bit in range(1, dev_count.bit_length() - 1)]
    waves = {}
    for order, first in ((masks, 0), (masks[::-1], half)):
        held = [(0, 0, omega[first : first + half])]
        for place, mask in enumerate(order):
            new = [
                (max(level, place) + (seen > 0), seen ^ mask, value) for level, seen, value in held
            ]
            for at, (level, seen, value) in enumerate(new):
                new[at] = (level, seen, swapped(value, "dev", mask))
            for level, seen, value in new:
                waves.setdefault(level, []).append((seen, first, value))
            held = held + new
    other = swapped(omega, "dev", 1)
    order = [mask * n_local + q for mask in (0, 1) for q in range(n_local)]
    groups = [[omega, other]]
    for level in sorted(waves):
        wave = waves[level]
        for flip in (0, 1):
            for seen, first, value in wave:
                order.extend((seen ^ flip) * n_local + first + q for q in range(half))

        values = [value for _, _, value in wave]
        groups.append(values + [swapped(value, "dev", 1) for value in values])
    return groups, order


def on_device(omega, u_factor, v_factor, columns, ranks):
    n_local, n_blocks = u_factor.shape[1:3]
    leaf_rows, width = u_factor.shape[3:]
    p = omega.shape[3]
    dev_count = lax.axis_size("dev")
    grp_count = lax.axis_size("grp")
    assert n_local == grp_count == 4
    clusters = n_local * dev_count
    most = -(-11 * n_local * n_blocks // (10 * clusters))
    v = jnp.swapaxes(v_factor[0], 2, 3).reshape(n_local * n_blocks, width, leaf_rows)
    u = jnp.swapaxes(u_factor[0], 2, 3).reshape(n_local * n_blocks, width, leaf_rows)
    groups, order = gathered(omega[0], dev_count)
    depth = -(-most // 8) * 8
    unit = 2 * width
    columns = jnp.swapaxes(columns[0], 1, 2)
    slots = slot_table(tuple(order), columns, ranks[0], depth, unit, n_local)
    coeff = None
    start = 0
    for pieces in groups:
        coeff = coefficients(slots, v, pieces, start, most, unit, coeff)
        start += sum(piece.shape[0] for piece in pieces)
    across = swapped(sketch(coeff, u, 3, n_blocks), "grp", 1)
    beside = swapped(sketch(coeff, u, 1, n_blocks), "grp", 1)
    across = swapped(sketch(coeff, u, 2, n_blocks) + across, "grp", 2)
    near, far, rows_own = gram_of([sketch(coeff, u, 0, n_blocks), beside, across], grp_count)
    quarter = rows_own.shape[0]
    far_in = swapped(far, "grp", 2)
    near_in = swapped(near, "grp", 1)
    pass_in = swapped(near_in[quarter:], "grp", 2)
    grams = [far[:p], near_in[quarter : quarter + p], far_in[:p], pass_in[:p]]
    rows_in = [rows_own, near_in[:quarter], far_in[p:], pass_in[p:]]
    current = (grams[0] + grams[1]) + (grams[2] + grams[3])
    lefts, rights = [], []
    for level in range(dev_count.bit_length() - 1):
        lefts.append(current)
        rights.append(swapped(current, "dev", 2**level))
        current = lefts[-1] + rights[-1]
    return tree(grams, rows_in, lefts, rights)


def solution(mesh):
    placed = (
        P("grp", "dev", None, None),
        P("grp", "dev", None, None, None),
        P("grp", "dev", None, None, None),
        P("grp", "dev", None, None),
        P("grp", "dev", None),
    )
    return jax.shard_map(
        on_device,
        mesh=mesh,
        in_specs=placed,
        out_specs=(P("dev", "grp", None), P("dev", None, None)),
        check_vma=False,
    )
```

time: 385 us -> 100 us (0.26); the launches traced: 379 us -> 99.7 us
  other arithmetic: 200 us -> 0.06 us
  matrix products: 55.5 us -> 0 us
  waiting for transfers between devices: 84.4 us -> 40.2 us
  Pallas kernels: 0 us -> 30.9 us
  starting transfers between devices: 3.22 us -> 20.2 us
  between operations: 14.8 us -> 0.87 us
  local copies, waits for them, and re-layouts: 20.8 us -> 7.48 us
    another operation x10 -> x0, other arithmetic: 197 us -> none  [the longest x4 117 us: on_device(): all_lower = jnp.linalg.cholesky(all_grams)]
    dot_general x3 -> x0, matrix products: 52.6 us -> none  [the longest x1 31.4 us: on_device(): jnp.einsum('bik,bip->bkp', v_flat, whole_probe[col_flat], precision=precise)]
    psum x1 -> x0, waiting for transfers between devices: 38.7 us -> none  [on_device(): total_sketch = lax.psum(partial_sketch, 'grp')]
    all_gather x1 -> x0, waiting for transfers between devices: 38.5 us -> none  [on_device(): whole_probe = lax.all_gather(omega, 'dev', axis=1, tiled=True)[0]]
    ppermute x3 -> x22, waiting for transfers between devices: 6.57 us -> 40.2 us  [swapped(): return lax.ppermute(value, axis, pairs)]
    pallas_call x0 -> x11, Pallas kernels: none -> 30.9 us  [the longest x1 16.3 us: tree(): pl.pallas_call(functools.partial(tree_kernel, panel, n_leaf, len(lefts)),...]
    gather x1 -> x0, local copies, waits for them, and re-layouts: 19.8 us -> none  [on_device(): whole_probe[col_flat]]
    ppermute x3 -> x22, starting transfers between devices: 3.14 us -> 20.2 us  [swapped(): return lax.ppermute(value, axis, pairs)]
  transfers between devices with their start and end apart: 5 -> 22, of which waited for: 5 -> 12; matrix products, arithmetic and copies ran while one was open for 1% -> 1% of each run, Pallas kernels for 0% -> 11%
where the time goes in v1:
time: 100 us; the launch traced here: 99.7 us
  waiting for transfers between devices  40.2 us (40%)
  Pallas kernels  30.9 us (31%)
  starting transfers between devices  20.2 us (20%)
  local copies, waits for them, and re-layouts  7.48 us (7%)
    ppermute x22, waiting for transfers between devices, swapped(): return lax.ppermute(value, axis, pairs)  40.2 us
    ppermute x22, starting transfers between devices, swapped(): return lax.ppermute(value, axis, pairs)  20.2 us
    pallas_call x1, Pallas kernels, tree(): pl.pallas_call(functools.partial(tree_kernel, panel, n_leaf, len(lefts)),...  16.3 us
    pallas_call x4, Pallas kernels, coefficients(): pl.pallas_call(functools.partial(coeff_kernel, most, start, unit, len(pie...  9.94 us
    unnamed x14, local copies, waits for them, and re-layouts  6.4 us
    pallas_call x4, Pallas kernels, sketch(): pl.pallas_call(functools.partial(sketch_kernel, m, n_blocks), out_shape=j...  3.59 us
  transfers between devices with their start and end apart: 22, of which 12 were waited for; matrix products, arithmetic and copies ran while one was open for 1% of the time, Pallas kernels for 11%

profile of v1, /device:TPU:0, one launch (start us, length us, event | category | flops | bytes accessed | tf_op | source)
XLA Modules:
  0.0 99.7 jit_solution(3357380987721546421)
XLA Ops:
  2.3 2.6 %collective-permute-start = (f32[2,256,128]{2,1,0:T(8,128)S(1)}, f32[2,256,128]{2,1,0:T(8,128)S(1)}, u32[]{:S(2)}, u32[]{:S(2)}) collective-permute-start(f32[2,256,128]{2,1,0:T(8,128)S(1)} %get-tuple-element.9), channel_id=1, source_target_pairs={{0,2},{1,3},{2,0},{3,1},{4,6},{5,7},{6,4},{7,5},{8,10},{9,11},{10,... | collective-permute-start | bytes 786440 | tf_op jit(solution)/shard_map/ppermute | solution.py:19
  4.8 1.5 %collective-permute-start.2 = (f32[2,256,128]{2,1,0:T(8,128)S(1)}, f32[2,256,128]{2,1,0:T(8,128)S(1)}, u32[]{:S(2)}, u32[]{:S(2)}) collective-permute-start(f32[2,256,128]{2,1,0:T(8,128)S(1)} %get-tuple-element.8), channel_id=1, source_target_pairs={{0,4},{1,5},{2,6},{3,7},{4,0},{5,1},{6,2},{7,3},{8,12},{9,13},{10,... | collective-permute-start | bytes 786440 | tf_op jit(solution)/shard_map/ppermute | solution.py:19
  6.9 5.1 %collective-permute-done.refs_2_ = f32[2,256,128]{2,1,0:T(8,128)S(1)} collective-permute-done((f32[2,256,128]{2,1,0:T(8,128)S(1)}, f32[2,256,128]{2,1,0:T(8,128)S(1)}, u32[]{:S(2)}, u32[]{:S(2)}) %collective-permute-start) | collective-permute-done | bytes 262176 | tf_op jit(solution)/shard_map/ppermute | solution.py:19
  12.0 2.0 %collective-permute-done.2.refs_3_ = f32[2,256,128]{2,1,0:T(8,128)S(1)} collective-permute-done((f32[2,256,128]{2,1,0:T(8,128)S(1)}, f32[2,256,128]{2,1,0:T(8,128)S(1)}, u32[]{:S(2)}, u32[]{:S(2)}) %collective-permute-start.2) | collective-permute-done | bytes 262176 | tf_op jit(solution)/shard_map/ppermute | solution.py:19
  15.5 4.1 %collective-permute-done.6.refs_2_ = f32[2,256,128]{2,1,0:T(8,128)S(1)} collective-permute-done((f32[2,256,128]{2,1,0:T(8,128)S(1)}, f32[2,256,128]{2,1,0:T(8,128)S(1)}, u32[]{:S(2)}, u32[]{:S(2)}) %collective-permute-start.6) | collective-permute-done | bytes 262176 | tf_op jit(solution)/shard_map/ppermute | solution.py:19
  20.3 4.2 %collective-permute-done.1.refs_2_ = f32[2,256,128]{2,1,0:T(8,128)S(1)} collective-permute-done((f32[2,256,128]{2,1,0:T(8,128)S(1)}, f32[2,256,128]{2,1,0:T(8,128)S(1)}, u32[]{:S(2)}, u32[]{:S(2)}) %collective-permute-start.1) | collective-permute-done | bytes 262176 | tf_op jit(solution)/shard_map/ppermute | solution.py:19
  24.5 1.9 %collective-permute-done.3.refs_3_ = f32[2,256,128]{2,1,0:T(8,128)S(1)} collective-permute-done((f32[2,256,128]{2,1,0:T(8,128)S(1)}, f32[2,256,128]{2,1,0:T(8,128)S(1)}, u32[]{:S(2)}, u32[]{:S(2)}) %collective-permute-start.3) | collective-permute-done | bytes 262176 | tf_op jit(solution)/shard_map/ppermute | solution.py:19
  28.5 4.0 %copy-done = f32[1,4,80,256,32]{3,4,2,1,0:T(8,128)S(1)} copy-done((f32[1,4,80,256,32]{3,4,2,1,0:T(8,128)S(1)}, f32[1,4,80,256,32]{3,4,2,1,0:T(8,128)}, u32[]{:S(2)}) %copy-start) | copy-done | bytes 10485784
  33.6 2.5 %coeff.4.refs_6_ = f32[321,32,128]{2,1,0:T(8,128)S(1)} custom-call(s32[16,32]{1,0:T(8,128)S(1)} %slots.1.refs_0_, f32[320,32,256]{2,1,0:T(8,128)S(1)} %bitcast.17, f32[4,256,128]{2,1,0:T(8,128)S(1)} %bitcast.28, f32[4,256,128]{2,1,0:T(8,128)S(1)} %collective-permute-done.12.refs_3_), custom_call_target="tpu_custom_call" | custom-call | flops 738197504 | bytes 8388608 | tf_op jit(solution)/shard_map/coeff/pallas_call | solution.py:127
  36.1 2.5 %coeff.5.refs_6_ = f32[321,32,128]{2,1,0:T(8,128)S(1)} custom-call(s32[16,32]{1,0:T(8,128)S(1)} %slots.1.refs_0_, f32[320,32,256]{2,1,0:T(8,128)S(1)} %bitcast.18, f32[2,256,128]{2,1,0:T(8,128)S(1)} %collective-permute-done.refs_2_, f32[2,256,128]{2,1,0:T(8,128)S(1)} %collective-permute-done.2.refs_3_, ...), custom_call_target="tpu_custom_call", output_to_operand_aliasing={{}: (6, {})} | custom-call | flops 738197504 | bytes 8388608 | tf_op jit(solution)/shard_map/coeff/pallas_call | solution.py:127
  38.6 2.5 %coeff.6.refs_6_ = f32[321,32,128]{2,1,0:T(8,128)S(1)} custom-call(s32[16,32]{1,0:T(8,128)S(1)} %slots.1.refs_0_, f32[320,32,256]{2,1,0:T(8,128)S(1)} %bitcast.19, f32[2,256,128]{2,1,0:T(8,128)S(1)} %collective-permute-done.6.refs_2_, f32[2,256,128]{2,1,0:T(8,128)S(1)} %collective-permute-done.7.refs_3_, ...), custom_call_target="tpu_custom_call", output_to_operand_aliasing={{}: (6, {})} | custom-call | flops 738197504 | bytes 8388608 | tf_op jit(solution)/shard_map/coeff/pallas_call | solution.py:127
  41.1 2.5 %coeff.7.c_ref = f32[321,32,128]{2,1,0:T(8,128)S(1)} custom-call(s32[16,32]{1,0:T(8,128)S(1)} %slots.1.refs_0_, f32[320,32,256]{2,1,0:T(8,128)S(1)} %bitcast.20, f32[2,256,128]{2,1,0:T(8,128)S(1)} %collective-permute-done.1.refs_2_, f32[2,256,128]{2,1,0:T(8,128)S(1)} %collective-permute-done.3.refs_3_, ...), custom_call_target="tpu_custom_call", output_to_operand_aliasing={{}: (6, {})} | custom-call | flops 738197504 | bytes 8388608 | tf_op jit(solution)/shard_map/coeff/pallas_call | solution.py:127
  44.6 1.6 %collective-permute-start.14 = (f32[128,256]{1,0:T(8,128)S(1)}, f32[128,256]{1,0:T(8,128)S(1)}, u32[]{:S(2)}, u32[]{:S(2)}) collective-permute-start(f32[128,256]{1,0:T(8,128)S(1)} %sketch.7), channel_id=1, source_target_pairs={{0,8},{8,0},{16,24},{24,16},{1,9},{9,1},{17,25},{25,17},{2,10},{10... | collective-permute-start | bytes 393224 | tf_op jit(solution)/shard_map/ppermute | solution.py:19
  48.5 2.5 %collective-permute-done.14 = f32[128,256]{1,0:T(8,128)S(1)} collective-permute-done((f32[128,256]{1,0:T(8,128)S(1)}, f32[128,256]{1,0:T(8,128)S(1)}, u32[]{:S(2)}, u32[]{:S(2)}) %collective-permute-start.14) | collective-permute-done | bytes 131104 | tf_op jit(solution)/shard_map/ppermute | solution.py:19
  51.0 2.6 %collective-permute-start.15 = (f32[128,256]{1,0:T(8,128)S(1)}, f32[128,256]{1,0:T(8,128)S(1)}, u32[]{:S(2)}, u32[]{:S(2)}) collective-permute-start(f32[128,256]{1,0:T(8,128)S(1)} %add.18), channel_id=1, source_target_pairs={{0,16},{8,24},{16,0},{24,8},{1,17},{9,25},{17,1},{25,9},{2,18},{10... | collective-permute-start | bytes 393224 | tf_op jit(solution)/shard_map/ppermute | solution.py:19
  54.6 4.9 %collective-permute-done.15.refs_2_ = f32[128,256]{1,0:T(8,128)S(1)} collective-permute-done((f32[128,256]{1,0:T(8,128)S(1)}, f32[128,256]{1,0:T(8,128)S(1)}, u32[]{:S(2)}, u32[]{:S(2)}) %collective-permute-start.15) | collective-permute-done | bytes 131104 | tf_op jit(solution)/shard_map/ppermute | solution.py:19
  60.4 3.4 %collective-permute-start.17 = (f32[192,128]{1,0:T(8,128)S(1)}, f32[192,128]{1,0:T(8,128)S(1)}, u32[]{:S(2)}, u32[]{:S(2)}) collective-permute-start(f32[192,128]{1,0:T(8,128)S(1)} %get-tuple-element.5), channel_id=1, source_target_pairs={{0,16},{8,24},{16,0},{24,8},{1,17},{9,25},{17,1},{25,9},{2,18},{10... | collective-permute-start | bytes 294920 | tf_op jit(solution)/shard_map/ppermute | solution.py:19
  63.8 2.9 %collective-permute-done.16 = f32[256,128]{1,0:T(8,128)S(1)} collective-permute-done((f32[256,128]{1,0:T(8,128)S(1)}, f32[256,128]{1,0:T(8,128)S(1)}, u32[]{:S(2)}, u32[]{:S(2)}) %collective-permute-start.16) | collective-permute-done | bytes 131104 | tf_op jit(solution)/shard_map/ppermute | solution.py:19
  66.7 1.5 %collective-permute-start.18 = (f32[192,128]{1,0:T(8,128)S(1)}, f32[192,128]{1,0:T(8,128)S(1)}, u32[]{:S(2)}, u32[]{:S(2)}) collective-permute-start(f32[192,128]{1,0:T(8,128)S(1)} %slice.50), channel_id=1, source_target_pairs={{0,16},{8,24},{16,0},{24,8},{1,17},{9,25},{17,1},{25,9},{2,18},{10... | collective-permute-start | bytes 294920 | tf_op jit(solution)/shard_map/ppermute | solution.py:19
  68.2 5.1 %collective-permute-done.18 = f32[192,128]{1,0:T(8,128)S(1)} collective-permute-done((f32[192,128]{1,0:T(8,128)S(1)}, f32[192,128]{1,0:T(8,128)S(1)}, u32[]{:S(2)}, u32[]{:S(2)}) %collective-permute-start.18) | collective-permute-done | bytes 98336 | tf_op jit(solution)/shard_map/ppermute | solution.py:19
  75.4 3.6 %collective-permute-done.20.refs_12_ = f32[128,128]{1,0:T(8,128)S(1)} collective-permute-done((f32[128,128]{1,0:T(8,128)S(1)}, f32[128,128]{1,0:T(8,128)S(1)}, u32[]{:S(2)}, u32[]{:S(2)}) %collective-permute-start.20) | collective-permute-done | bytes 65568 | tf_op jit(solution)/shard_map/ppermute | solution.py:19
  79.0 1.6 %collective-permute-start.21 = (f32[128,128]{1,0:T(8,128)S(1)}, f32[128,128]{1,0:T(8,128)S(1)}, u32[]{:S(2)}, u32[]{:S(2)}) collective-permute-start(f32[128,128]{1,0:T(8,128)S(1)} %add.23.refs_10_), channel_id=1, source_target_pairs={{0,4},{1,5},{2,6},{3,7},{4,0},{5,1},{6,2},{7,3},{8,12},{9,13},{10,... | collective-permute-start | bytes 196616 | tf_op jit(solution)/shard_map/ppermute | solution.py:19
  80.6 2.7 %collective-permute-done.21.refs_13_ = f32[128,128]{1,0:T(8,128)S(1)} collective-permute-done((f32[128,128]{1,0:T(8,128)S(1)}, f32[128,128]{1,0:T(8,128)S(1)}, u32[]{:S(2)}, u32[]{:S(2)}) %collective-permute-start.21) | collective-permute-done | bytes 65568 | tf_op jit(solution)/shard_map/ppermute | solution.py:19
  83.4 16.3 %tree.1 = (f32[4,64,128]{2,1,0:T(8,128)}, f32[4,256,128]{2,1,0:T(8,128)}) custom-call(f32[128,128]{1,0:T(8,128)S(1)} %get-tuple-element.12.refs_0_, f32[128,128]{1,0:T(8,128)S(1)} %get-tuple-element.11.refs_1_, f32[128,128]{1,0:T(8,128)S(1)} %get-tuple-element.13.refs_2_, f32[128,128]{1,0:T(8,128)S(1)} %get-tuple-element.14.refs_3_, ...), custom_call_target="tpu_custom_call" | custom-call | tf_op jit(solution)/shard_map/tree/pallas_call | solution.py:302
  (55 shorter events, 14.8 us)
Async XLA Ops:
  0.6 19.1 %collective-permute-start.12 = (f32[4,256,128]{2,1,0:T(8,128)}, f32[4,256,128]{2,1,0:T(8,128)S(1)}, u32[]{:S(2)}, u32[]{:S(2)}) collective-permute-start(f32[4,256,128]{2,1,0:T(8,128)} %bitcast.27), channel_id=1, source_target_pairs={{0,1},{1,0},{2,3},{3,2},{4,5},{5,4},{6,7},{7,6},{8,9},{9,8},{10,11... | collective-permute-start | bytes 1572872 | tf_op jit(solution)/shard_map/ppermute | solution.py:19
  2.3 9.7 %collective-permute-start = (f32[2,256,128]{2,1,0:T(8,128)S(1)}, f32[2,256,128]{2,1,0:T(8,128)S(1)}, u32[]{:S(2)}, u32[]{:S(2)}) collective-permute-start(f32[2,256,128]{2,1,0:T(8,128)S(1)} %get-tuple-element.9), channel_id=1, source_target_pairs={{0,2},{1,3},{2,0},{3,1},{4,6},{5,7},{6,4},{7,5},{8,10},{9,11},{10,... | collective-permute-start | bytes 786440 | tf_op jit(solution)/shard_map/ppermute | solution.py:19
  4.8 9.2 %collective-permute-start.2 = (f32[2,256,128]{2,1,0:T(8,128)S(1)}, f32[2,256,128]{2,1,0:T(8,128)S(1)}, u32[]{:S(2)}, u32[]{:S(2)}) collective-permute-start(f32[2,256,128]{2,1,0:T(8,128)S(1)} %get-tuple-element.8), channel_id=1, source_target_pairs={{0,4},{1,5},{2,6},{3,7},{4,0},{5,1},{6,2},{7,3},{8,12},{9,13},{10,... | collective-permute-start | bytes 786440 | tf_op jit(solution)/shard_map/ppermute | solution.py:19
  6.3 13.3 %collective-permute-start.6 = (f32[2,256,128]{2,1,0:T(8,128)S(1)}, f32[2,256,128]{2,1,0:T(8,128)S(1)}, u32[]{:S(2)}, u32[]{:S(2)}) collective-permute-start(f32[2,256,128]{2,1,0:T(8,128)S(1)} %get-tuple-element.9), channel_id=1, source_target_pairs={{0,4},{1,5},{2,6},{3,7},{4,0},{5,1},{6,2},{7,3},{8,12},{9,13},{10,... | collective-permute-start | bytes 786440 | tf_op jit(solution)/shard_map/ppermute | solution.py:19
  6.8 12.9 %collective-permute-start.7 = (f32[2,256,128]{2,1,0:T(8,128)S(1)}, f32[2,256,128]{2,1,0:T(8,128)S(1)}, u32[]{:S(2)}, u32[]{:S(2)}) collective-permute-start(f32[2,256,128]{2,1,0:T(8,128)S(1)} %get-tuple-element.8), channel_id=1, source_target_pairs={{0,2},{1,3},{2,0},{3,1},{4,6},{5,7},{6,4},{7,5},{8,10},{9,11},{10,... | collective-permute-start | bytes 786440 | tf_op jit(solution)/shard_map/ppermute | solution.py:19
  12.0 8.2 %collective-permute-start.10 = (f32[2,256,128]{2,1,0:T(8,128)S(1)}, f32[2,256,128]{2,1,0:T(8,128)S(1)}, u32[]{:S(2)}, u32[]{:S(2)}) collective-permute-start(f32[2,256,128]{2,1,0:T(8,128)S(1)} %collective-permute-done.refs_2_), channel_id=1, source_target_pairs={{0,1},{1,0},{2,3},{3,2},{4,5},{5,4},{6,7},{7,6},{8,9},{9,8},{10,11... | collective-permute-start | bytes 786440 | tf_op jit(solution)/shard_map/ppermute | solution.py:19
  14.0 10.5 %collective-permute-start.1 = (f32[2,256,128]{2,1,0:T(8,128)S(1)}, f32[2,256,128]{2,1,0:T(8,128)S(1)}, u32[]{:S(2)}, u32[]{:S(2)}) collective-permute-start(f32[2,256,128]{2,1,0:T(8,128)S(1)} %collective-permute-done.refs_2_), channel_id=1, source_target_pairs={{0,4},{1,5},{2,6},{3,7},{4,0},{5,1},{6,2},{7,3},{8,12},{9,13},{10,... | collective-permute-start | bytes 786440 | tf_op jit(solution)/shard_map/ppermute | solution.py:19
  19.6 6.8 %collective-permute-start.3 = (f32[2,256,128]{2,1,0:T(8,128)S(1)}, f32[2,256,128]{2,1,0:T(8,128)S(1)}, u32[]{:S(2)}, u32[]{:S(2)}) collective-permute-start(f32[2,256,128]{2,1,0:T(8,128)S(1)} %collective-permute-done.2.refs_3_), channel_id=1, source_target_pairs={{0,2},{1,3},{2,0},{3,1},{4,6},{5,7},{6,4},{7,5},{8,10},{9,11},{10,... | collective-permute-start | bytes 786440 | tf_op jit(solution)/shard_map/ppermute | solution.py:19
  19.7 16.4 %collective-permute-start.11 = (f32[2,256,128]{2,1,0:T(8,128)S(1)}, f32[2,256,128]{2,1,0:T(8,128)S(1)}, u32[]{:S(2)}, u32[]{:S(2)}) collective-permute-start(f32[2,256,128]{2,1,0:T(8,128)S(1)} %collective-permute-done.2.refs_3_), channel_id=1, source_target_pairs={{0,1},{1,0},{2,3},{3,2},{4,5},{5,4},{6,7},{7,6},{8,9},{9,8},{10,11... | collective-permute-start | bytes 786440 | tf_op jit(solution)/shard_map/ppermute | solution.py:19
  19.7 18.9 %collective-permute-start.8 = (f32[2,256,128]{2,1,0:T(8,128)S(1)}, f32[2,256,128]{2,1,0:T(8,128)S(1)}, u32[]{:S(2)}, u32[]{:S(2)}) collective-permute-start(f32[2,256,128]{2,1,0:T(8,128)S(1)} %collective-permute-done.6.refs_2_), channel_id=1, source_target_pairs={{0,1},{1,0},{2,3},{3,2},{4,5},{5,4},{6,7},{7,6},{8,9},{9,8},{10,11... | collective-permute-start | bytes 786440 | tf_op jit(solution)/shard_map/ppermute | solution.py:19
  20.2 18.4 %collective-permute-start.9 = (f32[2,256,128]{2,1,0:T(8,128)S(1)}, f32[2,256,128]{2,1,0:T(8,128)S(1)}, u32[]{:S(2)}, u32[]{:S(2)}) collective-permute-start(f32[2,256,128]{2,1,0:T(8,128)S(1)} %collective-permute-done.7.refs_3_), channel_id=1, source_target_pairs={{0,1},{1,0},{2,3},{3,2},{4,5},{5,4},{6,7},{7,6},{8,9},{9,8},{10,11... | collective-permute-start | bytes 786440 | tf_op jit(solution)/shard_map/ppermute | solution.py:19
  24.5 16.6 %collective-permute-start.4 = (f32[2,256,128]{2,1,0:T(8,128)S(1)}, f32[2,256,128]{2,1,0:T(8,128)S(1)}, u32[]{:S(2)}, u32[]{:S(2)}) collective-permute-start(f32[2,256,128]{2,1,0:T(8,128)S(1)} %collective-permute-done.1.refs_2_), channel_id=1, source_target_pairs={{0,1},{1,0},{2,3},{3,2},{4,5},{5,4},{6,7},{7,6},{8,9},{9,8},{10,11... | collective-permute-start | bytes 786440 | tf_op jit(solution)/shard_map/ppermute | solution.py:19
  26.4 14.7 %collective-permute-start.5 = (f32[2,256,128]{2,1,0:T(8,128)S(1)}, f32[2,256,128]{2,1,0:T(8,128)S(1)}, u32[]{:S(2)}, u32[]{:S(2)}) collective-permute-start(f32[2,256,128]{2,1,0:T(8,128)S(1)} %collective-permute-done.3.refs_3_), channel_id=1, source_target_pairs={{0,1},{1,0},{2,3},{3,2},{4,5},{5,4},{6,7},{7,6},{8,9},{9,8},{10,11... | collective-permute-start | bytes 786440 | tf_op jit(solution)/shard_map/ppermute | solution.py:19
  38.6 5.0 %slice-start = ((s8[10485760]{0:T(1024)(128)(4,1)}), s8[4194304]{0:T(1024)(128)(4,1)S(1)}, s32[]{:S(2)}) async-start(s8[10485760]{0:T(1024)(128)(4,1)} %bitcast.21), calls=%async_computation | async-start | bytes 8388608
  38.6 5.0 %slice-start.1 = ((s8[10485760]{0:T(1024)(128)(4,1)}), s8[4194304]{0:T(1024)(128)(4,1)S(1)}, s32[]{:S(2)}) async-start(s8[10485760]{0:T(1024)(128)(4,1)} %bitcast.21), calls=%async_computation.1 | async-start | bytes 8388608
  44.6 6.4 %collective-permute-start.14 = (f32[128,256]{1,0:T(8,128)S(1)}, f32[128,256]{1,0:T(8,128)S(1)}, u32[]{:S(2)}, u32[]{:S(2)}) collective-permute-start(f32[128,256]{1,0:T(8,128)S(1)} %sketch.7), channel_id=1, source_target_pairs={{0,8},{8,0},{16,24},{24,16},{1,9},{9,1},{17,25},{25,17},{2,10},{10... | collective-permute-start | bytes 393224 | tf_op jit(solution)/shard_map/ppermute | solution.py:19
  47.1 7.5 %collective-permute-start.13 = (f32[128,256]{1,0:T(8,128)S(1)}, f32[128,256]{1,0:T(8,128)S(1)}, u32[]{:S(2)}, u32[]{:S(2)}) collective-permute-start(f32[128,256]{1,0:T(8,128)S(1)} %sketch.5), channel_id=1, source_target_pairs={{0,8},{8,0},{16,24},{24,16},{1,9},{9,1},{17,25},{25,17},{2,10},{10... | collective-permute-start | bytes 393224 | tf_op jit(solution)/shard_map/ppermute | solution.py:19
  51.0 8.4 %collective-permute-start.15 = (f32[128,256]{1,0:T(8,128)S(1)}, f32[128,256]{1,0:T(8,128)S(1)}, u32[]{:S(2)}, u32[]{:S(2)}) collective-permute-start(f32[128,256]{1,0:T(8,128)S(1)} %add.18), channel_id=1, source_target_pairs={{0,16},{8,24},{16,0},{24,8},{1,17},{9,25},{17,1},{25,9},{2,18},{10... | collective-permute-start | bytes 393224 | tf_op jit(solution)/shard_map/ppermute | solution.py:19
  59.7 6.9 %collective-permute-start.16 = (f32[256,128]{1,0:T(8,128)S(1)}, f32[256,128]{1,0:T(8,128)S(1)}, u32[]{:S(2)}, u32[]{:S(2)}) collective-permute-start(f32[256,128]{1,0:T(8,128)S(1)} %get-tuple-element.6), channel_id=1, source_target_pairs={{0,8},{8,0},{16,24},{24,16},{1,9},{9,1},{17,25},{25,17},{2,10},{10... | collective-permute-start | bytes 393224 | tf_op jit(solution)/shard_map/ppermute | solution.py:19
  60.4 7.8 %collective-permute-start.17 = (f32[192,128]{1,0:T(8,128)S(1)}, f32[192,128]{1,0:T(8,128)S(1)}, u32[]{:S(2)}, u32[]{:S(2)}) collective-permute-start(f32[192,128]{1,0:T(8,128)S(1)} %get-tuple-element.5), channel_id=1, source_target_pairs={{0,16},{8,24},{16,0},{24,8},{1,17},{9,25},{17,1},{25,9},{2,18},{10... | collective-permute-start | bytes 294920 | tf_op jit(solution)/shard_map/ppermute | solution.py:19
  66.7 6.6 %collective-permute-start.18 = (f32[192,128]{1,0:T(8,128)S(1)}, f32[192,128]{1,0:T(8,128)S(1)}, u32[]{:S(2)}, u32[]{:S(2)}) collective-permute-start(f32[192,128]{1,0:T(8,128)S(1)} %slice.50), channel_id=1, source_target_pairs={{0,16},{8,24},{16,0},{24,8},{1,17},{9,25},{17,1},{25,9},{2,18},{10... | collective-permute-start | bytes 294920 | tf_op jit(solution)/shard_map/ppermute | solution.py:19
  73.3 1.3 %collective-permute-start.19 = (f32[128,128]{1,0:T(8,128)S(1)}, f32[128,128]{1,0:T(8,128)S(1)}, u32[]{:S(2)}, u32[]{:S(2)}) collective-permute-start(f32[128,128]{1,0:T(8,128)S(1)} %get-tuple-element.10.refs_8_), channel_id=1, source_target_pairs={{0,1},{1,0},{2,3},{3,2},{4,5},{5,4},{6,7},{7,6},{8,9},{9,8},{10,11... | collective-permute-start | bytes 196616 | tf_op jit(solution)/shard_map/ppermute | solution.py:19
  74.7 4.3 %collective-permute-start.20 = (f32[128,128]{1,0:T(8,128)S(1)}, f32[128,128]{1,0:T(8,128)S(1)}, u32[]{:S(2)}, u32[]{:S(2)}) collective-permute-start(f32[128,128]{1,0:T(8,128)S(1)} %add.22.refs_9_), channel_id=1, source_target_pairs={{0,2},{1,3},{2,0},{3,1},{4,6},{5,7},{6,4},{7,5},{8,10},{9,11},{10,... | collective-permute-start | bytes 196616 | tf_op jit(solution)/shard_map/ppermute | solution.py:19
  79.0 4.3 %collective-permute-start.21 = (f32[128,128]{1,0:T(8,128)S(1)}, f32[128,128]{1,0:T(8,128)S(1)}, u32[]{:S(2)}, u32[]{:S(2)}) collective-permute-start(f32[128,128]{1,0:T(8,128)S(1)} %add.23.refs_10_), channel_id=1, source_target_pairs={{0,4},{1,5},{2,6},{3,7},{4,0},{5,1},{6,2},{7,3},{8,12},{9,13},{10,... | collective-permute-start | bytes 196616 | tf_op jit(solution)/shard_map/ppermute | solution.py:19
  (5 other events, 8.9 us)

commit v2 on v1

--- a/solution.py
+++ b/solution.py
@@ -31,7 +31,9 @@
     )
 
 
-def table_kernel(order, unit, n_local, cols_ref, ranks_ref, slot_ref):
+def table_kernel(order, unit, n_local, cols_ref, ranks_ref, v_ref, slot_ref, held_ref, sem):
+    copy = pltpu.make_async_copy(v_ref, held_ref, sem)
+    copy.start()
     n_leaf, _, n_blocks = cols_ref.shape
     depth, clusters = slot_ref.shape
     position = lax.broadcasted_iota(jnp.int32, (clusters, 1), 0)
@@ -68,18 +70,23 @@
         offset = offset + jnp.dot(named_low, ones, preferred_element_type=f32)
     index = jnp.where(used > 0.5, index, float(n_leaf * n_blocks))
     slot_ref[...] = index.astype(jnp.int32) * unit + rank.astype(jnp.int32)
-
-
-def slot_table(order, cols, ranks, depth, unit, n_local):
+    copy.wait()
+
+
+def slot_table(order, cols, ranks, v, depth, unit, n_local):
     return pl.pallas_call(
         functools.partial(table_kernel, order, unit, n_local),
-        out_shape=jax.ShapeDtypeStruct((depth, len(order)), jnp.int32),
-        in_specs=[VM, VM],
-        out_specs=VM,
+        out_shape=(
+            jax.ShapeDtypeStruct((depth, len(order)), jnp.int32),
+            jax.ShapeDtypeStruct(v.shape, f32),
+        ),
+        in_specs=[VM, VM, pl.BlockSpec(memory_space=pltpu.HBM)],
+        out_specs=(VM, VM),
+        scratch_shapes=[pltpu.SemaphoreType.DMA],
         compiler_params=pltpu.CompilerParams(vmem_limit_bytes=4 << 20),
         cost_estimate=pl.CostEstimate(flops=0, bytes_accessed=24 << 20, transcendentals=0),
         name="slots",
-    )(cols, ranks)
+    )(cols, ranks, v)
 
 
 def coeff_kernel(most, start, unit, n_pieces, *refs):
@@ -115,7 +122,7 @@
             c_ref[ids[n]] = jnp.where(kept[n], total[n * k : (n + 1) * k], 0.0)
         return 0
 
-    lax.fori_loop(0, at, body, 0, unroll=2)
+    lax.fori_loop(0, at, body, 0, unroll=4)
 
 
 def coefficients(slots, v, pieces, start, most, unit, before):
@@ -131,7 +138,7 @@
         out_specs=VM,
         scratch_shapes=[pltpu.VMEM((held, rows, 2 * p), bf16)],
         input_output_aliases={len(args) - 1: 0} if chained else {},
-        compiler_params=pltpu.CompilerParams(vmem_limit_bytes=8 << 20),
+        compiler_params=pltpu.CompilerParams(vmem_limit_bytes=12 << 20),
         cost_estimate=pl.CostEstimate(
             flops=held * most * k * rows * p * 8, bytes_accessed=8 << 20, transcendentals=0
         ),
@@ -171,97 +178,108 @@
     )(coeff, u)
 
 
+def pack(gram):
+    p = gram.shape[0]
+    half = p // 2
+    ri = lax.broadcasted_iota(jnp.int32, (half, p), 0)
+    ci = lax.broadcasted_iota(jnp.int32, (half, p), 1)
+    lower = gram[half:]
+    body = jnp.where(ci < ri, pltpu.roll(lower, half, 1), gram[:half])
+    diagonal = jnp.sum(jnp.where(ci == ri + half, lower, 0.0), axis=0, keepdims=True)
+    return body, jnp.broadcast_to(diagonal, (8, p))
+
+
+def unpack(packed):
+    p = packed.shape[1]
+    half = p // 2
+    ri = lax.broadcasted_iota(jnp.int32, (half, p), 0)
+    ci = lax.broadcasted_iota(jnp.int32, (half, p), 1)
+    body = packed[:half]
+    upper = jnp.where(ci >= ri, body, 0.0)
+    lower = jnp.where((ci >= half) & (ci - half < ri), pltpu.roll(body, half, 1), 0.0)
+    lower = jnp.where(ci == ri + half, packed[half : half + 1], lower)
+    once = jnp.concatenate([upper, lower], axis=0)
+    rj = lax.broadcasted_iota(jnp.int32, (p, p), 0)
+    cj = lax.broadcasted_iota(jnp.int32, (p, p), 1)
+    return jnp.where(rj == cj, once, once + once.T)
+
+
 def gram_kernel(n_terms, *refs):
     terms = refs[:n_terms]
-    near_ref, far_ref, keep_ref, hold_ref = refs[n_terms:]
+    near_ref, far_ref, rows_ref, keep_ref, hold_ref = refs[n_terms:]
     total = terms[0][...]
     for term in terms[1:]:
         total = total + term[...]
-    gram = dot_full(total, total, ((1,), (1,)))
+    body, diagonal = pack(dot_full(total, total, ((1,), (1,))))
+    half = body.shape[0]
+    far_ref[:half] = body
+    far_ref[half:] = diagonal
     hold_ref[...] = total.T
-    p = gram.shape[0]
     quarter = keep_ref.shape[0]
 
     def rows_of(m):
         at = pl.multiple_of(jnp.bitwise_xor(lax.axis_index("grp"), m) * quarter, quarter)
         return hold_ref[pl.ds(at, quarter), :]
 
+    near_ref[:quarter] = rows_of(1)
+    near_ref[quarter : quarter + half] = body
+    near_ref[quarter + half : quarter + half + 8] = diagonal
+    near_ref[quarter + half + 8 :] = rows_of(3)
+    rows_ref[...] = rows_of(2)
     keep_ref[...] = rows_of(0)
-    near_ref[:quarter] = rows_of(1)
-    near_ref[quarter : quarter + p] = gram
-    near_ref[quarter + p :] = rows_of(3)
-    far_ref[:p] = gram
-    far_ref[p:] = rows_of(2)
 
 
 def gram_of(terms, n_grp):
     p, rows = terms[0].shape
     quarter = rows // n_grp
+    short = p // 2 + 8
     return pl.pallas_call(
         functools.partial(gram_kernel, len(terms)),
-        out_shape=(
-            jax.ShapeDtypeStruct((p + 2 * quarter, p), f32),
-            jax.ShapeDtypeStruct((p + quarter, p), f32),
-            jax.ShapeDtypeStruct((quarter, p), f32),
+        out_shape=tuple(
+            jax.ShapeDtypeStruct((height, p), f32)
+            for height in (short + 2 * quarter, short, quarter, quarter)
         ),
         in_specs=[VM] * len(terms),
-        out_specs=(VM, VM, VM),
+        out_specs=(VM, VM, VM, VM),
         scratch_shapes=[pltpu.VMEM((rows, p), f32)],
         compiler_params=pltpu.CompilerParams(vmem_limit_bytes=8 << 20),
         name="gram",
     )(*terms)
 
 
-def tree_kernel(panel, n_leaf, n_levels, *refs):
-    grams = refs[:n_leaf]
-    rows_in = refs[n_leaf : 2 * n_leaf]
-    lefts = refs[2 * n_leaf : 2 * n_leaf + n_levels]
-    rights = refs[2 * n_leaf + n_levels : 2 * n_leaf + 2 * n_levels]
-    basis_ref, tr_ref, m_ref = refs[2 * n_leaf + 2 * n_levels :]
+def factor(m_ref, panel, group):
     count, p, _ = m_ref.shape
-    own = lax.axis_index("grp")
-    device = lax.axis_index("dev")
-    ri = lax.broadcasted_iota(jnp.int32, (p, p), 0)
-    ci = lax.broadcasted_iota(jnp.int32, (p, p), 1)
-    for m in range(n_leaf):
-        m_ref[jnp.bitwise_xor(own, m)] = grams[m][...]
-    identity = jnp.where(ri == ci, 1.0, 0.0)
-    m_ref[7] = identity
-    m_ref[8] = identity
-    for level in range(n_levels):
-
-        @pl.when(device % 2 ** (level + 1) == 2**level - 1)
-        def _(level=level):
-            m_ref[7] = lefts[level][...]
-            m_ref[8] = rights[level][...]
-
-    m_ref[4] = m_ref[0] + m_ref[1]
-    m_ref[5] = m_ref[2] + m_ref[3]
-    m_ref[6] = m_ref[4] + m_ref[5]
-    m_ref[9] = m_ref[7] + m_ref[8]
     lane = lax.broadcasted_iota(jnp.int32, (1, 1, p), 2)
     sub8 = lax.broadcasted_iota(jnp.int32, (1, 8, p), 1)
-    n_panels = p // panel
     n_tiles = panel // 8
-    for pn in range(n_panels):
-        base = pn * panel
+    for base in range(0, p, panel):
+        after = base + panel
         x = [m_ref[:, base + 8 * i : base + 8 * i + 8, :] for i in range(n_tiles)]
-        for t in range(panel):
-            i0, ts = t // 8, t % 8
-            k = base + t
-            columns = [jnp.broadcast_to(x[i][:, :, k : k + 1], x[i].shape) for i in range(i0, n_tiles)]
-            scale = lax.rsqrt(columns[0][:, ts : ts + 1, :])
-            hit = lane == k
-            row = jnp.where(hit, 1.0, x[i0][:, ts : ts + 1, :]) * scale
-            for i in range(i0, n_tiles):
-                new = jnp.where(hit, 0.0, x[i]) - (columns[i - i0] * scale) * row
-                if i == i0:
-                    new = jnp.where(sub8 < ts, x[i], jnp.where(sub8 == ts, row, new))
-                x[i] = new
+        for t0 in range(0, panel, group):
+            i0 = t0 // 8
+            tiles = range(i0, n_tiles)
+            columns = []
+            for s in range(t0, t0 + group):
+                k = base + s
+                columns.append([jnp.broadcast_to(x[i][:, :, k : k + 1], x[i].shape) for i in tiles])
+            for t in range(group):
+                ts = (t0 + t) % 8
+                hit = lane == base + t0 + t
+                scale = lax.rsqrt(columns[t][0][:, ts : ts + 1, :])
+                parts = [column * scale for column in columns[t]]
+                for s in range(t + 1, group):
+                    ss = (t0 + s) % 8
+                    weight = parts[0][:, ss : ss + 1, :]
+                    columns[s] = [c - part * weight for c, part in zip(columns[s], parts)]
+                row = jnp.where(hit, 1.0, x[i0][:, ts : ts + 1, :]) * scale
+                for i in tiles:
+                    new = jnp.where(hit, 0.0, x[i]) - parts[i - i0] * row
+                    if i == i0:
+                        new = jnp.where(sub8 < ts, x[i], jnp.where(sub8 == ts, row, new))
+                    x[i] = new
         for i in range(n_tiles):
             m_ref[:, base + 8 * i : base + 8 * i + 8, :] = x[i]
-        if pn < n_panels - 1:
-            after = base + panel
+        if after < p:
             for b in range(count):
                 block = m_ref[b, base:after, :]
                 si = lax.broadcasted_iota(jnp.int32, block.shape, 0)
@@ -273,41 +291,73 @@
                 old = jnp.where((lj >= base) & (lj < after), 0.0, old)
                 m_ref[b, after:, :] = old - change
 
+
+def tree_kernel(panel, group, n_leaf, n_levels, *refs):
+    grams = refs[:n_leaf]
+    rows_in = refs[n_leaf : 2 * n_leaf]
+    lefts = refs[2 * n_leaf : 2 * n_leaf + n_levels]
+    rights = refs[2 * n_leaf + n_levels : 2 * n_leaf + 2 * n_levels]
+    basis_ref, tr_ref, m_ref, pick_ref = refs[2 * n_leaf + 2 * n_levels :]
+    p = m_ref.shape[1]
+    own = lax.axis_index("grp")
+    device = lax.axis_index("dev")
+    for m in range(n_leaf):
+        m_ref[jnp.bitwise_xor(own, m)] = unpack(grams[m][...])
+    m_ref[4] = m_ref[0] + m_ref[1]
+    m_ref[5] = m_ref[2] + m_ref[3]
+    m_ref[6] = m_ref[4] + m_ref[5]
+    pick_ref[0] = grams[0][...]
+    pick_ref[1] = grams[1][...]
+    for level in range(n_levels):
+
+        @pl.when(device % 2 ** (level + 1) == 2**level - 1)
+        def _(level=level):
+            pick_ref[0] = lefts[level][...]
+            pick_ref[1] = rights[level][...]
+
+    m_ref[7] = unpack(pick_ref[0])
+    m_ref[8] = unpack(pick_ref[1])
+    m_ref[9] = m_ref[7] + m_ref[8]
+    factor(m_ref, panel, group)
+    ri = lax.broadcasted_iota(jnp.int32, (p, p), 0)
+    ci = lax.broadcasted_iota(jnp.int32, (p, p), 1)
+
     def inverse(b):
-        return jnp.where(ci <= ri, m_ref[b], 0.0)
+        return jnp.concatenate(split(jnp.where(ci <= ri, m_ref[b], 0.0)), axis=0)
 
     def upper(b):
         whole = m_ref[b]
         return jnp.where(ci > ri, whole, jnp.where(ci == ri, 1.0 / whole, 0.0))
 
+    def applied(x, solve):
+        high, low = split(x)
+        dims = (((1,), (1,)), ((), ()))
+        both = lax.dot_general(high, solve, dims, preferred_element_type=f32)
+        both = both + lax.dot_general(low, solve, dims, preferred_element_type=f32)
+        return both[:, :p] + both[:, p:]
+
     for m in range(n_leaf):
         leaf = jnp.bitwise_xor(own, m)
-        basis_ref[leaf] = dot_full(rows_in[m][...], inverse(leaf), ((1,), (1,)))
+        basis_ref[leaf] = applied(rows_in[m][...], inverse(leaf))
     keep = device != lax.axis_size("dev") - 1
     for q, (a, b, node) in enumerate(((0, 1, 4), (2, 3, 5), (4, 5, 6), (7, 8, 9))):
-        solve = inverse(node)
-        top = dot_full(upper(a), solve, ((1,), (1,)))
-        bottom = dot_full(upper(b), solve, ((1,), (1,)))
-        if q == 3:
-            top = jnp.where(keep, top, 0.0)
-            bottom = jnp.where(keep, bottom, 0.0)
-        tr_ref[q, :p] = top
-        tr_ref[q, p:] = bottom
-
-
-def tree(grams, rows_in, lefts, rights, panel=32):
+        made = applied(jnp.concatenate([upper(a), upper(b)], axis=0), inverse(node))
+        tr_ref[q] = jnp.where(keep, made, 0.0) if q == 3 else made
+
+
+def tree(grams, rows_in, lefts, rights, panel=32, group=4):
     quarter, p = rows_in[0].shape
     n_leaf = len(grams)
     arrays = [*grams, *rows_in, *lefts, *rights]
     return pl.pallas_call(
-        functools.partial(tree_kernel, panel, n_leaf, len(lefts)),
+        functools.partial(tree_kernel, panel, group, n_leaf, len(lefts)),
         out_shape=(
             jax.ShapeDtypeStruct((n_leaf, quarter, p), f32),
             jax.ShapeDtypeStruct((4, 2 * p, p), f32),
         ),
         in_specs=[VM] * len(arrays),
         out_specs=(VM, VM),
-        scratch_shapes=[pltpu.VMEM((10, p, p), f32)],
+        scratch_shapes=[pltpu.VMEM((10, p, p), f32), pltpu.VMEM((2, *grams[0].shape), f32)],
         compiler_params=pltpu.CompilerParams(vmem_limit_bytes=16 << 20),
         name="tree",
     )(*arrays)
@@ -331,7 +381,7 @@
             held = held + new
     other = swapped(omega, "dev", 1)
     order = [mask * n_local + q for mask in (0, 1) for q in range(n_local)]
-    groups = [[omega, other]]
+    groups = [[omega[:half], omega[half:], other]]
     for level in sorted(waves):
         wave = waves[level]
         for flip in (0, 1):
@@ -346,7 +396,6 @@
 def on_device(omega, u_factor, v_factor, columns, ranks):
     n_local, n_blocks = u_factor.shape[1:3]
     leaf_rows, width = u_factor.shape[3:]
-    p = omega.shape[3]
     dev_count = lax.axis_size("dev")
     grp_count = lax.axis_size("grp")
     assert n_local == grp_count == 4
@@ -358,7 +407,7 @@
     depth = -(-most // 8) * 8
     unit = 2 * width
     columns = jnp.swapaxes(columns[0], 1, 2)
-    slots = slot_table(tuple(order), columns, ranks[0], depth, unit, n_local)
+    slots, v = slot_table(tuple(order), columns, ranks[0], v, depth, unit, n_local)
     coeff = None
     start = 0
     for pieces in groups:
@@ -367,19 +416,31 @@
     across = swapped(sketch(coeff, u, 3, n_blocks), "grp", 1)
     beside = swapped(sketch(coeff, u, 1, n_blocks), "grp", 1)
     across = swapped(sketch(coeff, u, 2, n_blocks) + across, "grp", 2)
-    near, far, rows_own = gram_of([sketch(coeff, u, 0, n_blocks), beside, across], grp_count)
-    quarter = rows_own.shape[0]
+    near, far, rows_far, rows_own = gram_of(
+        [sketch(coeff, u, 0, n_blocks), beside, across], grp_count
+    )
+    quarter, short = rows_own.shape[0], far.shape[0]
+    near_in = swapped(near, "grp", 1)
     far_in = swapped(far, "grp", 2)
-    near_in = swapped(near, "grp", 1)
-    pass_in = swapped(near_in[quarter:], "grp", 2)
-    grams = [far[:p], near_in[quarter : quarter + p], far_in[:p], pass_in[:p]]
-    rows_in = [rows_own, near_in[:quarter], far_in[p:], pass_in[p:]]
-    current = (grams[0] + grams[1]) + (grams[2] + grams[3])
+    gram_in = near_in[quarter : quarter + short]
+    pass_in = swapped(gram_in, "grp", 2)
+    grams = [far, gram_in, far_in, pass_in]
+    current = (far + gram_in) + (far_in + pass_in)
     lefts, rights = [], []
-    for level in range(dev_count.bit_length() - 1):
+    masks = [2**bit for bit in range(dev_count.bit_length() - 1)]
+    steps = [masks[:1]] + [masks[at : at + 2] for at in range(1, len(masks), 2)]
+    for step in steps:
+        first = swapped(current, "dev", step[0])
+        wider = [swapped(current, "dev", extra ^ step[1]) for extra in (0, step[0])] if step[1:] else []
         lefts.append(current)
-        rights.append(swapped(current, "dev", 2**level))
-        current = lefts[-1] + rights[-1]
+        rights.append(first)
+        current = current + first
+        if wider:
+            lefts.append(current)
+            rights.append(wider[0] + wider[1])
+            current = current + rights[-1]
+    both_in = swapped(jnp.concatenate([rows_far, near_in[quarter + short :]]), "grp", 2)
+    rows_in = [rows_own, near_in[:quarter], both_in[:quarter], both_in[quarter:]]
     return tree(grams, rows_in, lefts, rights)
 
 

time: 100 us -> 86.8 us (0.87)
  waiting for transfers between devices: 40.2 us -> 32 us
  Pallas kernels: 30.9 us -> 24.3 us
  starting transfers between devices: 20.2 us -> 22.8 us
  local copies, waits for them, and re-layouts: 7.48 us -> 6.44 us
    ppermute x22 -> x24, waiting for transfers between devices: 40.2 us -> 32 us  [swapped(): return lax.ppermute(value, axis, pairs)]
    pallas_call x2, Pallas kernels: 16.6 us -> 10.8 us  [the longest x1 10.4 us: tree(): pl.pallas_call(functools.partial(tree_kernel, panel, group, n_leaf, len(l...]
    ppermute x22 -> x24, starting transfers between devices: 20.2 us -> 22.8 us  [swapped(): return lax.ppermute(value, axis, pairs)]
    pallas_call x4, Pallas kernels: 9.94 us -> 8.52 us  [coefficients(): pl.pallas_call(functools.partial(coeff_kernel, most, start, unit, len(pie...]
    unnamed x14 -> x12, local copies, waits for them, and re-layouts: 6.4 us -> 5.36 us
  transfers between devices with their start and end apart: 22 -> 24, of which waited for: 12 -> 12; matrix products, arithmetic and copies ran while one was open for 1% -> 1% of each run, Pallas kernels for 11% -> 12%
where the time goes in v2:
time: 86.8 us; the launch traced here: 86.6 us
  waiting for transfers between devices  32 us (37%)
  Pallas kernels  24.3 us (28%)
  starting transfers between devices  22.8 us (26%)
  local copies, waits for them, and re-layouts  6.44 us (7%)
  between operations  0.87 us (1%)
    ppermute x24, waiting for transfers between devices, swapped(): return lax.ppermute(value, axis, pairs)  32 us
    ppermute x24, starting transfers between devices, swapped(): return lax.ppermute(value, axis, pairs)  22.8 us
    pallas_call x1, Pallas kernels, tree(): pl.pallas_call(functools.partial(tree_kernel, panel, group, n_leaf, len(l...  10.4 us
    pallas_call x4, Pallas kernels, coefficients(): pl.pallas_call(functools.partial(coeff_kernel, most, start, unit, len(pie...  8.52 us
    unnamed x12, local copies, waits for them, and re-layouts  5.36 us
    pallas_call x4, Pallas kernels, sketch(): pl.pallas_call(functools.partial(sketch_kernel, m, n_blocks), out_shape=j...  3.59 us
  transfers between devices with their start and end apart: 24, of which 12 were waited for; matrix products, arithmetic and copies ran while one was open for 1% of the time, Pallas kernels for 12%

profile of v2, /device:TPU:0, one launch (start us, length us, event | category | flops | bytes accessed | tf_op | source)
XLA Modules:
  0.0 86.6 jit_solution(2352323815500633464)
XLA Ops:
  2.3 2.6 %collective-permute-start = (f32[2,256,128]{2,1,0:T(8,128)S(1)}, f32[2,256,128]{2,1,0:T(8,128)S(1)}, u32[]{:S(2)}, u32[]{:S(2)}) collective-permute-start(f32[2,256,128]{2,1,0:T(8,128)S(1)} %get-tuple-element.15.refs_2_), channel_id=1, source_target_pairs={{0,2},{1,3},{2,0},{3,1},{4,6},{5,7},{6,4},{7,5},{8,10},{9,11},{10,... | collective-permute-start | bytes 786440 | tf_op jit(solution)/shard_map/ppermute | solution.py:19
  4.8 1.5 %collective-permute-start.2 = (f32[2,256,128]{2,1,0:T(8,128)S(1)}, f32[2,256,128]{2,1,0:T(8,128)S(1)}, u32[]{:S(2)}, u32[]{:S(2)}) collective-permute-start(f32[2,256,128]{2,1,0:T(8,128)S(1)} %get-tuple-element.14.refs_3_), channel_id=1, source_target_pairs={{0,4},{1,5},{2,6},{3,7},{4,0},{5,1},{6,2},{7,3},{8,12},{9,13},{10,... | collective-permute-start | bytes 786440 | tf_op jit(solution)/shard_map/ppermute | solution.py:19
  6.9 5.1 %collective-permute-done.refs_2_ = f32[2,256,128]{2,1,0:T(8,128)S(1)} collective-permute-done((f32[2,256,128]{2,1,0:T(8,128)S(1)}, f32[2,256,128]{2,1,0:T(8,128)S(1)}, u32[]{:S(2)}, u32[]{:S(2)}) %collective-permute-start) | collective-permute-done | bytes 262176 | tf_op jit(solution)/shard_map/ppermute | solution.py:19
  12.0 2.0 %collective-permute-done.2.refs_3_ = f32[2,256,128]{2,1,0:T(8,128)S(1)} collective-permute-done((f32[2,256,128]{2,1,0:T(8,128)S(1)}, f32[2,256,128]{2,1,0:T(8,128)S(1)}, u32[]{:S(2)}, u32[]{:S(2)}) %collective-permute-start.2) | collective-permute-done | bytes 262176 | tf_op jit(solution)/shard_map/ppermute | solution.py:19
  14.0 1.5 %collective-permute-start.1 = (f32[2,256,128]{2,1,0:T(8,128)S(1)}, f32[2,256,128]{2,1,0:T(8,128)S(1)}, u32[]{:S(2)}, u32[]{:S(2)}) collective-permute-start(f32[2,256,128]{2,1,0:T(8,128)S(1)} %collective-permute-done.refs_2_), channel_id=1, source_target_pairs={{0,4},{1,5},{2,6},{3,7},{4,0},{5,1},{6,2},{7,3},{8,12},{9,13},{10,... | collective-permute-start | bytes 786440 | tf_op jit(solution)/shard_map/ppermute | solution.py:19
  15.5 4.1 %collective-permute-done.6.refs_2_ = f32[2,256,128]{2,1,0:T(8,128)S(1)} collective-permute-done((f32[2,256,128]{2,1,0:T(8,128)S(1)}, f32[2,256,128]{2,1,0:T(8,128)S(1)}, u32[]{:S(2)}, u32[]{:S(2)}) %collective-permute-start.6) | collective-permute-done | bytes 262176 | tf_op jit(solution)/shard_map/ppermute | solution.py:19
  20.3 4.2 %collective-permute-done.1.refs_2_ = f32[2,256,128]{2,1,0:T(8,128)S(1)} collective-permute-done((f32[2,256,128]{2,1,0:T(8,128)S(1)}, f32[2,256,128]{2,1,0:T(8,128)S(1)}, u32[]{:S(2)}, u32[]{:S(2)}) %collective-permute-start.1) | collective-permute-done | bytes 262176 | tf_op jit(solution)/shard_map/ppermute | solution.py:19
  24.5 1.9 %collective-permute-done.3.refs_3_ = f32[2,256,128]{2,1,0:T(8,128)S(1)} collective-permute-done((f32[2,256,128]{2,1,0:T(8,128)S(1)}, f32[2,256,128]{2,1,0:T(8,128)S(1)}, u32[]{:S(2)}, u32[]{:S(2)}) %collective-permute-start.3) | collective-permute-done | bytes 262176 | tf_op jit(solution)/shard_map/ppermute | solution.py:19
  26.4 4.0 %copy-done = f32[1,4,80,256,32]{3,4,2,1,0:T(8,128)S(1)} copy-done((f32[1,4,80,256,32]{3,4,2,1,0:T(8,128)S(1)}, f32[1,4,80,256,32]{3,4,2,1,0:T(8,128)}, u32[]{:S(2)}) %copy-start) | copy-done | bytes 10485784
  33.2 2.1 %coeff.4.refs_6_ = f32[321,32,128]{2,1,0:T(8,128)S(1)} custom-call(s32[16,32]{1,0:T(8,128)S(1)} %get-tuple-element.8.refs_0_, f32[320,32,256]{2,1,0:T(8,128)S(1)} %get-tuple-element.9.refs_1_, f32[2,256,128]{2,1,0:T(8,128)S(1)} %get-tuple-element.15.refs_2_, f32[2,256,128]{2,1,0:T(8,128)S(1)} %get-tuple-element.14.refs_3_, ...), custom_call_target="tpu_custom_call" | custom-call | flops 738197504 | bytes 8388608 | tf_op jit(solution)/shard_map/coeff/pallas_call | solution.py:134
  35.4 2.1 %coeff.5.refs_6_ = f32[321,32,128]{2,1,0:T(8,128)S(1)} custom-call(s32[16,32]{1,0:T(8,128)S(1)} %get-tuple-element.8.refs_0_, f32[320,32,256]{2,1,0:T(8,128)S(1)} %get-tuple-element.9.refs_1_, f32[2,256,128]{2,1,0:T(8,128)S(1)} %collective-permute-done.refs_2_, f32[2,256,128]{2,1,0:T(8,128)S(1)} %collective-permute-done.2.refs_3_, ...), custom_call_target="tpu_custom_call", output_to_operand_aliasing={{}: (6, {})} | custom-call | flops 738197504 | bytes 8388608 | tf_op jit(solution)/shard_map/coeff/pallas_call | solution.py:134
  37.6 2.1 %coeff.6.refs_6_ = f32[321,32,128]{2,1,0:T(8,128)S(1)} custom-call(s32[16,32]{1,0:T(8,128)S(1)} %get-tuple-element.8.refs_0_, f32[320,32,256]{2,1,0:T(8,128)S(1)} %get-tuple-element.9.refs_1_, f32[2,256,128]{2,1,0:T(8,128)S(1)} %collective-permute-done.6.refs_2_, f32[2,256,128]{2,1,0:T(8,128)S(1)} %collective-permute-done.7.refs_3_, ...), custom_call_target="tpu_custom_call", output_to_operand_aliasing={{}: (6, {})} | custom-call | flops 738197504 | bytes 8388608 | tf_op jit(solution)/shard_map/coeff/pallas_call | solution.py:134
  39.7 2.1 %coeff.7.c_ref = f32[321,32,128]{2,1,0:T(8,128)S(1)} custom-call(s32[16,32]{1,0:T(8,128)S(1)} %get-tuple-element.8.refs_0_, f32[320,32,256]{2,1,0:T(8,128)S(1)} %get-tuple-element.9.refs_1_, f32[2,256,128]{2,1,0:T(8,128)S(1)} %collective-permute-done.1.refs_2_, f32[2,256,128]{2,1,0:T(8,128)S(1)} %collective-permute-done.3.refs_3_, ...), custom_call_target="tpu_custom_call", output_to_operand_aliasing={{}: (6, {})} | custom-call | flops 738197504 | bytes 8388608 | tf_op jit(solution)/shard_map/coeff/pallas_call | solution.py:134
  42.8 1.6 %collective-permute-start.14 = (f32[128,256]{1,0:T(8,128)S(1)}, f32[128,256]{1,0:T(8,128)S(1)}, u32[]{:S(2)}, u32[]{:S(2)}) collective-permute-start(f32[128,256]{1,0:T(8,128)S(1)} %sketch.7), channel_id=1, source_target_pairs={{0,8},{8,0},{16,24},{24,16},{1,9},{9,1},{17,25},{25,17},{2,10},{10... | collective-permute-start | bytes 393224 | tf_op jit(solution)/shard_map/ppermute | solution.py:19
  46.8 2.5 %collective-permute-done.14 = f32[128,256]{1,0:T(8,128)S(1)} collective-permute-done((f32[128,256]{1,0:T(8,128)S(1)}, f32[128,256]{1,0:T(8,128)S(1)}, u32[]{:S(2)}, u32[]{:S(2)}) %collective-permute-start.14) | collective-permute-done | bytes 131104 | tf_op jit(solution)/shard_map/ppermute | solution.py:19
  49.3 2.7 %collective-permute-start.15 = (f32[128,256]{1,0:T(8,128)S(1)}, f32[128,256]{1,0:T(8,128)S(1)}, u32[]{:S(2)}, u32[]{:S(2)}) collective-permute-start(f32[128,256]{1,0:T(8,128)S(1)} %add.21), channel_id=1, source_target_pairs={{0,16},{8,24},{16,0},{24,8},{1,17},{9,25},{17,1},{25,9},{2,18},{10... | collective-permute-start | bytes 393224 | tf_op jit(solution)/shard_map/ppermute | solution.py:19
  52.8 4.9 %collective-permute-done.15.refs_2_ = f32[128,256]{1,0:T(8,128)S(1)} collective-permute-done((f32[128,256]{1,0:T(8,128)S(1)}, f32[128,256]{1,0:T(8,128)S(1)}, u32[]{:S(2)}, u32[]{:S(2)}) %collective-permute-start.15) | collective-permute-done | bytes 131104 | tf_op jit(solution)/shard_map/ppermute | solution.py:19
  58.8 3.4 %collective-permute-start.17 = (f32[72,128]{1,0:T(8,128)S(1)}, f32[72,128]{1,0:T(8,128)S(1)}, u32[]{:S(2)}, u32[]{:S(2)}) collective-permute-start(f32[72,128]{1,0:T(8,128)S(1)} %get-tuple-element.10.refs_0_), channel_id=1, source_target_pairs={{0,16},{8,24},{16,0},{24,8},{1,17},{9,25},{17,1},{25,9},{2,18},{10... | collective-permute-start | bytes 110600 | tf_op jit(solution)/shard_map/ppermute | solution.py:19
  63.3 2.1 %collective-permute-start.18 = (f32[72,128]{1,0:T(8,128)S(1)}, f32[72,128]{1,0:T(8,128)S(1)}, u32[]{:S(2)}, u32[]{:S(2)}) collective-permute-start(f32[72,128]{1,0:T(8,128)S(1)} %slice.38.refs_1_), channel_id=1, source_target_pairs={{0,16},{8,24},{16,0},{24,8},{1,17},{9,25},{17,1},{25,9},{2,18},{10... | collective-permute-start | bytes 110600 | tf_op jit(solution)/shard_map/ppermute | solution.py:19
  66.3 2.2 %collective-permute-done.18.refs_3_ = f32[72,128]{1,0:T(8,128)S(1)} collective-permute-done((f32[72,128]{1,0:T(8,128)S(1)}, f32[72,128]{1,0:T(8,128)S(1)}, u32[]{:S(2)}, u32[]{:S(2)}) %collective-permute-start.18) | collective-permute-done | bytes 36896 | tf_op jit(solution)/shard_map/ppermute | solution.py:19
  69.8 1.5 %collective-permute-start.22 = (f32[72,128]{1,0:T(8,128)S(1)}, f32[72,128]{1,0:T(8,128)S(1)}, u32[]{:S(2)}, u32[]{:S(2)}) collective-permute-start(f32[72,128]{1,0:T(8,128)S(1)} %add.25.refs_9_), channel_id=1, source_target_pairs={{0,4},{1,5},{2,6},{3,7},{4,0},{5,1},{6,2},{7,3},{8,12},{9,13},{10,... | collective-permute-start | bytes 110600 | tf_op jit(solution)/shard_map/ppermute | solution.py:19
  71.8 1.5 %collective-permute-start.21 = (f32[72,128]{1,0:T(8,128)S(1)}, f32[72,128]{1,0:T(8,128)S(1)}, u32[]{:S(2)}, u32[]{:S(2)}) collective-permute-start(f32[72,128]{1,0:T(8,128)S(1)} %add.25.refs_9_), channel_id=1, source_target_pairs={{0,2},{1,3},{2,0},{3,1},{4,6},{5,7},{6,4},{7,5},{8,10},{9,11},{10,... | collective-permute-start | bytes 110600 | tf_op jit(solution)/shard_map/ppermute | solution.py:19
  73.3 2.5 %collective-permute-done.21.refs_12_ = f32[72,128]{1,0:T(8,128)S(1)} collective-permute-done((f32[72,128]{1,0:T(8,128)S(1)}, f32[72,128]{1,0:T(8,128)S(1)}, u32[]{:S(2)}, u32[]{:S(2)}) %collective-permute-start.21) | collective-permute-done | bytes 36896 | tf_op jit(solution)/shard_map/ppermute | solution.py:19
  76.2 10.4 %tree.1 = (f32[4,64,128]{2,1,0:T(8,128)}, f32[4,256,128]{2,1,0:T(8,128)}) custom-call(f32[72,128]{1,0:T(8,128)S(1)} %get-tuple-element.10.refs_0_, f32[72,128]{1,0:T(8,128)S(1)} %slice.38.refs_1_, f32[72,128]{1,0:T(8,128)S(1)} %collective-permute-done.17.refs_2_, f32[72,128]{1,0:T(8,128)S(1)} %collective-permute-done.18.refs_3_, ...), custom_call_target="tpu_custom_call" | custom-call | tf_op jit(solution)/shard_map/tree/pallas_call | solution.py:352
  (58 shorter events, 15.1 us)
Async XLA Ops:
  0.6 19.1 %collective-permute-start.12 = (f32[4,256,128]{2,1,0:T(8,128)}, f32[4,256,128]{2,1,0:T(8,128)S(1)}, u32[]{:S(2)}, u32[]{:S(2)}) collective-permute-start(f32[4,256,128]{2,1,0:T(8,128)} %bitcast.26), channel_id=1, source_target_pairs={{0,1},{1,0},{2,3},{3,2},{4,5},{5,4},{6,7},{7,6},{8,9},{9,8},{10,11... | collective-permute-start | bytes 1572872 | tf_op jit(solution)/shard_map/ppermute | solution.py:19
  2.3 9.7 %collective-permute-start = (f32[2,256,128]{2,1,0:T(8,128)S(1)}, f32[2,256,128]{2,1,0:T(8,128)S(1)}, u32[]{:S(2)}, u32[]{:S(2)}) collective-permute-start(f32[2,256,128]{2,1,0:T(8,128)S(1)} %get-tuple-element.15.refs_2_), channel_id=1, source_target_pairs={{0,2},{1,3},{2,0},{3,1},{4,6},{5,7},{6,4},{7,5},{8,10},{9,11},{10,... | collective-permute-start | bytes 786440 | tf_op jit(solution)/shard_map/ppermute | solution.py:19
  4.8 9.2 %collective-permute-start.2 = (f32[2,256,128]{2,1,0:T(8,128)S(1)}, f32[2,256,128]{2,1,0:T(8,128)S(1)}, u32[]{:S(2)}, u32[]{:S(2)}) collective-permute-start(f32[2,256,128]{2,1,0:T(8,128)S(1)} %get-tuple-element.14.refs_3_), channel_id=1, source_target_pairs={{0,4},{1,5},{2,6},{3,7},{4,0},{5,1},{6,2},{7,3},{8,12},{9,13},{10,... | collective-permute-start | bytes 786440 | tf_op jit(solution)/shard_map/ppermute | solution.py:19
  6.3 13.3 %collective-permute-start.6 = (f32[2,256,128]{2,1,0:T(8,128)S(1)}, f32[2,256,128]{2,1,0:T(8,128)S(1)}, u32[]{:S(2)}, u32[]{:S(2)}) collective-permute-start(f32[2,256,128]{2,1,0:T(8,128)S(1)} %get-tuple-element.15.refs_2_), channel_id=1, source_target_pairs={{0,4},{1,5},{2,6},{3,7},{4,0},{5,1},{6,2},{7,3},{8,12},{9,13},{10,... | collective-permute-start | bytes 786440 | tf_op jit(solution)/shard_map/ppermute | solution.py:19
  6.8 12.9 %collective-permute-start.7 = (f32[2,256,128]{2,1,0:T(8,128)S(1)}, f32[2,256,128]{2,1,0:T(8,128)S(1)}, u32[]{:S(2)}, u32[]{:S(2)}) collective-permute-start(f32[2,256,128]{2,1,0:T(8,128)S(1)} %get-tuple-element.14.refs_3_), channel_id=1, source_target_pairs={{0,2},{1,3},{2,0},{3,1},{4,6},{5,7},{6,4},{7,5},{8,10},{9,11},{10,... | collective-permute-start | bytes 786440 | tf_op jit(solution)/shard_map/ppermute | solution.py:19
  12.0 8.2 %collective-permute-start.10 = (f32[2,256,128]{2,1,0:T(8,128)S(1)}, f32[2,256,128]{2,1,0:T(8,128)S(1)}, u32[]{:S(2)}, u32[]{:S(2)}) collective-permute-start(f32[2,256,128]{2,1,0:T(8,128)S(1)} %collective-permute-done.refs_2_), channel_id=1, source_target_pairs={{0,1},{1,0},{2,3},{3,2},{4,5},{5,4},{6,7},{7,6},{8,9},{9,8},{10,11... | collective-permute-start | bytes 786440 | tf_op jit(solution)/shard_map/ppermute | solution.py:19
  14.0 10.5 %collective-permute-start.1 = (f32[2,256,128]{2,1,0:T(8,128)S(1)}, f32[2,256,128]{2,1,0:T(8,128)S(1)}, u32[]{:S(2)}, u32[]{:S(2)}) collective-permute-start(f32[2,256,128]{2,1,0:T(8,128)S(1)} %collective-permute-done.refs_2_), channel_id=1, source_target_pairs={{0,4},{1,5},{2,6},{3,7},{4,0},{5,1},{6,2},{7,3},{8,12},{9,13},{10,... | collective-permute-start | bytes 786440 | tf_op jit(solution)/shard_map/ppermute | solution.py:19
  19.6 6.8 %collective-permute-start.3 = (f32[2,256,128]{2,1,0:T(8,128)S(1)}, f32[2,256,128]{2,1,0:T(8,128)S(1)}, u32[]{:S(2)}, u32[]{:S(2)}) collective-permute-start(f32[2,256,128]{2,1,0:T(8,128)S(1)} %collective-permute-done.2.refs_3_), channel_id=1, source_target_pairs={{0,2},{1,3},{2,0},{3,1},{4,6},{5,7},{6,4},{7,5},{8,10},{9,11},{10,... | collective-permute-start | bytes 786440 | tf_op jit(solution)/shard_map/ppermute | solution.py:19
  19.7 15.7 %collective-permute-start.11 = (f32[2,256,128]{2,1,0:T(8,128)S(1)}, f32[2,256,128]{2,1,0:T(8,128)S(1)}, u32[]{:S(2)}, u32[]{:S(2)}) collective-permute-start(f32[2,256,128]{2,1,0:T(8,128)S(1)} %collective-permute-done.2.refs_3_), channel_id=1, source_target_pairs={{0,1},{1,0},{2,3},{3,2},{4,5},{5,4},{6,7},{7,6},{8,9},{9,8},{10,11... | collective-permute-start | bytes 786440 | tf_op jit(solution)/shard_map/ppermute | solution.py:19
  19.7 17.8 %collective-permute-start.8 = (f32[2,256,128]{2,1,0:T(8,128)S(1)}, f32[2,256,128]{2,1,0:T(8,128)S(1)}, u32[]{:S(2)}, u32[]{:S(2)}) collective-permute-start(f32[2,256,128]{2,1,0:T(8,128)S(1)} %collective-permute-done.6.refs_2_), channel_id=1, source_target_pairs={{0,1},{1,0},{2,3},{3,2},{4,5},{5,4},{6,7},{7,6},{8,9},{9,8},{10,11... | collective-permute-start | bytes 786440 | tf_op jit(solution)/shard_map/ppermute | solution.py:19
  20.2 17.3 %collective-permute-start.9 = (f32[2,256,128]{2,1,0:T(8,128)S(1)}, f32[2,256,128]{2,1,0:T(8,128)S(1)}, u32[]{:S(2)}, u32[]{:S(2)}) collective-permute-start(f32[2,256,128]{2,1,0:T(8,128)S(1)} %collective-permute-done.7.refs_3_), channel_id=1, source_target_pairs={{0,1},{1,0},{2,3},{3,2},{4,5},{5,4},{6,7},{7,6},{8,9},{9,8},{10,11... | collective-permute-start | bytes 786440 | tf_op jit(solution)/shard_map/ppermute | solution.py:19
  24.5 15.2 %collective-permute-start.4 = (f32[2,256,128]{2,1,0:T(8,128)S(1)}, f32[2,256,128]{2,1,0:T(8,128)S(1)}, u32[]{:S(2)}, u32[]{:S(2)}) collective-permute-start(f32[2,256,128]{2,1,0:T(8,128)S(1)} %collective-permute-done.1.refs_2_), channel_id=1, source_target_pairs={{0,1},{1,0},{2,3},{3,2},{4,5},{5,4},{6,7},{7,6},{8,9},{9,8},{10,11... | collective-permute-start | bytes 786440 | tf_op jit(solution)/shard_map/ppermute | solution.py:19
  26.4 13.3 %collective-permute-start.5 = (f32[2,256,128]{2,1,0:T(8,128)S(1)}, f32[2,256,128]{2,1,0:T(8,128)S(1)}, u32[]{:S(2)}, u32[]{:S(2)}) collective-permute-start(f32[2,256,128]{2,1,0:T(8,128)S(1)} %collective-permute-done.3.refs_3_), channel_id=1, source_target_pairs={{0,1},{1,0},{2,3},{3,2},{4,5},{5,4},{6,7},{7,6},{8,9},{9,8},{10,11... | collective-permute-start | bytes 786440 | tf_op jit(solution)/shard_map/ppermute | solution.py:19
  42.8 6.4 %collective-permute-start.14 = (f32[128,256]{1,0:T(8,128)S(1)}, f32[128,256]{1,0:T(8,128)S(1)}, u32[]{:S(2)}, u32[]{:S(2)}) collective-permute-start(f32[128,256]{1,0:T(8,128)S(1)} %sketch.7), channel_id=1, source_target_pairs={{0,8},{8,0},{16,24},{24,16},{1,9},{9,1},{17,25},{25,17},{2,10},{10... | collective-permute-start | bytes 393224 | tf_op jit(solution)/shard_map/ppermute | solution.py:19
  45.4 7.5 %collective-permute-start.13 = (f32[128,256]{1,0:T(8,128)S(1)}, f32[128,256]{1,0:T(8,128)S(1)}, u32[]{:S(2)}, u32[]{:S(2)}) collective-permute-start(f32[128,256]{1,0:T(8,128)S(1)} %sketch.5), channel_id=1, source_target_pairs={{0,8},{8,0},{16,24},{24,16},{1,9},{9,1},{17,25},{25,17},{2,10},{10... | collective-permute-start | bytes 393224 | tf_op jit(solution)/shard_map/ppermute | solution.py:19
  49.3 8.4 %collective-permute-start.15 = (f32[128,256]{1,0:T(8,128)S(1)}, f32[128,256]{1,0:T(8,128)S(1)}, u32[]{:S(2)}, u32[]{:S(2)}) collective-permute-start(f32[128,256]{1,0:T(8,128)S(1)} %add.21), channel_id=1, source_target_pairs={{0,16},{8,24},{16,0},{24,8},{1,17},{9,25},{17,1},{25,9},{2,18},{10... | collective-permute-start | bytes 393224 | tf_op jit(solution)/shard_map/ppermute | solution.py:19
  58.1 5.1 %collective-permute-start.16 = (f32[200,128]{1,0:T(8,128)S(1)}, f32[200,128]{1,0:T(8,128)S(1)}, u32[]{:S(2)}, u32[]{:S(2)}) collective-permute-start(f32[200,128]{1,0:T(8,128)S(1)} %get-tuple-element.11), channel_id=1, source_target_pairs={{0,8},{8,0},{16,24},{24,16},{1,9},{9,1},{17,25},{25,17},{2,10},{10... | collective-permute-start | bytes 307208 | tf_op jit(solution)/shard_map/ppermute | solution.py:19
  58.8 7.5 %collective-permute-start.17 = (f32[72,128]{1,0:T(8,128)S(1)}, f32[72,128]{1,0:T(8,128)S(1)}, u32[]{:S(2)}, u32[]{:S(2)}) collective-permute-start(f32[72,128]{1,0:T(8,128)S(1)} %get-tuple-element.10.refs_0_), channel_id=1, source_target_pairs={{0,16},{8,24},{16,0},{24,8},{1,17},{9,25},{17,1},{25,9},{2,18},{10... | collective-permute-start | bytes 110600 | tf_op jit(solution)/shard_map/ppermute | solution.py:19
  63.3 5.3 %collective-permute-start.18 = (f32[72,128]{1,0:T(8,128)S(1)}, f32[72,128]{1,0:T(8,128)S(1)}, u32[]{:S(2)}, u32[]{:S(2)}) collective-permute-start(f32[72,128]{1,0:T(8,128)S(1)} %slice.38.refs_1_), channel_id=1, source_target_pairs={{0,16},{8,24},{16,0},{24,8},{1,17},{9,25},{17,1},{25,9},{2,18},{10... | collective-permute-start | bytes 110600 | tf_op jit(solution)/shard_map/ppermute | solution.py:19
  65.4 7.9 %collective-permute-start.19 = (f32[128,128]{1,0:T(8,128)S(1)}, f32[128,128]{1,0:T(8,128)S(1)}, u32[]{:S(2)}, u32[]{:S(2)}) collective-permute-start(f32[128,128]{1,0:T(8,128)S(1)} %pad_maximum_fusion), channel_id=1, source_target_pairs={{0,16},{8,24},{16,0},{24,8},{1,17},{9,25},{17,1},{25,9},{2,18},{10... | collective-permute-start | bytes 196616 | tf_op jit(solution)/shard_map/ppermute | solution.py:19
  68.5 1.3 %collective-permute-start.20 = (f32[72,128]{1,0:T(8,128)S(1)}, f32[72,128]{1,0:T(8,128)S(1)}, u32[]{:S(2)}, u32[]{:S(2)}) collective-permute-start(f32[72,128]{1,0:T(8,128)S(1)} %add_add_fusion.refs_8_), channel_id=1, source_target_pairs={{0,1},{1,0},{2,3},{3,2},{4,5},{5,4},{6,7},{7,6},{8,9},{9,8},{10,11... | collective-permute-start | bytes 110600 | tf_op jit(solution)/shard_map/ppermute | solution.py:19
  69.8 6.0 %collective-permute-start.22 = (f32[72,128]{1,0:T(8,128)S(1)}, f32[72,128]{1,0:T(8,128)S(1)}, u32[]{:S(2)}, u32[]{:S(2)}) collective-permute-start(f32[72,128]{1,0:T(8,128)S(1)} %add.25.refs_9_), channel_id=1, source_target_pairs={{0,4},{1,5},{2,6},{3,7},{4,0},{5,1},{6,2},{7,3},{8,12},{9,13},{10,... | collective-permute-start | bytes 110600 | tf_op jit(solution)/shard_map/ppermute | solution.py:19
  71.3 4.9 %collective-permute-start.23 = (f32[72,128]{1,0:T(8,128)S(1)}, f32[72,128]{1,0:T(8,128)S(1)}, u32[]{:S(2)}, u32[]{:S(2)}) collective-permute-start(f32[72,128]{1,0:T(8,128)S(1)} %add.25.refs_9_), channel_id=1, source_target_pairs={{0,6},{1,7},{2,4},{3,5},{4,2},{5,3},{6,0},{7,1},{8,14},{9,15},{10,... | collective-permute-start | bytes 110600 | tf_op jit(solution)/shard_map/ppermute | solution.py:19
  71.8 4.0 %collective-permute-start.21 = (f32[72,128]{1,0:T(8,128)S(1)}, f32[72,128]{1,0:T(8,128)S(1)}, u32[]{:S(2)}, u32[]{:S(2)}) collective-permute-start(f32[72,128]{1,0:T(8,128)S(1)} %add.25.refs_9_), channel_id=1, source_target_pairs={{0,2},{1,3},{2,0},{3,1},{4,6},{5,7},{6,4},{7,5},{8,10},{9,11},{10,... | collective-permute-start | bytes 110600 | tf_op jit(solution)/shard_map/ppermute | solution.py:19
  (6 other events, 16.2 us)

commit v3 on v2

--- a/solution.py
+++ b/solution.py
@@ -83,7 +83,7 @@
         in_specs=[VM, VM, pl.BlockSpec(memory_space=pltpu.HBM)],
         out_specs=(VM, VM),
         scratch_shapes=[pltpu.SemaphoreType.DMA],
-        compiler_params=pltpu.CompilerParams(vmem_limit_bytes=4 << 20),
+        compiler_params=pltpu.CompilerParams(vmem_limit_bytes=38 << 20),
         cost_estimate=pl.CostEstimate(flops=0, bytes_accessed=24 << 20, transcendentals=0),
         name="slots",
     )(cols, ranks, v)
@@ -206,14 +206,14 @@
 
 def gram_kernel(n_terms, *refs):
     terms = refs[:n_terms]
-    near_ref, far_ref, rows_ref, keep_ref, hold_ref = refs[n_terms:]
+    gram_ref, near_ref, far_ref, keep_ref, hold_ref = refs[n_terms:]
     total = terms[0][...]
     for term in terms[1:]:
         total = total + term[...]
     body, diagonal = pack(dot_full(total, total, ((1,), (1,))))
     half = body.shape[0]
-    far_ref[:half] = body
-    far_ref[half:] = diagonal
+    gram_ref[:half] = body
+    gram_ref[half:] = diagonal
     hold_ref[...] = total.T
     quarter = keep_ref.shape[0]
 
@@ -222,22 +222,19 @@
         return hold_ref[pl.ds(at, quarter), :]
 
     near_ref[:quarter] = rows_of(1)
-    near_ref[quarter : quarter + half] = body
-    near_ref[quarter + half : quarter + half + 8] = diagonal
-    near_ref[quarter + half + 8 :] = rows_of(3)
-    rows_ref[...] = rows_of(2)
+    near_ref[quarter:] = rows_of(3)
+    far_ref[...] = rows_of(2)
     keep_ref[...] = rows_of(0)
 
 
 def gram_of(terms, n_grp):
     p, rows = terms[0].shape
     quarter = rows // n_grp
-    short = p // 2 + 8
     return pl.pallas_call(
         functools.partial(gram_kernel, len(terms)),
         out_shape=tuple(
             jax.ShapeDtypeStruct((height, p), f32)
-            for height in (short + 2 * quarter, short, quarter, quarter)
+            for height in (p // 2 + 8, 2 * quarter, quarter, quarter)
         ),
         in_specs=[VM] * len(terms),
         out_specs=(VM, VM, VM, VM),
@@ -292,12 +289,20 @@
                 m_ref[b, after:, :] = old - change
 
 
+def applied(x, solve):
+    p = x.shape[1]
+    high, low = split(x)
+    dims = (((1,), (1,)), ((), ()))
+    both = lax.dot_general(high, solve, dims, preferred_element_type=f32)
+    both = both + lax.dot_general(low, solve, dims, preferred_element_type=f32)
+    return both[:, :p] + both[:, p:]
+
+
 def tree_kernel(panel, group, n_leaf, n_levels, *refs):
     grams = refs[:n_leaf]
-    rows_in = refs[n_leaf : 2 * n_leaf]
-    lefts = refs[2 * n_leaf : 2 * n_leaf + n_levels]
-    rights = refs[2 * n_leaf + n_levels : 2 * n_leaf + 2 * n_levels]
-    basis_ref, tr_ref, m_ref, pick_ref = refs[2 * n_leaf + 2 * n_levels :]
+    lefts = refs[n_leaf : n_leaf + n_levels]
+    rights = refs[n_leaf + n_levels : n_leaf + 2 * n_levels]
+    solve_ref, tr_ref, m_ref, pick_ref = refs[n_leaf + 2 * n_levels :]
     p = m_ref.shape[1]
     own = lax.axis_index("grp")
     device = lax.axis_index("dev")
@@ -329,38 +334,53 @@
         whole = m_ref[b]
         return jnp.where(ci > ri, whole, jnp.where(ci == ri, 1.0 / whole, 0.0))
 
-    def applied(x, solve):
-        high, low = split(x)
-        dims = (((1,), (1,)), ((), ()))
-        both = lax.dot_general(high, solve, dims, preferred_element_type=f32)
-        both = both + lax.dot_general(low, solve, dims, preferred_element_type=f32)
-        return both[:, :p] + both[:, p:]
-
-    for m in range(n_leaf):
-        leaf = jnp.bitwise_xor(own, m)
-        basis_ref[leaf] = applied(rows_in[m][...], inverse(leaf))
+    for leaf in range(n_leaf):
+        solve_ref[leaf] = inverse(leaf)
     keep = device != lax.axis_size("dev") - 1
     for q, (a, b, node) in enumerate(((0, 1, 4), (2, 3, 5), (4, 5, 6), (7, 8, 9))):
         made = applied(jnp.concatenate([upper(a), upper(b)], axis=0), inverse(node))
         tr_ref[q] = jnp.where(keep, made, 0.0) if q == 3 else made
 
 
-def tree(grams, rows_in, lefts, rights, panel=32, group=4):
-    quarter, p = rows_in[0].shape
+def tree(grams, lefts, rights, panel=32, group=4):
+    p = grams[0].shape[1]
     n_leaf = len(grams)
-    arrays = [*grams, *rows_in, *lefts, *rights]
+    arrays = [*grams, *lefts, *rights]
     return pl.pallas_call(
         functools.partial(tree_kernel, panel, group, n_leaf, len(lefts)),
         out_shape=(
-            jax.ShapeDtypeStruct((n_leaf, quarter, p), f32),
+            jax.ShapeDtypeStruct((n_leaf, 2 * p, p), bf16),
             jax.ShapeDtypeStruct((4, 2 * p, p), f32),
         ),
         in_specs=[VM] * len(arrays),
         out_specs=(VM, VM),
         scratch_shapes=[pltpu.VMEM((10, p, p), f32), pltpu.VMEM((2, *grams[0].shape), f32)],
         compiler_params=pltpu.CompilerParams(vmem_limit_bytes=16 << 20),
+        cost_estimate=pl.CostEstimate(flops=0, bytes_accessed=24 << 20, transcendentals=0),
         name="tree",
     )(*arrays)
+
+
+def basis_kernel(solve_ref, own_ref, near_ref, far_ref, basis_ref):
+    own = lax.axis_index("grp")
+    quarter = own_ref.shape[0]
+    rows = (own_ref[...], near_ref[:quarter], far_ref[:quarter], far_ref[quarter:])
+    for m, value in enumerate(rows):
+        leaf = jnp.bitwise_xor(own, m)
+        basis_ref[leaf] = applied(value, solve_ref[leaf])
+
+
+def basis(solves, own, near, far):
+    n_leaf = solves.shape[0]
+    quarter, p = own.shape
+    return pl.pallas_call(
+        basis_kernel,
+        out_shape=jax.ShapeDtypeStruct((n_leaf, quarter, p), f32),
+        in_specs=[VM] * 4,
+        out_specs=VM,
+        compiler_params=pltpu.CompilerParams(vmem_limit_bytes=8 << 20),
+        name="basis",
+    )(solves, own, near, far)
 
 
 def gathered(omega, dev_count):
@@ -389,7 +409,11 @@
                 order.extend((seen ^ flip) * n_local + first + q for q in range(half))
 
         values = [value for _, _, value in wave]
-        groups.append(values + [swapped(value, "dev", 1) for value in values])
+        others = [swapped(value, "dev", 1) for value in values]
+        if level < max(waves):
+            groups.append(values + others)
+        else:
+            groups.extend([values, others])
     return groups, order
 
 
@@ -413,19 +437,19 @@
     for pieces in groups:
         coeff = coefficients(slots, v, pieces, start, most, unit, coeff)
         start += sum(piece.shape[0] for piece in pieces)
-    across = swapped(sketch(coeff, u, 3, n_blocks), "grp", 1)
-    beside = swapped(sketch(coeff, u, 1, n_blocks), "grp", 1)
-    across = swapped(sketch(coeff, u, 2, n_blocks) + across, "grp", 2)
-    near, far, rows_far, rows_own = gram_of(
-        [sketch(coeff, u, 0, n_blocks), beside, across], grp_count
-    )
-    quarter, short = rows_own.shape[0], far.shape[0]
-    near_in = swapped(near, "grp", 1)
-    far_in = swapped(far, "grp", 2)
-    gram_in = near_in[quarter : quarter + short]
-    pass_in = swapped(gram_in, "grp", 2)
-    grams = [far, gram_in, far_in, pass_in]
-    current = (far + gram_in) + (far_in + pass_in)
+    made = {}
+    for m in (3, 2, 1, 0):
+        made[m] = sketch(coeff, u, m, n_blocks)
+    across = swapped(made[3], "grp", 1)
+    across = swapped(made[2] + across, "grp", 2)
+    beside = swapped(made[1], "grp", 1)
+    gram, rows_near, rows_far, rows_own = gram_of([made[0], beside, across], grp_count)
+    near_in = swapped(gram, "grp", 1)
+    far_in = swapped(gram, "grp", 2)
+    pass_in = swapped(near_in, "grp", 2)
+    rows_near = swapped(rows_near, "grp", 1)
+    grams = [gram, near_in, far_in, pass_in]
+    current = (gram + near_in) + (far_in + pass_in)
     lefts, rights = [], []
     masks = [2**bit for bit in range(dev_count.bit_length() - 1)]
     steps = [masks[:1]] + [masks[at : at + 2] for at in range(1, len(masks), 2)]
@@ -439,9 +463,10 @@
             lefts.append(current)
             rights.append(wider[0] + wider[1])
             current = current + rights[-1]
-    both_in = swapped(jnp.concatenate([rows_far, near_in[quarter + short :]]), "grp", 2)
-    rows_in = [rows_own, near_in[:quarter], both_in[:quarter], both_in[quarter:]]
-    return tree(grams, rows_in, lefts, rights)
+    quarter = rows_own.shape[0]
+    rows_far = swapped(jnp.concatenate([rows_far, rows_near[quarter:]]), "grp", 2)
+    solves, transfer = tree(grams, lefts, rights)
+    return basis(solves, rows_own, rows_near, rows_far), transfer
 
 
 def solution(mesh):

time: 86.8 us -> 87.7 us (1.010)
  Pallas kernels: 24.3 us -> 27.6 us
  local copies, waits for them, and re-layouts: 6.44 us -> 4.01 us
  starting transfers between devices: 22.8 us -> 23.8 us
    pallas_call x1, Pallas kernels: 1.45 us -> 3.99 us  [slot_table(): pl.pallas_call(functools.partial(table_kernel, order, unit, n_local), out...]
    unnamed x12 -> x10, local copies, waits for them, and re-layouts: 5.36 us -> 2.94 us
    pallas_call x0 -> x1, Pallas kernels: none -> 0.96 us  [basis(): pl.pallas_call(basis_kernel, out_shape=jax.ShapeDtypeStruct((n_leaf, quar...]
    ppermute x24 -> x25, starting transfers between devices: 22.8 us -> 23.8 us  [swapped(): return lax.ppermute(value, axis, pairs)]
    ppermute x24 -> x25, waiting for transfers between devices: 32 us -> 31.3 us  [swapped(): return lax.ppermute(value, axis, pairs)]
    pallas_call x4 -> x5, Pallas kernels: 8.52 us -> 8.94 us  [coefficients(): pl.pallas_call(functools.partial(coeff_kernel, most, start, unit, len(pie...]
  transfers between devices with their start and end apart: 24 -> 25, of which waited for: 12 -> 12; matrix products, arithmetic and copies ran while one was open for 1% -> 1% of each run, Pallas kernels for 12% -> 28%
where the time goes in v3:
time: 87.7 us; the launch traced here: 87.5 us
  waiting for transfers between devices  31.3 us (36%)
  Pallas kernels  27.6 us (31%)
  starting transfers between devices  23.8 us (27%)
  local copies, waits for them, and re-layouts  4.01 us (5%)
    ppermute x25, waiting for transfers between devices, swapped(): return lax.ppermute(value, axis, pairs)  31.3 us
    ppermute x25, starting transfers between devices, swapped(): return lax.ppermute(value, axis, pairs)  23.8 us
    pallas_call x1, Pallas kernels, tree(): pl.pallas_call(functools.partial(tree_kernel, panel, group, n_leaf, len(l...  9.95 us
    pallas_call x5, Pallas kernels, coefficients(): pl.pallas_call(functools.partial(coeff_kernel, most, start, unit, len(pie...  8.94 us
    pallas_call x1, Pallas kernels, slot_table(): pl.pallas_call(functools.partial(table_kernel, order, unit, n_local), out...  3.99 us
    pallas_call x4, Pallas kernels, sketch(): pl.pallas_call(functools.partial(sketch_kernel, m, n_blocks), out_shape=j...  3.32 us
    unnamed x10, local copies, waits for them, and re-layouts  2.94 us
  transfers between devices with their start and end apart: 25, of which 12 were waited for; matrix products, arithmetic and copies ran while one was open for 1% of the time, Pallas kernels for 28%

profile of v3, /device:TPU:0, one launch (start us, length us, event | category | flops | bytes accessed | tf_op | source)
XLA Modules:
  0.0 87.5 jit_solution(10183431725243800631)
XLA Ops:
  2.3 2.6 %collective-permute-start = (f32[2,256,128]{2,1,0:T(8,128)S(1)}, f32[2,256,128]{2,1,0:T(8,128)S(1)}, u32[]{:S(2)}, u32[]{:S(2)}) collective-permute-start(f32[2,256,128]{2,1,0:T(8,128)S(1)} %get-tuple-element.19.refs_2_), channel_id=1, source_target_pairs={{0,2},{1,3},{2,0},{3,1},{4,6},{5,7},{6,4},{7,5},{8,10},{9,11},{10,... | collective-permute-start | bytes 786440 | tf_op jit(solution)/shard_map/ppermute | solution.py:19
  4.8 1.5 %collective-permute-start.3 = (f32[2,256,128]{2,1,0:T(8,128)S(1)}, f32[2,256,128]{2,1,0:T(8,128)S(1)}, u32[]{:S(2)}, u32[]{:S(2)}) collective-permute-start(f32[2,256,128]{2,1,0:T(8,128)S(1)} %get-tuple-element.18.refs_3_), channel_id=1, source_target_pairs={{0,4},{1,5},{2,6},{3,7},{4,0},{5,1},{6,2},{7,3},{8,12},{9,13},{10,... | collective-permute-start | bytes 786440 | tf_op jit(solution)/shard_map/ppermute | solution.py:19
  6.9 5.1 %collective-permute-done.refs_2_ = f32[2,256,128]{2,1,0:T(8,128)S(1)} collective-permute-done((f32[2,256,128]{2,1,0:T(8,128)S(1)}, f32[2,256,128]{2,1,0:T(8,128)S(1)}, u32[]{:S(2)}, u32[]{:S(2)}) %collective-permute-start) | collective-permute-done | bytes 262176 | tf_op jit(solution)/shard_map/ppermute | solution.py:19
  12.0 2.0 %collective-permute-done.3.refs_3_ = f32[2,256,128]{2,1,0:T(8,128)S(1)} collective-permute-done((f32[2,256,128]{2,1,0:T(8,128)S(1)}, f32[2,256,128]{2,1,0:T(8,128)S(1)}, u32[]{:S(2)}, u32[]{:S(2)}) %collective-permute-start.3) | collective-permute-done | bytes 262176 | tf_op jit(solution)/shard_map/ppermute | solution.py:19
  14.0 1.5 %collective-permute-start.1 = (f32[2,256,128]{2,1,0:T(8,128)S(1)}, f32[2,256,128]{2,1,0:T(8,128)S(1)}, u32[]{:S(2)}, u32[]{:S(2)}) collective-permute-start(f32[2,256,128]{2,1,0:T(8,128)S(1)} %collective-permute-done.refs_2_), channel_id=1, source_target_pairs={{0,4},{1,5},{2,6},{3,7},{4,0},{5,1},{6,2},{7,3},{8,12},{9,13},{10,... | collective-permute-start | bytes 786440 | tf_op jit(solution)/shard_map/ppermute | solution.py:19
  15.5 4.1 %collective-permute-done.6.refs_2_ = f32[2,256,128]{2,1,0:T(8,128)S(1)} collective-permute-done((f32[2,256,128]{2,1,0:T(8,128)S(1)}, f32[2,256,128]{2,1,0:T(8,128)S(1)}, u32[]{:S(2)}, u32[]{:S(2)}) %collective-permute-start.6) | collective-permute-done | bytes 262176 | tf_op jit(solution)/shard_map/ppermute | solution.py:19
  20.3 4.2 %collective-permute-done.1.refs_2_ = f32[2,256,128]{2,1,0:T(8,128)S(1)} collective-permute-done((f32[2,256,128]{2,1,0:T(8,128)S(1)}, f32[2,256,128]{2,1,0:T(8,128)S(1)}, u32[]{:S(2)}, u32[]{:S(2)}) %collective-permute-start.1) | collective-permute-done | bytes 262176 | tf_op jit(solution)/shard_map/ppermute | solution.py:19
  24.5 1.9 %collective-permute-done.4.refs_3_ = f32[2,256,128]{2,1,0:T(8,128)S(1)} collective-permute-done((f32[2,256,128]{2,1,0:T(8,128)S(1)}, f32[2,256,128]{2,1,0:T(8,128)S(1)}, u32[]{:S(2)}, u32[]{:S(2)}) %collective-permute-start.4) | collective-permute-done | bytes 262176 | tf_op jit(solution)/shard_map/ppermute | solution.py:19
  27.8 4.0 %slots.1 = (s32[16,32]{1,0:T(8,128)S(1)}, f32[320,32,256]{2,1,0:T(8,128)S(1)}) custom-call(s32[4,1,80]{2,1,0:T(1,128)S(1)} %bitcast.23, s32[4,80]{1,0:T(4,128)S(1)} %bitcast.24, f32[320,32,256]{2,1,0:T(8,128)} %bitcast.25), custom_call_target="tpu_custom_call" | custom-call | bytes 25165824 | tf_op jit(solution)/shard_map/slots/pallas_call | solution.py:77
  31.8 2.1 %coeff.5.refs_6_ = f32[321,32,128]{2,1,0:T(8,128)S(1)} custom-call(s32[16,32]{1,0:T(8,128)S(1)} %get-tuple-element.10.refs_0_, f32[320,32,256]{2,1,0:T(8,128)S(1)} %get-tuple-element.11.refs_1_, f32[2,256,128]{2,1,0:T(8,128)S(1)} %get-tuple-element.19.refs_2_, f32[2,256,128]{2,1,0:T(8,128)S(1)} %get-tuple-element.18.refs_3_, ...), custom_call_target="tpu_custom_call" | custom-call | flops 738197504 | bytes 8388608 | tf_op jit(solution)/shard_map/coeff/pallas_call | solution.py:134
  33.9 2.1 %coeff.6.refs_6_ = f32[321,32,128]{2,1,0:T(8,128)S(1)} custom-call(s32[16,32]{1,0:T(8,128)S(1)} %get-tuple-element.10.refs_0_, f32[320,32,256]{2,1,0:T(8,128)S(1)} %get-tuple-element.11.refs_1_, f32[2,256,128]{2,1,0:T(8,128)S(1)} %collective-permute-done.refs_2_, f32[2,256,128]{2,1,0:T(8,128)S(1)} %collective-permute-done.3.refs_3_, ...), custom_call_target="tpu_custom_call", output_to_operand_aliasing={{}: (6, {})} | custom-call | flops 738197504 | bytes 8388608 | tf_op jit(solution)/shard_map/coeff/pallas_call | solution.py:134
  36.0 2.1 %coeff.7.refs_4_ = f32[321,32,128]{2,1,0:T(8,128)S(1)} custom-call(s32[16,32]{1,0:T(8,128)S(1)} %get-tuple-element.10.refs_0_, f32[320,32,256]{2,1,0:T(8,128)S(1)} %get-tuple-element.11.refs_1_, f32[2,256,128]{2,1,0:T(8,128)S(1)} %collective-permute-done.6.refs_2_, ...), custom_call_target="tpu_custom_call", output_to_operand_aliasing={{}: (6, {})} | custom-call | flops 738197504 | bytes 8388608 | tf_op jit(solution)/shard_map/coeff/pallas_call | solution.py:134
  43.3 1.6 %collective-permute-start.14 = (f32[128,256]{1,0:T(8,128)S(1)}, f32[128,256]{1,0:T(8,128)S(1)}, u32[]{:S(2)}, u32[]{:S(2)}) collective-permute-start(f32[128,256]{1,0:T(8,128)S(1)} %sketch.7), channel_id=1, source_target_pairs={{0,8},{8,0},{16,24},{24,16},{1,9},{9,1},{17,25},{25,17},{2,10},{10... | collective-permute-start | bytes 393224 | tf_op jit(solution)/shard_map/ppermute | solution.py:19
  47.1 2.6 %collective-permute-done.14 = f32[128,256]{1,0:T(8,128)S(1)} collective-permute-done((f32[128,256]{1,0:T(8,128)S(1)}, f32[128,256]{1,0:T(8,128)S(1)}, u32[]{:S(2)}, u32[]{:S(2)}) %collective-permute-start.14) | collective-permute-done | bytes 131104 | tf_op jit(solution)/shard_map/ppermute | solution.py:19
  49.7 2.7 %collective-permute-start.15 = (f32[128,256]{1,0:T(8,128)S(1)}, f32[128,256]{1,0:T(8,128)S(1)}, u32[]{:S(2)}, u32[]{:S(2)}) collective-permute-start(f32[128,256]{1,0:T(8,128)S(1)} %add.21), channel_id=1, source_target_pairs={{0,16},{8,24},{16,0},{24,8},{1,17},{9,25},{17,1},{25,9},{2,18},{10... | collective-permute-start | bytes 393224 | tf_op jit(solution)/shard_map/ppermute | solution.py:19
  53.2 4.9 %collective-permute-done.15.refs_2_ = f32[128,256]{1,0:T(8,128)S(1)} collective-permute-done((f32[128,256]{1,0:T(8,128)S(1)}, f32[128,256]{1,0:T(8,128)S(1)}, u32[]{:S(2)}, u32[]{:S(2)}) %collective-permute-start.15) | collective-permute-done | bytes 131104 | tf_op jit(solution)/shard_map/ppermute | solution.py:19
  60.7 2.1 %collective-permute-start.17 = (f32[72,128]{1,0:T(8,128)S(1)}, f32[72,128]{1,0:T(8,128)S(1)}, u32[]{:S(2)}, u32[]{:S(2)}) collective-permute-start(f32[72,128]{1,0:T(8,128)S(1)} %get-tuple-element.12.refs_0_), channel_id=1, source_target_pairs={{0,16},{8,24},{16,0},{24,8},{1,17},{9,25},{17,1},{25,9},{2,18},{10... | collective-permute-start | bytes 110600 | tf_op jit(solution)/shard_map/ppermute | solution.py:19
  62.7 1.9 %collective-permute-start.18 = (f32[72,128]{1,0:T(8,128)S(1)}, f32[72,128]{1,0:T(8,128)S(1)}, u32[]{:S(2)}, u32[]{:S(2)}) collective-permute-start(f32[72,128]{1,0:T(8,128)S(1)} %collective-permute-done.16.refs_1_), channel_id=1, source_target_pairs={{0,16},{8,24},{16,0},{24,8},{1,17},{9,25},{17,1},{25,9},{2,18},{10... | collective-permute-start | bytes 110600 | tf_op jit(solution)/shard_map/ppermute | solution.py:19
  65.9 1.7 %collective-permute-done.18.refs_3_ = f32[72,128]{1,0:T(8,128)S(1)} collective-permute-done((f32[72,128]{1,0:T(8,128)S(1)}, f32[72,128]{1,0:T(8,128)S(1)}, u32[]{:S(2)}, u32[]{:S(2)}) %collective-permute-start.18) | collective-permute-done | bytes 36896 | tf_op jit(solution)/shard_map/ppermute | solution.py:19
  67.7 1.9 %collective-permute-start.24 = (f32[128,128]{1,0:T(8,128)S(1)}, f32[128,128]{1,0:T(8,128)S(1)}, u32[]{:S(2)}, u32[]{:S(2)}) collective-permute-start(f32[128,128]{1,0:T(8,128)S(1)} %pad_maximum_fusion), channel_id=1, source_target_pairs={{0,16},{8,24},{16,0},{24,8},{1,17},{9,25},{17,1},{25,9},{2,18},{10... | collective-permute-start | bytes 196616 | tf_op jit(solution)/shard_map/ppermute | solution.py:19
  70.2 1.5 %collective-permute-start.21 = (f32[72,128]{1,0:T(8,128)S(1)}, f32[72,128]{1,0:T(8,128)S(1)}, u32[]{:S(2)}, u32[]{:S(2)}) collective-permute-start(f32[72,128]{1,0:T(8,128)S(1)} %add.25.refs_5_), channel_id=1, source_target_pairs={{0,4},{1,5},{2,6},{3,7},{4,0},{5,1},{6,2},{7,3},{8,12},{9,13},{10,... | collective-permute-start | bytes 110600 | tf_op jit(solution)/shard_map/ppermute | solution.py:19
  71.7 1.5 %collective-permute-start.22 = (f32[72,128]{1,0:T(8,128)S(1)}, f32[72,128]{1,0:T(8,128)S(1)}, u32[]{:S(2)}, u32[]{:S(2)}) collective-permute-start(f32[72,128]{1,0:T(8,128)S(1)} %add.25.refs_5_), channel_id=1, source_target_pairs={{0,6},{1,7},{2,4},{3,5},{4,2},{5,3},{6,0},{7,1},{8,14},{9,15},{10,... | collective-permute-start | bytes 110600 | tf_op jit(solution)/shard_map/ppermute | solution.py:19
  74.2 2.4 %collective-permute-done.22 = f32[72,128]{1,0:T(8,128)S(1)} collective-permute-done((f32[72,128]{1,0:T(8,128)S(1)}, f32[72,128]{1,0:T(8,128)S(1)}, u32[]{:S(2)}, u32[]{:S(2)}) %collective-permute-start.22) | collective-permute-done | bytes 36896 | tf_op jit(solution)/shard_map/ppermute | solution.py:19
  76.6 10.0 %tree.1 = (bf16[4,256,128]{2,1,0:T(8,128)(2,1)S(1)}, f32[4,256,128]{2,1,0:T(8,128)}) custom-call(f32[72,128]{1,0:T(8,128)S(1)} %get-tuple-element.12.refs_0_, f32[72,128]{1,0:T(8,128)S(1)} %collective-permute-done.16.refs_1_, f32[72,128]{1,0:T(8,128)S(1)} %collective-permute-done.17.refs_2_, f32[72,128]{1,0:T(8,128)S(1)} %collective-permute-done.18.refs_3_, ...), custom_call_target="tpu_custom_call" | custom-call | bytes 25165824 | tf_op jit(solution)/shard_map/tree/pallas_call | solution.py:349
  (58 shorter events, 18.7 us)
Async XLA Ops:
  0.6 19.1 %collective-permute-start.12 = (f32[4,256,128]{2,1,0:T(8,128)}, f32[4,256,128]{2,1,0:T(8,128)S(1)}, u32[]{:S(2)}, u32[]{:S(2)}) collective-permute-start(f32[4,256,128]{2,1,0:T(8,128)} %bitcast.26), channel_id=1, source_target_pairs={{0,1},{1,0},{2,3},{3,2},{4,5},{5,4},{6,7},{7,6},{8,9},{9,8},{10,11... | collective-permute-start | bytes 1572872 | tf_op jit(solution)/shard_map/ppermute | solution.py:19
  2.3 9.7 %collective-permute-start = (f32[2,256,128]{2,1,0:T(8,128)S(1)}, f32[2,256,128]{2,1,0:T(8,128)S(1)}, u32[]{:S(2)}, u32[]{:S(2)}) collective-permute-start(f32[2,256,128]{2,1,0:T(8,128)S(1)} %get-tuple-element.19.refs_2_), channel_id=1, source_target_pairs={{0,2},{1,3},{2,0},{3,1},{4,6},{5,7},{6,4},{7,5},{8,10},{9,11},{10,... | collective-permute-start | bytes 786440 | tf_op jit(solution)/shard_map/ppermute | solution.py:19
  4.8 9.2 %collective-permute-start.3 = (f32[2,256,128]{2,1,0:T(8,128)S(1)}, f32[2,256,128]{2,1,0:T(8,128)S(1)}, u32[]{:S(2)}, u32[]{:S(2)}) collective-permute-start(f32[2,256,128]{2,1,0:T(8,128)S(1)} %get-tuple-element.18.refs_3_), channel_id=1, source_target_pairs={{0,4},{1,5},{2,6},{3,7},{4,0},{5,1},{6,2},{7,3},{8,12},{9,13},{10,... | collective-permute-start | bytes 786440 | tf_op jit(solution)/shard_map/ppermute | solution.py:19
  6.3 13.3 %collective-permute-start.6 = (f32[2,256,128]{2,1,0:T(8,128)S(1)}, f32[2,256,128]{2,1,0:T(8,128)S(1)}, u32[]{:S(2)}, u32[]{:S(2)}) collective-permute-start(f32[2,256,128]{2,1,0:T(8,128)S(1)} %get-tuple-element.19.refs_2_), channel_id=1, source_target_pairs={{0,4},{1,5},{2,6},{3,7},{4,0},{5,1},{6,2},{7,3},{8,12},{9,13},{10,... | collective-permute-start | bytes 786440 | tf_op jit(solution)/shard_map/ppermute | solution.py:19
  6.8 12.9 %collective-permute-start.7 = (f32[2,256,128]{2,1,0:T(8,128)S(1)}, f32[2,256,128]{2,1,0:T(8,128)S(1)}, u32[]{:S(2)}, u32[]{:S(2)}) collective-permute-start(f32[2,256,128]{2,1,0:T(8,128)S(1)} %get-tuple-element.18.refs_3_), channel_id=1, source_target_pairs={{0,2},{1,3},{2,0},{3,1},{4,6},{5,7},{6,4},{7,5},{8,10},{9,11},{10,... | collective-permute-start | bytes 786440 | tf_op jit(solution)/shard_map/ppermute | solution.py:19
  12.0 8.2 %collective-permute-start.10 = (f32[2,256,128]{2,1,0:T(8,128)S(1)}, f32[2,256,128]{2,1,0:T(8,128)S(1)}, u32[]{:S(2)}, u32[]{:S(2)}) collective-permute-start(f32[2,256,128]{2,1,0:T(8,128)S(1)} %collective-permute-done.refs_2_), channel_id=1, source_target_pairs={{0,1},{1,0},{2,3},{3,2},{4,5},{5,4},{6,7},{7,6},{8,9},{9,8},{10,11... | collective-permute-start | bytes 786440 | tf_op jit(solution)/shard_map/ppermute | solution.py:19
  14.0 10.5 %collective-permute-start.1 = (f32[2,256,128]{2,1,0:T(8,128)S(1)}, f32[2,256,128]{2,1,0:T(8,128)S(1)}, u32[]{:S(2)}, u32[]{:S(2)}) collective-permute-start(f32[2,256,128]{2,1,0:T(8,128)S(1)} %collective-permute-done.refs_2_), channel_id=1, source_target_pairs={{0,4},{1,5},{2,6},{3,7},{4,0},{5,1},{6,2},{7,3},{8,12},{9,13},{10,... | collective-permute-start | bytes 786440 | tf_op jit(solution)/shard_map/ppermute | solution.py:19
  19.6 6.8 %collective-permute-start.4 = (f32[2,256,128]{2,1,0:T(8,128)S(1)}, f32[2,256,128]{2,1,0:T(8,128)S(1)}, u32[]{:S(2)}, u32[]{:S(2)}) collective-permute-start(f32[2,256,128]{2,1,0:T(8,128)S(1)} %collective-permute-done.3.refs_3_), channel_id=1, source_target_pairs={{0,2},{1,3},{2,0},{3,1},{4,6},{5,7},{6,4},{7,5},{8,10},{9,11},{10,... | collective-permute-start | bytes 786440 | tf_op jit(solution)/shard_map/ppermute | solution.py:19
  19.7 14.2 %collective-permute-start.11 = (f32[2,256,128]{2,1,0:T(8,128)S(1)}, f32[2,256,128]{2,1,0:T(8,128)S(1)}, u32[]{:S(2)}, u32[]{:S(2)}) collective-permute-start(f32[2,256,128]{2,1,0:T(8,128)S(1)} %collective-permute-done.3.refs_3_), channel_id=1, source_target_pairs={{0,1},{1,0},{2,3},{3,2},{4,5},{5,4},{6,7},{7,6},{8,9},{9,8},{10,11... | collective-permute-start | bytes 786440 | tf_op jit(solution)/shard_map/ppermute | solution.py:19
  19.7 16.3 %collective-permute-start.8 = (f32[2,256,128]{2,1,0:T(8,128)S(1)}, f32[2,256,128]{2,1,0:T(8,128)S(1)}, u32[]{:S(2)}, u32[]{:S(2)}) collective-permute-start(f32[2,256,128]{2,1,0:T(8,128)S(1)} %collective-permute-done.6.refs_2_), channel_id=1, source_target_pairs={{0,1},{1,0},{2,3},{3,2},{4,5},{5,4},{6,7},{7,6},{8,9},{9,8},{10,11... | collective-permute-start | bytes 786440 | tf_op jit(solution)/shard_map/ppermute | solution.py:19
  20.2 15.8 %collective-permute-start.9 = (f32[2,256,128]{2,1,0:T(8,128)S(1)}, f32[2,256,128]{2,1,0:T(8,128)S(1)}, u32[]{:S(2)}, u32[]{:S(2)}) collective-permute-start(f32[2,256,128]{2,1,0:T(8,128)S(1)} %collective-permute-done.7.refs_3_), channel_id=1, source_target_pairs={{0,1},{1,0},{2,3},{3,2},{4,5},{5,4},{6,7},{7,6},{8,9},{9,8},{10,11... | collective-permute-start | bytes 786440 | tf_op jit(solution)/shard_map/ppermute | solution.py:19
  24.5 15.1 %collective-permute-start.2 = (f32[2,256,128]{2,1,0:T(8,128)S(1)}, f32[2,256,128]{2,1,0:T(8,128)S(1)}, u32[]{:S(2)}, u32[]{:S(2)}) collective-permute-start(f32[2,256,128]{2,1,0:T(8,128)S(1)} %collective-permute-done.1.refs_2_), channel_id=1, source_target_pairs={{0,1},{1,0},{2,3},{3,2},{4,5},{5,4},{6,7},{7,6},{8,9},{9,8},{10,11... | collective-permute-start | bytes 786440 | tf_op jit(solution)/shard_map/ppermute | solution.py:19
  26.4 13.1 %collective-permute-start.5 = (f32[2,256,128]{2,1,0:T(8,128)S(1)}, f32[2,256,128]{2,1,0:T(8,128)S(1)}, u32[]{:S(2)}, u32[]{:S(2)}) collective-permute-start(f32[2,256,128]{2,1,0:T(8,128)S(1)} %collective-permute-done.4.refs_3_), channel_id=1, source_target_pairs={{0,1},{1,0},{2,3},{3,2},{4,5},{5,4},{6,7},{7,6},{8,9},{9,8},{10,11... | collective-permute-start | bytes 786440 | tf_op jit(solution)/shard_map/ppermute | solution.py:19
  43.3 6.4 %collective-permute-start.14 = (f32[128,256]{1,0:T(8,128)S(1)}, f32[128,256]{1,0:T(8,128)S(1)}, u32[]{:S(2)}, u32[]{:S(2)}) collective-permute-start(f32[128,256]{1,0:T(8,128)S(1)} %sketch.7), channel_id=1, source_target_pairs={{0,8},{8,0},{16,24},{24,16},{1,9},{9,1},{17,25},{25,17},{2,10},{10... | collective-permute-start | bytes 393224 | tf_op jit(solution)/shard_map/ppermute | solution.py:19
  45.8 7.5 %collective-permute-start.13 = (f32[128,256]{1,0:T(8,128)S(1)}, f32[128,256]{1,0:T(8,128)S(1)}, u32[]{:S(2)}, u32[]{:S(2)}) collective-permute-start(f32[128,256]{1,0:T(8,128)S(1)} %sketch.5), channel_id=1, source_target_pairs={{0,8},{8,0},{16,24},{24,16},{1,9},{9,1},{17,25},{25,17},{2,10},{10... | collective-permute-start | bytes 393224 | tf_op jit(solution)/shard_map/ppermute | solution.py:19
  49.7 8.4 %collective-permute-start.15 = (f32[128,256]{1,0:T(8,128)S(1)}, f32[128,256]{1,0:T(8,128)S(1)}, u32[]{:S(2)}, u32[]{:S(2)}) collective-permute-start(f32[128,256]{1,0:T(8,128)S(1)} %add.21), channel_id=1, source_target_pairs={{0,16},{8,24},{16,0},{24,8},{1,17},{9,25},{17,1},{25,9},{2,18},{10... | collective-permute-start | bytes 393224 | tf_op jit(solution)/shard_map/ppermute | solution.py:19
  58.6 4.2 %collective-permute-start.16 = (f32[72,128]{1,0:T(8,128)S(1)}, f32[72,128]{1,0:T(8,128)S(1)}, u32[]{:S(2)}, u32[]{:S(2)}) collective-permute-start(f32[72,128]{1,0:T(8,128)S(1)} %get-tuple-element.12.refs_0_), channel_id=1, source_target_pairs={{0,8},{8,0},{16,24},{24,16},{1,9},{9,1},{17,25},{25,17},{2,10},{10... | collective-permute-start | bytes 110600 | tf_op jit(solution)/shard_map/ppermute | solution.py:19
  59.3 5.3 %collective-permute-start.23 = (f32[128,128]{1,0:T(8,128)S(1)}, f32[128,128]{1,0:T(8,128)S(1)}, u32[]{:S(2)}, u32[]{:S(2)}) collective-permute-start(f32[128,128]{1,0:T(8,128)S(1)} %get-tuple-element.15), channel_id=1, source_target_pairs={{0,8},{8,0},{16,24},{24,16},{1,9},{9,1},{17,25},{25,17},{2,10},{10... | collective-permute-start | bytes 196616 | tf_op jit(solution)/shard_map/ppermute | solution.py:19
  60.7 5.2 %collective-permute-start.17 = (f32[72,128]{1,0:T(8,128)S(1)}, f32[72,128]{1,0:T(8,128)S(1)}, u32[]{:S(2)}, u32[]{:S(2)}) collective-permute-start(f32[72,128]{1,0:T(8,128)S(1)} %get-tuple-element.12.refs_0_), channel_id=1, source_target_pairs={{0,16},{8,24},{16,0},{24,8},{1,17},{9,25},{17,1},{25,9},{2,18},{10... | collective-permute-start | bytes 110600 | tf_op jit(solution)/shard_map/ppermute | solution.py:19
  62.7 4.9 %collective-permute-start.18 = (f32[72,128]{1,0:T(8,128)S(1)}, f32[72,128]{1,0:T(8,128)S(1)}, u32[]{:S(2)}, u32[]{:S(2)}) collective-permute-start(f32[72,128]{1,0:T(8,128)S(1)} %collective-permute-done.16.refs_1_), channel_id=1, source_target_pairs={{0,16},{8,24},{16,0},{24,8},{1,17},{9,25},{17,1},{25,9},{2,18},{10... | collective-permute-start | bytes 110600 | tf_op jit(solution)/shard_map/ppermute | solution.py:19
  67.7 18.9 %collective-permute-start.24 = (f32[128,128]{1,0:T(8,128)S(1)}, f32[128,128]{1,0:T(8,128)S(1)}, u32[]{:S(2)}, u32[]{:S(2)}) collective-permute-start(f32[128,128]{1,0:T(8,128)S(1)} %pad_maximum_fusion), channel_id=1, source_target_pairs={{0,16},{8,24},{16,0},{24,8},{1,17},{9,25},{17,1},{25,9},{2,18},{10... | collective-permute-start | bytes 196616 | tf_op jit(solution)/shard_map/ppermute | solution.py:19
  69.6 4.0 %collective-permute-start.20 = (f32[72,128]{1,0:T(8,128)S(1)}, f32[72,128]{1,0:T(8,128)S(1)}, u32[]{:S(2)}, u32[]{:S(2)}) collective-permute-start(f32[72,128]{1,0:T(8,128)S(1)} %add.25.refs_5_), channel_id=1, source_target_pairs={{0,2},{1,3},{2,0},{3,1},{4,6},{5,7},{6,4},{7,5},{8,10},{9,11},{10,... | collective-permute-start | bytes 110600 | tf_op jit(solution)/shard_map/ppermute | solution.py:19
  70.2 4.0 %collective-permute-start.21 = (f32[72,128]{1,0:T(8,128)S(1)}, f32[72,128]{1,0:T(8,128)S(1)}, u32[]{:S(2)}, u32[]{:S(2)}) collective-permute-start(f32[72,128]{1,0:T(8,128)S(1)} %add.25.refs_5_), channel_id=1, source_target_pairs={{0,4},{1,5},{2,6},{3,7},{4,0},{5,1},{6,2},{7,3},{8,12},{9,13},{10,... | collective-permute-start | bytes 110600 | tf_op jit(solution)/shard_map/ppermute | solution.py:19
  71.7 4.9 %collective-permute-start.22 = (f32[72,128]{1,0:T(8,128)S(1)}, f32[72,128]{1,0:T(8,128)S(1)}, u32[]{:S(2)}, u32[]{:S(2)}) collective-permute-start(f32[72,128]{1,0:T(8,128)S(1)} %add.25.refs_5_), channel_id=1, source_target_pairs={{0,6},{1,7},{2,4},{3,5},{4,2},{5,3},{6,0},{7,1},{8,14},{9,15},{10,... | collective-permute-start | bytes 110600 | tf_op jit(solution)/shard_map/ppermute | solution.py:19
  (6 other events, 12.5 us)

commit v4 on v3

--- a/solution.py
+++ b/solution.py
@@ -89,10 +89,18 @@
     )(cols, ranks, v)
 
 
-def coeff_kernel(most, start, unit, n_pieces, *refs):
+def coeff_kernel(most, start, unit, n_pieces, part, parts, *refs):
     slot_ref, v_ref = refs[:2]
     pieces = refs[2 : 2 + n_pieces]
-    c_ref, w_ref = refs[-2:]
+    if part is None:
+        c_ref, w_ref = refs[-2:]
+    else:
+        u_ref = refs[2 + n_pieces]
+        c_ref, held_ref, w_ref, sem = refs[-4:]
+        length = u_ref.shape[0] // parts
+        stretch = pl.ds(part * length, length)
+        copy = pltpu.make_async_copy(u_ref.at[stretch], held_ref.at[stretch], sem)
+        copy.start()
     p = pieces[0].shape[2]
     n_all, k, _ = v_ref.shape
     at = 0
@@ -123,27 +131,44 @@
         return 0
 
     lax.fori_loop(0, at, body, 0, unroll=4)
-
-
-def coefficients(slots, v, pieces, start, most, unit, before):
+    if part is not None:
+        copy.wait()
+
+
+def coefficients(slots, v, pieces, start, most, unit, before, u=None, held_u=None, part=None, parts=1):
     n_all, k, rows = v.shape
     p = pieces[0].shape[2]
     held = sum(piece.shape[0] for piece in pieces)
-    chained = before is not None
-    args = [slots, v, *pieces] + ([before] if chained else [])
-    return pl.pallas_call(
-        functools.partial(coeff_kernel, most, start, unit, len(pieces)),
-        out_shape=jax.ShapeDtypeStruct((n_all + 1, k, p), f32),
-        in_specs=[SM, VM] + [VM] * len(pieces) + [VM] * chained,
-        out_specs=VM,
-        scratch_shapes=[pltpu.VMEM((held, rows, 2 * p), bf16)],
-        input_output_aliases={len(args) - 1: 0} if chained else {},
-        compiler_params=pltpu.CompilerParams(vmem_limit_bytes=12 << 20),
+    args = [slots, v, *pieces]
+    specs = [SM] + [VM] * (1 + len(pieces))
+    shapes = [jax.ShapeDtypeStruct((n_all + 1, k, p), f32)]
+    scratch = [pltpu.VMEM((held, rows, 2 * p), bf16)]
+    copying = part is not None
+    if copying:
+        args.append(u)
+        specs.append(pl.BlockSpec(memory_space=pltpu.HBM))
+        shapes.append(jax.ShapeDtypeStruct(u.shape, f32))
+        scratch.append(pltpu.SemaphoreType.DMA)
+    aliases = {}
+    for output, value in enumerate((before, held_u)):
+        if value is not None:
+            aliases[len(args)] = output
+            args.append(value)
+            specs.append(VM)
+    out = pl.pallas_call(
+        functools.partial(coeff_kernel, most, start, unit, len(pieces), part, parts),
+        out_shape=tuple(shapes),
+        in_specs=specs,
+        out_specs=(VM,) * len(shapes),
+        scratch_shapes=scratch,
+        input_output_aliases=aliases,
+        compiler_params=pltpu.CompilerParams(vmem_limit_bytes=(20 if copying else 12) << 20),
         cost_estimate=pl.CostEstimate(
-            flops=held * most * k * rows * p * 8, bytes_accessed=8 << 20, transcendentals=0
+            flops=0, bytes_accessed=held * 192 << 10, transcendentals=0
         ),
         name="coeff",
     )(*args)
+    return out if copying else (out[0], None)
 
 
 def sketch_kernel(m, n_blocks, c_ref, u_ref, o_ref):
@@ -180,28 +205,23 @@
 
 def pack(gram):
     p = gram.shape[0]
-    half = p // 2
-    ri = lax.broadcasted_iota(jnp.int32, (half, p), 0)
-    ci = lax.broadcasted_iota(jnp.int32, (half, p), 1)
-    lower = gram[half:]
-    body = jnp.where(ci < ri, pltpu.roll(lower, half, 1), gram[:half])
-    diagonal = jnp.sum(jnp.where(ci == ri + half, lower, 0.0), axis=0, keepdims=True)
-    return body, jnp.broadcast_to(diagonal, (8, p))
-
-
-def unpack(packed):
+    block = p // 4
+    half = block // 2
+    lane = lax.broadcasted_iota(jnp.int32, (block, p), 1)
+    second = jnp.where(lane < block, pltpu.roll(gram[3 * block :], block, 1), gram[block : 2 * block])
+    third = gram[2 * block : 3 * block]
+    third = jnp.where(lane[:half] < 2 * block, pltpu.roll(third[half:], 2 * block, 1), third[:half])
+    return jnp.concatenate([gram[:block], second, third], axis=0)
+
+
+def unpack_to(ref, index, packed):
     p = packed.shape[1]
-    half = p // 2
-    ri = lax.broadcasted_iota(jnp.int32, (half, p), 0)
-    ci = lax.broadcasted_iota(jnp.int32, (half, p), 1)
-    body = packed[:half]
-    upper = jnp.where(ci >= ri, body, 0.0)
-    lower = jnp.where((ci >= half) & (ci - half < ri), pltpu.roll(body, half, 1), 0.0)
-    lower = jnp.where(ci == ri + half, packed[half : half + 1], lower)
-    once = jnp.concatenate([upper, lower], axis=0)
-    rj = lax.broadcasted_iota(jnp.int32, (p, p), 0)
-    cj = lax.broadcasted_iota(jnp.int32, (p, p), 1)
-    return jnp.where(rj == cj, once, once + once.T)
+    block = p // 4
+    half = block // 2
+    third = packed[2 * block :]
+    ref[index, : 2 * block + half] = packed
+    ref[index, 2 * block + half : 3 * block] = pltpu.roll(third, 2 * block, 1)
+    ref[index, 3 * block :] = pltpu.roll(packed[block : 2 * block], 3 * block, 1)
 
 
 def gram_kernel(n_terms, *refs):
@@ -210,10 +230,7 @@
     total = terms[0][...]
     for term in terms[1:]:
         total = total + term[...]
-    body, diagonal = pack(dot_full(total, total, ((1,), (1,))))
-    half = body.shape[0]
-    gram_ref[:half] = body
-    gram_ref[half:] = diagonal
+    gram_ref[...] = pack(dot_full(total, total, ((1,), (1,))))
     hold_ref[...] = total.T
     quarter = keep_ref.shape[0]
 
@@ -234,7 +251,7 @@
         functools.partial(gram_kernel, len(terms)),
         out_shape=tuple(
             jax.ShapeDtypeStruct((height, p), f32)
-            for height in (p // 2 + 8, 2 * quarter, quarter, quarter)
+            for height in (p // 8 * 5, 2 * quarter, quarter, quarter)
         ),
         in_specs=[VM] * len(terms),
         out_specs=(VM, VM, VM, VM),
@@ -242,6 +259,13 @@
         compiler_params=pltpu.CompilerParams(vmem_limit_bytes=8 << 20),
         name="gram",
     )(*terms)
+
+
+def split3(x):
+    high = x.astype(bf16)
+    rest = x - high.astype(f32)
+    mid = rest.astype(bf16)
+    return high, mid, (rest - mid.astype(f32)).astype(bf16)
 
 
 def factor(m_ref, panel, group):
@@ -282,7 +306,15 @@
                 si = lax.broadcasted_iota(jnp.int32, block.shape, 0)
                 li = lax.broadcasted_iota(jnp.int32, block.shape, 1)
                 right = jnp.where((li < after) & (li - base > si), 0.0, block)
-                change = dot_full(block.T[after:, :], right, ((1,), (0,)))
+                high, mid, low = split3(block)
+                r_high, r_mid, r_low = split3(right)
+                zero = jnp.zeros_like(r_low)
+                lhs = jnp.concatenate([high, mid, low, high], axis=0).T[after:, :]
+                first = jnp.concatenate([r_high, r_high, r_high, r_low], axis=0)
+                second = jnp.concatenate([r_mid, r_mid, zero, zero], axis=0)
+                rhs = jnp.concatenate([first, second], axis=1)
+                both = jnp.dot(lhs, rhs, preferred_element_type=f32)
+                change = both[:, :p] + both[:, p:]
                 old = m_ref[b, after:, :]
                 lj = lax.broadcasted_iota(jnp.int32, old.shape, 1)
                 old = jnp.where((lj >= base) & (lj < after), 0.0, old)
@@ -307,7 +339,7 @@
     own = lax.axis_index("grp")
     device = lax.axis_index("dev")
     for m in range(n_leaf):
-        m_ref[jnp.bitwise_xor(own, m)] = unpack(grams[m][...])
+        unpack_to(m_ref, jnp.bitwise_xor(own, m), grams[m][...])
     m_ref[4] = m_ref[0] + m_ref[1]
     m_ref[5] = m_ref[2] + m_ref[3]
     m_ref[6] = m_ref[4] + m_ref[5]
@@ -320,8 +352,8 @@
             pick_ref[0] = lefts[level][...]
             pick_ref[1] = rights[level][...]
 
-    m_ref[7] = unpack(pick_ref[0])
-    m_ref[8] = unpack(pick_ref[1])
+    unpack_to(m_ref, 7, pick_ref[0])
+    unpack_to(m_ref, 8, pick_ref[1])
     m_ref[9] = m_ref[7] + m_ref[8]
     factor(m_ref, panel, group)
     ri = lax.broadcasted_iota(jnp.int32, (p, p), 0)
@@ -342,8 +374,9 @@
         tr_ref[q] = jnp.where(keep, made, 0.0) if q == 3 else made
 
 
-def tree(grams, lefts, rights, panel=32, group=4):
+def tree(grams, lefts, rights, group=4):
     p = grams[0].shape[1]
+    panel = p // 4
     n_leaf = len(grams)
     arrays = [*grams, *lefts, *rights]
     return pl.pallas_call(
@@ -410,7 +443,7 @@
 
         values = [value for _, _, value in wave]
         others = [swapped(value, "dev", 1) for value in values]
-        if level < max(waves):
+        if level == 0:
             groups.append(values + others)
         else:
             groups.extend([values, others])
@@ -432,14 +465,18 @@
     unit = 2 * width
     columns = jnp.swapaxes(columns[0], 1, 2)
     slots, v = slot_table(tuple(order), columns, ranks[0], v, depth, unit, n_local)
-    coeff = None
+    coeff = held_u = None
     start = 0
-    for pieces in groups:
-        coeff = coefficients(slots, v, pieces, start, most, unit, coeff)
+    for index, pieces in enumerate(groups):
+        if index < 2:
+            copied = (u, held_u, index, 2)
+            coeff, held_u = coefficients(slots, v, pieces, start, most, unit, coeff, *copied)
+        else:
+            coeff, _ = coefficients(slots, v, pieces, start, most, unit, coeff)
         start += sum(piece.shape[0] for piece in pieces)
     made = {}
     for m in (3, 2, 1, 0):
-        made[m] = sketch(coeff, u, m, n_blocks)
+        made[m] = sketch(coeff, held_u, m, n_blocks)
     across = swapped(made[3], "grp", 1)
     across = swapped(made[2] + across, "grp", 2)
     beside = swapped(made[1], "grp", 1)

time: 87.7 us -> 87.5 us (level)
  local copies, waits for them, and re-layouts: 4.01 us -> 2.43 us
  Pallas kernels: 27.6 us -> 28.9 us
    pallas_call x5 -> x6, Pallas kernels: 8.94 us -> 11.6 us  [coefficients(): pl.pallas_call(functools.partial(coeff_kernel, most, start, unit, len(pie...]
    pallas_call x1, Pallas kernels: 9.95 us -> 8.33 us  [tree(): pl.pallas_call(functools.partial(tree_kernel, panel, group, n_leaf, len(l...]
    unnamed x10 -> x4, local copies, waits for them, and re-layouts: 2.94 us -> 1.36 us
  transfers between devices with their start and end apart: 25 -> 25, of which waited for: 12 -> 12; matrix products, arithmetic and copies ran while one was open for 1% -> 1% of each run, Pallas kernels for 28% -> 29%
where the time goes in v4:
time: 87.5 us; the launch traced here: 87.2 us
  waiting for transfers between devices  31.2 us (36%)
  Pallas kernels  28.9 us (33%)
  starting transfers between devices  23.8 us (27%)
  local copies, waits for them, and re-layouts  2.43 us (3%)
    ppermute x25, waiting for transfers between devices, swapped(): return lax.ppermute(value, axis, pairs)  31.2 us
    ppermute x25, starting transfers between devices, swapped(): return lax.ppermute(value, axis, pairs)  23.8 us
    pallas_call x6, Pallas kernels, coefficients(): pl.pallas_call(functools.partial(coeff_kernel, most, start, unit, len(pie...  11.6 us
    pallas_call x1, Pallas kernels, tree(): pl.pallas_call(functools.partial(tree_kernel, panel, group, n_leaf, len(l...  8.33 us
    pallas_call x1, Pallas kernels, slot_table(): pl.pallas_call(functools.partial(table_kernel, order, unit, n_local), out...  3.99 us
    pallas_call x4, Pallas kernels, sketch(): pl.pallas_call(functools.partial(sketch_kernel, m, n_blocks), out_shape=j...  3.59 us
  transfers between devices with their start and end apart: 25, of which 12 were waited for; matrix products, arithmetic and copies ran while one was open for 1% of the time, Pallas kernels for 29%

profile of v4, /device:TPU:0, one launch (start us, length us, event | category | flops | bytes accessed | tf_op | source)
XLA Modules:
  0.0 87.2 jit_solution(17760548114356094104)
XLA Ops:
  2.3 2.6 %collective-permute-start = (f32[2,256,128]{2,1,0:T(8,128)S(1)}, f32[2,256,128]{2,1,0:T(8,128)S(1)}, u32[]{:S(2)}, u32[]{:S(2)}) collective-permute-start(f32[2,256,128]{2,1,0:T(8,128)S(1)} %get-tuple-element.27.refs_2_), channel_id=1, source_target_pairs={{0,2},{1,3},{2,0},{3,1},{4,6},{5,7},{6,4},{7,5},{8,10},{9,11},{10,... | collective-permute-start | bytes 786440 | tf_op jit(solution)/shard_map/ppermute | solution.py:19
  4.8 1.5 %collective-permute-start.3 = (f32[2,256,128]{2,1,0:T(8,128)S(1)}, f32[2,256,128]{2,1,0:T(8,128)S(1)}, u32[]{:S(2)}, u32[]{:S(2)}) collective-permute-start(f32[2,256,128]{2,1,0:T(8,128)S(1)} %get-tuple-element.26.refs_3_), channel_id=1, source_target_pairs={{0,4},{1,5},{2,6},{3,7},{4,0},{5,1},{6,2},{7,3},{8,12},{9,13},{10,... | collective-permute-start | bytes 786440 | tf_op jit(solution)/shard_map/ppermute | solution.py:19
  6.9 5.1 %collective-permute-done.refs_2_ = f32[2,256,128]{2,1,0:T(8,128)S(1)} collective-permute-done((f32[2,256,128]{2,1,0:T(8,128)S(1)}, f32[2,256,128]{2,1,0:T(8,128)S(1)}, u32[]{:S(2)}, u32[]{:S(2)}) %collective-permute-start) | collective-permute-done | bytes 262176 | tf_op jit(solution)/shard_map/ppermute | solution.py:19
  12.0 2.0 %collective-permute-done.3.refs_3_ = f32[2,256,128]{2,1,0:T(8,128)S(1)} collective-permute-done((f32[2,256,128]{2,1,0:T(8,128)S(1)}, f32[2,256,128]{2,1,0:T(8,128)S(1)}, u32[]{:S(2)}, u32[]{:S(2)}) %collective-permute-start.3) | collective-permute-done | bytes 262176 | tf_op jit(solution)/shard_map/ppermute | solution.py:19
  14.0 1.5 %collective-permute-start.1 = (f32[2,256,128]{2,1,0:T(8,128)S(1)}, f32[2,256,128]{2,1,0:T(8,128)S(1)}, u32[]{:S(2)}, u32[]{:S(2)}) collective-permute-start(f32[2,256,128]{2,1,0:T(8,128)S(1)} %collective-permute-done.refs_2_), channel_id=1, source_target_pairs={{0,4},{1,5},{2,6},{3,7},{4,0},{5,1},{6,2},{7,3},{8,12},{9,13},{10,... | collective-permute-start | bytes 786440 | tf_op jit(solution)/shard_map/ppermute | solution.py:19
  15.5 4.1 %collective-permute-done.6.refs_2_ = f32[2,256,128]{2,1,0:T(8,128)S(1)} collective-permute-done((f32[2,256,128]{2,1,0:T(8,128)S(1)}, f32[2,256,128]{2,1,0:T(8,128)S(1)}, u32[]{:S(2)}, u32[]{:S(2)}) %collective-permute-start.6) | collective-permute-done | bytes 262176 | tf_op jit(solution)/shard_map/ppermute | solution.py:19
  20.3 4.2 %collective-permute-done.1.refs_2_ = f32[2,256,128]{2,1,0:T(8,128)S(1)} collective-permute-done((f32[2,256,128]{2,1,0:T(8,128)S(1)}, f32[2,256,128]{2,1,0:T(8,128)S(1)}, u32[]{:S(2)}, u32[]{:S(2)}) %collective-permute-start.1) | collective-permute-done | bytes 262176 | tf_op jit(solution)/shard_map/ppermute | solution.py:19
  24.5 1.9 %collective-permute-done.4.refs_3_ = f32[2,256,128]{2,1,0:T(8,128)S(1)} collective-permute-done((f32[2,256,128]{2,1,0:T(8,128)S(1)}, f32[2,256,128]{2,1,0:T(8,128)S(1)}, u32[]{:S(2)}, u32[]{:S(2)}) %collective-permute-start.4) | collective-permute-done | bytes 262176 | tf_op jit(solution)/shard_map/ppermute | solution.py:19
  27.8 4.0 %slots.1 = (s32[16,32]{1,0:T(8,128)S(1)}, f32[320,32,256]{2,1,0:T(8,128)S(1)}) custom-call(s32[4,1,80]{2,1,0:T(1,128)S(1)} %bitcast.17, s32[4,80]{1,0:T(4,128)S(1)} %bitcast.18, f32[320,32,256]{2,1,0:T(8,128)} %bitcast.21), custom_call_target="tpu_custom_call" | custom-call | bytes 25165824 | tf_op jit(solution)/shard_map/slots/pallas_call | solution.py:77
  31.8 3.2 %coeff.6 = (f32[321,32,128]{2,1,0:T(8,128)S(1)}, f32[320,32,256]{2,1,0:T(8,128)S(1)}) custom-call(s32[16,32]{1,0:T(8,128)S(1)} %get-tuple-element.14.refs_0_, f32[320,32,256]{2,1,0:T(8,128)S(1)} %get-tuple-element.15.refs_1_, f32[2,256,128]{2,1,0:T(8,128)S(1)} %get-tuple-element.27.refs_2_, f32[2,256,128]{2,1,0:T(8,128)S(1)} %get-tuple-element.26.refs_3_, ...), custom_call_target="tpu_custom_call" | custom-call | bytes 1572864 | tf_op jit(solution)/shard_map/coeff/pallas_call | solution.py:158
  35.0 3.2 %coeff.7 = (f32[321,32,128]{2,1,0:T(8,128)S(1)}, f32[320,32,256]{2,1,0:T(8,128)S(1)}) custom-call(s32[16,32]{1,0:T(8,128)S(1)} %get-tuple-element.14.refs_0_, f32[320,32,256]{2,1,0:T(8,128)S(1)} %get-tuple-element.15.refs_1_, f32[2,256,128]{2,1,0:T(8,128)S(1)} %collective-permute-done.refs_2_, ...), custom_call_target="tpu_custom_call", output_to_operand_aliasing={{0}: (7, {}), {1}: (8, {})} | custom-call | bytes 1572864 | tf_op jit(solution)/shard_map/coeff/pallas_call | solution.py:158
  44.4 1.6 %collective-permute-start.14 = (f32[128,256]{1,0:T(8,128)S(1)}, f32[128,256]{1,0:T(8,128)S(1)}, u32[]{:S(2)}, u32[]{:S(2)}) collective-permute-start(f32[128,256]{1,0:T(8,128)S(1)} %sketch.7), channel_id=1, source_target_pairs={{0,8},{8,0},{16,24},{24,16},{1,9},{9,1},{17,25},{25,17},{2,10},{10... | collective-permute-start | bytes 393224 | tf_op jit(solution)/shard_map/ppermute | solution.py:19
  48.4 2.5 %collective-permute-done.14 = f32[128,256]{1,0:T(8,128)S(1)} collective-permute-done((f32[128,256]{1,0:T(8,128)S(1)}, f32[128,256]{1,0:T(8,128)S(1)}, u32[]{:S(2)}, u32[]{:S(2)}) %collective-permute-start.14) | collective-permute-done | bytes 131104 | tf_op jit(solution)/shard_map/ppermute | solution.py:19
  50.9 2.7 %collective-permute-start.15 = (f32[128,256]{1,0:T(8,128)S(1)}, f32[128,256]{1,0:T(8,128)S(1)}, u32[]{:S(2)}, u32[]{:S(2)}) collective-permute-start(f32[128,256]{1,0:T(8,128)S(1)} %add.21), channel_id=1, source_target_pairs={{0,16},{8,24},{16,0},{24,8},{1,17},{9,25},{17,1},{25,9},{2,18},{10... | collective-permute-start | bytes 393224 | tf_op jit(solution)/shard_map/ppermute | solution.py:19
  54.5 4.9 %collective-permute-done.15.refs_2_ = f32[128,256]{1,0:T(8,128)S(1)} collective-permute-done((f32[128,256]{1,0:T(8,128)S(1)}, f32[128,256]{1,0:T(8,128)S(1)}, u32[]{:S(2)}, u32[]{:S(2)}) %collective-permute-start.15) | collective-permute-done | bytes 131104 | tf_op jit(solution)/shard_map/ppermute | solution.py:19
  60.4 1.4 %collective-permute-start.23 = (f32[128,128]{1,0:T(8,128)S(1)}, f32[128,128]{1,0:T(8,128)S(1)}, u32[]{:S(2)}, u32[]{:S(2)}) collective-permute-start(f32[128,128]{1,0:T(8,128)S(1)} %get-tuple-element.23), channel_id=1, source_target_pairs={{0,8},{8,0},{16,24},{24,16},{1,9},{9,1},{17,25},{25,17},{2,10},{10... | collective-permute-start | bytes 196616 | tf_op jit(solution)/shard_map/ppermute | solution.py:19
  61.8 2.1 %collective-permute-start.17 = (f32[80,128]{1,0:T(8,128)S(1)}, f32[80,128]{1,0:T(8,128)S(1)}, u32[]{:S(2)}, u32[]{:S(2)}) collective-permute-start(f32[80,128]{1,0:T(8,128)S(1)} %get-tuple-element.20.refs_0_), channel_id=1, source_target_pairs={{0,16},{8,24},{16,0},{24,8},{1,17},{9,25},{17,1},{25,9},{2,18},{10... | collective-permute-start | bytes 122888 | tf_op jit(solution)/shard_map/ppermute | solution.py:19
  63.9 1.9 %collective-permute-start.18 = (f32[80,128]{1,0:T(8,128)S(1)}, f32[80,128]{1,0:T(8,128)S(1)}, u32[]{:S(2)}, u32[]{:S(2)}) collective-permute-start(f32[80,128]{1,0:T(8,128)S(1)} %collective-permute-done.16.refs_1_), channel_id=1, source_target_pairs={{0,16},{8,24},{16,0},{24,8},{1,17},{9,25},{17,1},{25,9},{2,18},{10... | collective-permute-start | bytes 122888 | tf_op jit(solution)/shard_map/ppermute | solution.py:19
  67.2 1.6 %collective-permute-done.18.refs_3_ = f32[80,128]{1,0:T(8,128)S(1)} collective-permute-done((f32[80,128]{1,0:T(8,128)S(1)}, f32[80,128]{1,0:T(8,128)S(1)}, u32[]{:S(2)}, u32[]{:S(2)}) %collective-permute-start.18) | collective-permute-done | bytes 40992 | tf_op jit(solution)/shard_map/ppermute | solution.py:19
  68.9 1.9 %collective-permute-start.24 = (f32[128,128]{1,0:T(8,128)S(1)}, f32[128,128]{1,0:T(8,128)S(1)}, u32[]{:S(2)}, u32[]{:S(2)}) collective-permute-start(f32[128,128]{1,0:T(8,128)S(1)} %pad_maximum_fusion), channel_id=1, source_target_pairs={{0,16},{8,24},{16,0},{24,8},{1,17},{9,25},{17,1},{25,9},{2,18},{10... | collective-permute-start | bytes 196616 | tf_op jit(solution)/shard_map/ppermute | solution.py:19
  71.5 1.5 %collective-permute-start.21 = (f32[80,128]{1,0:T(8,128)S(1)}, f32[80,128]{1,0:T(8,128)S(1)}, u32[]{:S(2)}, u32[]{:S(2)}) collective-permute-start(f32[80,128]{1,0:T(8,128)S(1)} %add.25.refs_5_), channel_id=1, source_target_pairs={{0,4},{1,5},{2,6},{3,7},{4,0},{5,1},{6,2},{7,3},{8,12},{9,13},{10,... | collective-permute-start | bytes 122888 | tf_op jit(solution)/shard_map/ppermute | solution.py:19
  73.0 1.4 %collective-permute-start.22 = (f32[80,128]{1,0:T(8,128)S(1)}, f32[80,128]{1,0:T(8,128)S(1)}, u32[]{:S(2)}, u32[]{:S(2)}) collective-permute-start(f32[80,128]{1,0:T(8,128)S(1)} %add.25.refs_5_), channel_id=1, source_target_pairs={{0,6},{1,7},{2,4},{3,5},{4,2},{5,3},{6,0},{7,1},{8,14},{9,15},{10,... | collective-permute-start | bytes 122888 | tf_op jit(solution)/shard_map/ppermute | solution.py:19
  75.5 2.4 %collective-permute-done.22 = f32[80,128]{1,0:T(8,128)S(1)} collective-permute-done((f32[80,128]{1,0:T(8,128)S(1)}, f32[80,128]{1,0:T(8,128)S(1)}, u32[]{:S(2)}, u32[]{:S(2)}) %collective-permute-start.22) | collective-permute-done | bytes 40992 | tf_op jit(solution)/shard_map/ppermute | solution.py:19
  77.9 8.3 %tree.1 = (bf16[4,256,128]{2,1,0:T(8,128)(2,1)S(1)}, f32[4,256,128]{2,1,0:T(8,128)}) custom-call(f32[80,128]{1,0:T(8,128)S(1)} %get-tuple-element.20.refs_0_, f32[80,128]{1,0:T(8,128)S(1)} %collective-permute-done.16.refs_1_, f32[80,128]{1,0:T(8,128)S(1)} %collective-permute-done.17.refs_2_, f32[80,128]{1,0:T(8,128)S(1)} %collective-permute-done.18.refs_3_, ...), custom_call_target="tpu_custom_call" | custom-call | bytes 25165824 | tf_op jit(solution)/shard_map/tree/pallas_call | solution.py:382
  (52 shorter events, 18.9 us)
Async XLA Ops:
  0.6 19.1 %collective-permute-start.12 = (f32[4,256,128]{2,1,0:T(8,128)}, f32[4,256,128]{2,1,0:T(8,128)S(1)}, u32[]{:S(2)}, u32[]{:S(2)}) collective-permute-start(f32[4,256,128]{2,1,0:T(8,128)} %bitcast.22), channel_id=1, source_target_pairs={{0,1},{1,0},{2,3},{3,2},{4,5},{5,4},{6,7},{7,6},{8,9},{9,8},{10,11... | collective-permute-start | bytes 1572872 | tf_op jit(solution)/shard_map/ppermute | solution.py:19
  2.3 9.7 %collective-permute-start = (f32[2,256,128]{2,1,0:T(8,128)S(1)}, f32[2,256,128]{2,1,0:T(8,128)S(1)}, u32[]{:S(2)}, u32[]{:S(2)}) collective-permute-start(f32[2,256,128]{2,1,0:T(8,128)S(1)} %get-tuple-element.27.refs_2_), channel_id=1, source_target_pairs={{0,2},{1,3},{2,0},{3,1},{4,6},{5,7},{6,4},{7,5},{8,10},{9,11},{10,... | collective-permute-start | bytes 786440 | tf_op jit(solution)/shard_map/ppermute | solution.py:19
  4.8 9.2 %collective-permute-start.3 = (f32[2,256,128]{2,1,0:T(8,128)S(1)}, f32[2,256,128]{2,1,0:T(8,128)S(1)}, u32[]{:S(2)}, u32[]{:S(2)}) collective-permute-start(f32[2,256,128]{2,1,0:T(8,128)S(1)} %get-tuple-element.26.refs_3_), channel_id=1, source_target_pairs={{0,4},{1,5},{2,6},{3,7},{4,0},{5,1},{6,2},{7,3},{8,12},{9,13},{10,... | collective-permute-start | bytes 786440 | tf_op jit(solution)/shard_map/ppermute | solution.py:19
  6.3 13.3 %collective-permute-start.6 = (f32[2,256,128]{2,1,0:T(8,128)S(1)}, f32[2,256,128]{2,1,0:T(8,128)S(1)}, u32[]{:S(2)}, u32[]{:S(2)}) collective-permute-start(f32[2,256,128]{2,1,0:T(8,128)S(1)} %get-tuple-element.27.refs_2_), channel_id=1, source_target_pairs={{0,4},{1,5},{2,6},{3,7},{4,0},{5,1},{6,2},{7,3},{8,12},{9,13},{10,... | collective-permute-start | bytes 786440 | tf_op jit(solution)/shard_map/ppermute | solution.py:19
  6.8 12.9 %collective-permute-start.8 = (f32[2,256,128]{2,1,0:T(8,128)S(1)}, f32[2,256,128]{2,1,0:T(8,128)S(1)}, u32[]{:S(2)}, u32[]{:S(2)}) collective-permute-start(f32[2,256,128]{2,1,0:T(8,128)S(1)} %get-tuple-element.26.refs_3_), channel_id=1, source_target_pairs={{0,2},{1,3},{2,0},{3,1},{4,6},{5,7},{6,4},{7,5},{8,10},{9,11},{10,... | collective-permute-start | bytes 786440 | tf_op jit(solution)/shard_map/ppermute | solution.py:19
  12.0 8.2 %collective-permute-start.10 = (f32[2,256,128]{2,1,0:T(8,128)S(1)}, f32[2,256,128]{2,1,0:T(8,128)S(1)}, u32[]{:S(2)}, u32[]{:S(2)}) collective-permute-start(f32[2,256,128]{2,1,0:T(8,128)S(1)} %collective-permute-done.refs_2_), channel_id=1, source_target_pairs={{0,1},{1,0},{2,3},{3,2},{4,5},{5,4},{6,7},{7,6},{8,9},{9,8},{10,11... | collective-permute-start | bytes 786440 | tf_op jit(solution)/shard_map/ppermute | solution.py:19
  14.0 10.5 %collective-permute-start.1 = (f32[2,256,128]{2,1,0:T(8,128)S(1)}, f32[2,256,128]{2,1,0:T(8,128)S(1)}, u32[]{:S(2)}, u32[]{:S(2)}) collective-permute-start(f32[2,256,128]{2,1,0:T(8,128)S(1)} %collective-permute-done.refs_2_), channel_id=1, source_target_pairs={{0,4},{1,5},{2,6},{3,7},{4,0},{5,1},{6,2},{7,3},{8,12},{9,13},{10,... | collective-permute-start | bytes 786440 | tf_op jit(solution)/shard_map/ppermute | solution.py:19
  19.6 6.8 %collective-permute-start.4 = (f32[2,256,128]{2,1,0:T(8,128)S(1)}, f32[2,256,128]{2,1,0:T(8,128)S(1)}, u32[]{:S(2)}, u32[]{:S(2)}) collective-permute-start(f32[2,256,128]{2,1,0:T(8,128)S(1)} %collective-permute-done.3.refs_3_), channel_id=1, source_target_pairs={{0,2},{1,3},{2,0},{3,1},{4,6},{5,7},{6,4},{7,5},{8,10},{9,11},{10,... | collective-permute-start | bytes 786440 | tf_op jit(solution)/shard_map/ppermute | solution.py:19
  19.7 15.3 %collective-permute-start.11 = (f32[2,256,128]{2,1,0:T(8,128)S(1)}, f32[2,256,128]{2,1,0:T(8,128)S(1)}, u32[]{:S(2)}, u32[]{:S(2)}) collective-permute-start(f32[2,256,128]{2,1,0:T(8,128)S(1)} %collective-permute-done.3.refs_3_), channel_id=1, source_target_pairs={{0,1},{1,0},{2,3},{3,2},{4,5},{5,4},{6,7},{7,6},{8,9},{9,8},{10,11... | collective-permute-start | bytes 786440 | tf_op jit(solution)/shard_map/ppermute | solution.py:19
  19.7 19.8 %collective-permute-start.7 = (f32[2,256,128]{2,1,0:T(8,128)S(1)}, f32[2,256,128]{2,1,0:T(8,128)S(1)}, u32[]{:S(2)}, u32[]{:S(2)}) collective-permute-start(f32[2,256,128]{2,1,0:T(8,128)S(1)} %collective-permute-done.6.refs_2_), channel_id=1, source_target_pairs={{0,1},{1,0},{2,3},{3,2},{4,5},{5,4},{6,7},{7,6},{8,9},{9,8},{10,11... | collective-permute-start | bytes 786440 | tf_op jit(solution)/shard_map/ppermute | solution.py:19
  20.2 19.3 %collective-permute-start.9 = (f32[2,256,128]{2,1,0:T(8,128)S(1)}, f32[2,256,128]{2,1,0:T(8,128)S(1)}, u32[]{:S(2)}, u32[]{:S(2)}) collective-permute-start(f32[2,256,128]{2,1,0:T(8,128)S(1)} %collective-permute-done.8.refs_3_), channel_id=1, source_target_pairs={{0,1},{1,0},{2,3},{3,2},{4,5},{5,4},{6,7},{7,6},{8,9},{9,8},{10,11... | collective-permute-start | bytes 786440 | tf_op jit(solution)/shard_map/ppermute | solution.py:19
  24.5 17.7 %collective-permute-start.2 = (f32[2,256,128]{2,1,0:T(8,128)S(1)}, f32[2,256,128]{2,1,0:T(8,128)S(1)}, u32[]{:S(2)}, u32[]{:S(2)}) collective-permute-start(f32[2,256,128]{2,1,0:T(8,128)S(1)} %collective-permute-done.1.refs_2_), channel_id=1, source_target_pairs={{0,1},{1,0},{2,3},{3,2},{4,5},{5,4},{6,7},{7,6},{8,9},{9,8},{10,11... | collective-permute-start | bytes 786440 | tf_op jit(solution)/shard_map/ppermute | solution.py:19
  26.4 15.8 %collective-permute-start.5 = (f32[2,256,128]{2,1,0:T(8,128)S(1)}, f32[2,256,128]{2,1,0:T(8,128)S(1)}, u32[]{:S(2)}, u32[]{:S(2)}) collective-permute-start(f32[2,256,128]{2,1,0:T(8,128)S(1)} %collective-permute-done.4.refs_3_), channel_id=1, source_target_pairs={{0,1},{1,0},{2,3},{3,2},{4,5},{5,4},{6,7},{7,6},{8,9},{9,8},{10,11... | collective-permute-start | bytes 786440 | tf_op jit(solution)/shard_map/ppermute | solution.py:19
  44.4 6.4 %collective-permute-start.14 = (f32[128,256]{1,0:T(8,128)S(1)}, f32[128,256]{1,0:T(8,128)S(1)}, u32[]{:S(2)}, u32[]{:S(2)}) collective-permute-start(f32[128,256]{1,0:T(8,128)S(1)} %sketch.7), channel_id=1, source_target_pairs={{0,8},{8,0},{16,24},{24,16},{1,9},{9,1},{17,25},{25,17},{2,10},{10... | collective-permute-start | bytes 393224 | tf_op jit(solution)/shard_map/ppermute | solution.py:19
  47.0 7.5 %collective-permute-start.13 = (f32[128,256]{1,0:T(8,128)S(1)}, f32[128,256]{1,0:T(8,128)S(1)}, u32[]{:S(2)}, u32[]{:S(2)}) collective-permute-start(f32[128,256]{1,0:T(8,128)S(1)} %sketch.5), channel_id=1, source_target_pairs={{0,8},{8,0},{16,24},{24,16},{1,9},{9,1},{17,25},{25,17},{2,10},{10... | collective-permute-start | bytes 393224 | tf_op jit(solution)/shard_map/ppermute | solution.py:19
  50.9 8.4 %collective-permute-start.15 = (f32[128,256]{1,0:T(8,128)S(1)}, f32[128,256]{1,0:T(8,128)S(1)}, u32[]{:S(2)}, u32[]{:S(2)}) collective-permute-start(f32[128,256]{1,0:T(8,128)S(1)} %add.21), channel_id=1, source_target_pairs={{0,16},{8,24},{16,0},{24,8},{1,17},{9,25},{17,1},{25,9},{2,18},{10... | collective-permute-start | bytes 393224 | tf_op jit(solution)/shard_map/ppermute | solution.py:19
  59.8 4.1 %collective-permute-start.16 = (f32[80,128]{1,0:T(8,128)S(1)}, f32[80,128]{1,0:T(8,128)S(1)}, u32[]{:S(2)}, u32[]{:S(2)}) collective-permute-start(f32[80,128]{1,0:T(8,128)S(1)} %get-tuple-element.20.refs_0_), channel_id=1, source_target_pairs={{0,8},{8,0},{16,24},{24,16},{1,9},{9,1},{17,25},{25,17},{2,10},{10... | collective-permute-start | bytes 122888 | tf_op jit(solution)/shard_map/ppermute | solution.py:19
  60.4 5.4 %collective-permute-start.23 = (f32[128,128]{1,0:T(8,128)S(1)}, f32[128,128]{1,0:T(8,128)S(1)}, u32[]{:S(2)}, u32[]{:S(2)}) collective-permute-start(f32[128,128]{1,0:T(8,128)S(1)} %get-tuple-element.23), channel_id=1, source_target_pairs={{0,8},{8,0},{16,24},{24,16},{1,9},{9,1},{17,25},{25,17},{2,10},{10... | collective-permute-start | bytes 196616 | tf_op jit(solution)/shard_map/ppermute | solution.py:19
  61.8 5.4 %collective-permute-start.17 = (f32[80,128]{1,0:T(8,128)S(1)}, f32[80,128]{1,0:T(8,128)S(1)}, u32[]{:S(2)}, u32[]{:S(2)}) collective-permute-start(f32[80,128]{1,0:T(8,128)S(1)} %get-tuple-element.20.refs_0_), channel_id=1, source_target_pairs={{0,16},{8,24},{16,0},{24,8},{1,17},{9,25},{17,1},{25,9},{2,18},{10... | collective-permute-start | bytes 122888 | tf_op jit(solution)/shard_map/ppermute | solution.py:19
  63.9 4.9 %collective-permute-start.18 = (f32[80,128]{1,0:T(8,128)S(1)}, f32[80,128]{1,0:T(8,128)S(1)}, u32[]{:S(2)}, u32[]{:S(2)}) collective-permute-start(f32[80,128]{1,0:T(8,128)S(1)} %collective-permute-done.16.refs_1_), channel_id=1, source_target_pairs={{0,16},{8,24},{16,0},{24,8},{1,17},{9,25},{17,1},{25,9},{2,18},{10... | collective-permute-start | bytes 122888 | tf_op jit(solution)/shard_map/ppermute | solution.py:19
  68.9 17.3 %collective-permute-start.24 = (f32[128,128]{1,0:T(8,128)S(1)}, f32[128,128]{1,0:T(8,128)S(1)}, u32[]{:S(2)}, u32[]{:S(2)}) collective-permute-start(f32[128,128]{1,0:T(8,128)S(1)} %pad_maximum_fusion), channel_id=1, source_target_pairs={{0,16},{8,24},{16,0},{24,8},{1,17},{9,25},{17,1},{25,9},{2,18},{10... | collective-permute-start | bytes 196616 | tf_op jit(solution)/shard_map/ppermute | solution.py:19
  70.9 4.1 %collective-permute-start.20 = (f32[80,128]{1,0:T(8,128)S(1)}, f32[80,128]{1,0:T(8,128)S(1)}, u32[]{:S(2)}, u32[]{:S(2)}) collective-permute-start(f32[80,128]{1,0:T(8,128)S(1)} %add.25.refs_5_), channel_id=1, source_target_pairs={{0,2},{1,3},{2,0},{3,1},{4,6},{5,7},{6,4},{7,5},{8,10},{9,11},{10,... | collective-permute-start | bytes 122888 | tf_op jit(solution)/shard_map/ppermute | solution.py:19
  71.5 4.0 %collective-permute-start.21 = (f32[80,128]{1,0:T(8,128)S(1)}, f32[80,128]{1,0:T(8,128)S(1)}, u32[]{:S(2)}, u32[]{:S(2)}) collective-permute-start(f32[80,128]{1,0:T(8,128)S(1)} %add.25.refs_5_), channel_id=1, source_target_pairs={{0,4},{1,5},{2,6},{3,7},{4,0},{5,1},{6,2},{7,3},{8,12},{9,13},{10,... | collective-permute-start | bytes 122888 | tf_op jit(solution)/shard_map/ppermute | solution.py:19
  73.0 4.9 %collective-permute-start.22 = (f32[80,128]{1,0:T(8,128)S(1)}, f32[80,128]{1,0:T(8,128)S(1)}, u32[]{:S(2)}, u32[]{:S(2)}) collective-permute-start(f32[80,128]{1,0:T(8,128)S(1)} %add.25.refs_5_), channel_id=1, source_target_pairs={{0,6},{1,7},{2,4},{3,5},{4,2},{5,3},{6,0},{7,1},{8,14},{9,15},{10,... | collective-permute-start | bytes 122888 | tf_op jit(solution)/shard_map/ppermute | solution.py:19
  (3 other events, 3.4 us)

commit v5 on v4

--- a/solution.py
+++ b/solution.py
@@ -31,9 +31,17 @@
     )
 
 
-def table_kernel(order, unit, n_local, cols_ref, ranks_ref, v_ref, slot_ref, held_ref, sem):
+def in_hbm(x):
+    return pltpu.with_memory_space_constraint(x, pltpu.HBM)
+
+
+def table_kernel(order, unit, n_local, part, cols_ref, ranks_ref, v_ref, u_ref, *refs):
+    slot_ref, held_ref, held_u_ref, sem, sem_u = refs
     copy = pltpu.make_async_copy(v_ref, held_ref, sem)
     copy.start()
+    stretch = pl.ds(*part)
+    copy_u = pltpu.make_async_copy(u_ref.at[stretch], held_u_ref.at[stretch], sem_u)
+    copy_u.start()
     n_leaf, _, n_blocks = cols_ref.shape
     depth, clusters = slot_ref.shape
     position = lax.broadcasted_iota(jnp.int32, (clusters, 1), 0)
@@ -71,81 +79,74 @@
     index = jnp.where(used > 0.5, index, float(n_leaf * n_blocks))
     slot_ref[...] = index.astype(jnp.int32) * unit + rank.astype(jnp.int32)
     copy.wait()
-
-
-def slot_table(order, cols, ranks, v, depth, unit, n_local):
+    copy_u.wait()
+
+
+def slot_table(order, cols, ranks, v, u, part, depth, unit, n_local):
     return pl.pallas_call(
-        functools.partial(table_kernel, order, unit, n_local),
+        functools.partial(table_kernel, order, unit, n_local, part),
         out_shape=(
             jax.ShapeDtypeStruct((depth, len(order)), jnp.int32),
             jax.ShapeDtypeStruct(v.shape, f32),
+            jax.ShapeDtypeStruct(u.shape, f32),
         ),
-        in_specs=[VM, VM, pl.BlockSpec(memory_space=pltpu.HBM)],
-        out_specs=(VM, VM),
-        scratch_shapes=[pltpu.SemaphoreType.DMA],
-        compiler_params=pltpu.CompilerParams(vmem_limit_bytes=38 << 20),
+        in_specs=[VM, VM] + [pl.BlockSpec(memory_space=pltpu.HBM)] * 2,
+        out_specs=(VM, VM, VM),
+        scratch_shapes=[pltpu.SemaphoreType.DMA, pltpu.SemaphoreType.DMA],
+        compiler_params=pltpu.CompilerParams(vmem_limit_bytes=4 << 20),
         cost_estimate=pl.CostEstimate(flops=0, bytes_accessed=24 << 20, transcendentals=0),
         name="slots",
-    )(cols, ranks, v)
-
-
-def coeff_kernel(most, start, unit, n_pieces, part, parts, *refs):
+    )(cols, ranks, in_hbm(v), in_hbm(u))
+
+
+def coeff_kernel(most, start, unit, n_pieces, part, *refs):
     slot_ref, v_ref = refs[:2]
     pieces = refs[2 : 2 + n_pieces]
     if part is None:
-        c_ref, w_ref = refs[-2:]
+        c_ref = refs[-1]
     else:
         u_ref = refs[2 + n_pieces]
-        c_ref, held_ref, w_ref, sem = refs[-4:]
-        length = u_ref.shape[0] // parts
-        stretch = pl.ds(part * length, length)
+        c_ref, held_ref, sem = refs[-3:]
+        stretch = pl.ds(*part)
         copy = pltpu.make_async_copy(u_ref.at[stretch], held_ref.at[stretch], sem)
         copy.start()
     p = pieces[0].shape[2]
     n_all, k, _ = v_ref.shape
-    at = 0
+    sub = lax.broadcasted_iota(jnp.int32, (k, p), 0)
+    at = start
     for piece in pieces:
         for q in range(piece.shape[0]):
-            high, low = split(piece[q])
-            w_ref[at, :, :p] = high
-            w_ref[at, :, p:] = low
+            w = jnp.concatenate(split(piece[q]), axis=1)
+            highs, lows, ids, kept = [], [], [], []
+            for n in range(most):
+                entry = slot_ref[n, at]
+                b = entry // unit
+                ids.append(b)
+                kept.append(sub < entry % unit)
+                high, low = split(v_ref[jnp.minimum(b, n_all - 1)])
+                highs.append(high)
+                lows.append(low)
+            both = jnp.dot(jnp.concatenate(highs, 0), w, preferred_element_type=f32)
+            both = both + jnp.dot(jnp.concatenate(lows, 0), w, preferred_element_type=f32)
+            total = both[:, :p] + both[:, p:]
+            for n in range(most):
+                c_ref[ids[n]] = jnp.where(kept[n], total[n * k : (n + 1) * k], 0.0)
             at += 1
-    sub = lax.broadcasted_iota(jnp.int32, (k, p), 0)
-
-    def body(j, _):
-        highs, lows, ids, kept = [], [], [], []
-        for n in range(most):
-            entry = slot_ref[n, start + j]
-            b = entry // unit
-            ids.append(b)
-            kept.append(sub < entry % unit)
-            high, low = split(v_ref[jnp.minimum(b, n_all - 1)])
-            highs.append(high)
-            lows.append(low)
-        w = w_ref[j]
-        both = jnp.dot(jnp.concatenate(highs, 0), w, preferred_element_type=f32)
-        both = both + jnp.dot(jnp.concatenate(lows, 0), w, preferred_element_type=f32)
-        total = both[:, :p] + both[:, p:]
-        for n in range(most):
-            c_ref[ids[n]] = jnp.where(kept[n], total[n * k : (n + 1) * k], 0.0)
-        return 0
-
-    lax.fori_loop(0, at, body, 0, unroll=4)
     if part is not None:
         copy.wait()
 
 
-def coefficients(slots, v, pieces, start, most, unit, before, u=None, held_u=None, part=None, parts=1):
-    n_all, k, rows = v.shape
+def coefficients(slots, v, pieces, start, most, unit, before, u=None, held_u=None, part=None):
+    n_all, k, _ = v.shape
     p = pieces[0].shape[2]
     held = sum(piece.shape[0] for piece in pieces)
     args = [slots, v, *pieces]
     specs = [SM] + [VM] * (1 + len(pieces))
     shapes = [jax.ShapeDtypeStruct((n_all + 1, k, p), f32)]
-    scratch = [pltpu.VMEM((held, rows, 2 * p), bf16)]
+    scratch = []
     copying = part is not None
     if copying:
-        args.append(u)
+        args.append(in_hbm(u))
         specs.append(pl.BlockSpec(memory_space=pltpu.HBM))
         shapes.append(jax.ShapeDtypeStruct(u.shape, f32))
         scratch.append(pltpu.SemaphoreType.DMA)
@@ -156,13 +157,13 @@
             args.append(value)
             specs.append(VM)
     out = pl.pallas_call(
-        functools.partial(coeff_kernel, most, start, unit, len(pieces), part, parts),
+        functools.partial(coeff_kernel, most, start, unit, len(pieces), part),
         out_shape=tuple(shapes),
         in_specs=specs,
         out_specs=(VM,) * len(shapes),
         scratch_shapes=scratch,
         input_output_aliases=aliases,
-        compiler_params=pltpu.CompilerParams(vmem_limit_bytes=(20 if copying else 12) << 20),
+        compiler_params=pltpu.CompilerParams(vmem_limit_bytes=12 << 20),
         cost_estimate=pl.CostEstimate(
             flops=0, bytes_accessed=held * 192 << 10, transcendentals=0
         ),
@@ -464,12 +465,16 @@
     depth = -(-most // 8) * 8
     unit = 2 * width
     columns = jnp.swapaxes(columns[0], 1, 2)
-    slots, v = slot_table(tuple(order), columns, ranks[0], v, depth, unit, n_local)
-    coeff = held_u = None
+    cuts = [n_local * n_blocks * tenths // 10 for tenths in (0, 4, 7, 10)]
+    parts = [(low, high - low) for low, high in zip(cuts, cuts[1:])]
+    slots, v, held_u = slot_table(
+        tuple(order), columns, ranks[0], v, u, parts[0], depth, unit, n_local
+    )
+    coeff = None
     start = 0
     for index, pieces in enumerate(groups):
         if index < 2:
-            copied = (u, held_u, index, 2)
+            copied = (u, held_u, parts[index + 1])
             coeff, held_u = coefficients(slots, v, pieces, start, most, unit, coeff, *copied)
         else:
             coeff, _ = coefficients(slots, v, pieces, start, most, unit, coeff)

time: 87.5 us -> 89.2 us (1.019)
  Pallas kernels: 28.9 us -> 30.7 us
    pallas_call x1, Pallas kernels: 3.99 us -> 5.19 us  [slot_table(): pl.pallas_call(functools.partial(table_kernel, order, unit, n_local, part...]
  transfers between devices with their start and end apart: 25 -> 25, of which waited for: 12 -> 12; matrix products, arithmetic and copies ran while one was open for 1% -> 1% of each run, Pallas kernels for 29% -> 30%
where the time goes in v5:
time: 89.2 us; the launch traced here: 89 us
  waiting for transfers between devices  31.2 us (35%)
  Pallas kernels  30.7 us (34%)
  starting transfers between devices  23.8 us (27%)
  local copies, waits for them, and re-layouts  2.43 us (3%)
    ppermute x25, waiting for transfers between devices, swapped(): return lax.ppermute(value, axis, pairs)  31.2 us
    ppermute x25, starting transfers between devices, swapped(): return lax.ppermute(value, axis, pairs)  23.8 us
    pallas_call x6, Pallas kernels, coefficients(): pl.pallas_call(functools.partial(coeff_kernel, most, start, unit, len(pie...  12.2 us
    pallas_call x1, Pallas kernels, tree(): pl.pallas_call(functools.partial(tree_kernel, panel, group, n_leaf, len(l...  8.33 us
    pallas_call x1, Pallas kernels, slot_table(): pl.pallas_call(functools.partial(table_kernel, order, unit, n_local, part...  5.19 us
    pallas_call x4, Pallas kernels, sketch(): pl.pallas_call(functools.partial(sketch_kernel, m, n_blocks), out_shape=j...  3.59 us
  transfers between devices with their start and end apart: 25, of which 12 were waited for; matrix products, arithmetic and copies ran while one was open for 1% of the time, Pallas kernels for 30%

profile of v5, /device:TPU:0, one launch (start us, length us, event | category | flops | bytes accessed | tf_op | source)
XLA Modules:
  0.0 89.0 jit_solution(10221312007958989390)
XLA Ops:
  2.3 2.6 %collective-permute-start = (f32[2,256,128]{2,1,0:T(8,128)S(1)}, f32[2,256,128]{2,1,0:T(8,128)S(1)}, u32[]{:S(2)}, u32[]{:S(2)}) collective-permute-start(f32[2,256,128]{2,1,0:T(8,128)S(1)} %get-tuple-element.29.refs_2_), channel_id=1, source_target_pairs={{0,2},{1,3},{2,0},{3,1},{4,6},{5,7},{6,4},{7,5},{8,10},{9,11},{10,... | collective-permute-start | bytes 786440 | tf_op jit(solution)/shard_map/ppermute | solution.py:19
  4.8 1.5 %collective-permute-start.3 = (f32[2,256,128]{2,1,0:T(8,128)S(1)}, f32[2,256,128]{2,1,0:T(8,128)S(1)}, u32[]{:S(2)}, u32[]{:S(2)}) collective-permute-start(f32[2,256,128]{2,1,0:T(8,128)S(1)} %get-tuple-element.28.refs_3_), channel_id=1, source_target_pairs={{0,4},{1,5},{2,6},{3,7},{4,0},{5,1},{6,2},{7,3},{8,12},{9,13},{10,... | collective-permute-start | bytes 786440 | tf_op jit(solution)/shard_map/ppermute | solution.py:19
  6.9 5.1 %collective-permute-done.refs_2_ = f32[2,256,128]{2,1,0:T(8,128)S(1)} collective-permute-done((f32[2,256,128]{2,1,0:T(8,128)S(1)}, f32[2,256,128]{2,1,0:T(8,128)S(1)}, u32[]{:S(2)}, u32[]{:S(2)}) %collective-permute-start) | collective-permute-done | bytes 262176 | tf_op jit(solution)/shard_map/ppermute | solution.py:19
  12.0 2.0 %collective-permute-done.3.refs_3_ = f32[2,256,128]{2,1,0:T(8,128)S(1)} collective-permute-done((f32[2,256,128]{2,1,0:T(8,128)S(1)}, f32[2,256,128]{2,1,0:T(8,128)S(1)}, u32[]{:S(2)}, u32[]{:S(2)}) %collective-permute-start.3) | collective-permute-done | bytes 262176 | tf_op jit(solution)/shard_map/ppermute | solution.py:19
  14.0 1.5 %collective-permute-start.1 = (f32[2,256,128]{2,1,0:T(8,128)S(1)}, f32[2,256,128]{2,1,0:T(8,128)S(1)}, u32[]{:S(2)}, u32[]{:S(2)}) collective-permute-start(f32[2,256,128]{2,1,0:T(8,128)S(1)} %collective-permute-done.refs_2_), channel_id=1, source_target_pairs={{0,4},{1,5},{2,6},{3,7},{4,0},{5,1},{6,2},{7,3},{8,12},{9,13},{10,... | collective-permute-start | bytes 786440 | tf_op jit(solution)/shard_map/ppermute | solution.py:19
  15.5 4.1 %collective-permute-done.6.refs_2_ = f32[2,256,128]{2,1,0:T(8,128)S(1)} collective-permute-done((f32[2,256,128]{2,1,0:T(8,128)S(1)}, f32[2,256,128]{2,1,0:T(8,128)S(1)}, u32[]{:S(2)}, u32[]{:S(2)}) %collective-permute-start.6) | collective-permute-done | bytes 262176 | tf_op jit(solution)/shard_map/ppermute | solution.py:19
  20.3 4.2 %collective-permute-done.1.refs_2_ = f32[2,256,128]{2,1,0:T(8,128)S(1)} collective-permute-done((f32[2,256,128]{2,1,0:T(8,128)S(1)}, f32[2,256,128]{2,1,0:T(8,128)S(1)}, u32[]{:S(2)}, u32[]{:S(2)}) %collective-permute-start.1) | collective-permute-done | bytes 262176 | tf_op jit(solution)/shard_map/ppermute | solution.py:19
  24.5 1.9 %collective-permute-done.4.refs_3_ = f32[2,256,128]{2,1,0:T(8,128)S(1)} collective-permute-done((f32[2,256,128]{2,1,0:T(8,128)S(1)}, f32[2,256,128]{2,1,0:T(8,128)S(1)}, u32[]{:S(2)}, u32[]{:S(2)}) %collective-permute-start.4) | collective-permute-done | bytes 262176 | tf_op jit(solution)/shard_map/ppermute | solution.py:19
  27.8 5.2 %slots.1 = (s32[16,32]{1,0:T(8,128)S(1)}, f32[320,32,256]{2,1,0:T(8,128)S(1)}, f32[320,32,256]{2,1,0:T(8,128)S(1)}) custom-call(s32[4,1,80]{2,1,0:T(1,128)S(1)} %bitcast.17, s32[4,80]{1,0:T(4,128)S(1)} %bitcast.18, f32[320,32,256]{2,1,0:T(8,128)} %bitcast.22, f32[320,32,256]{2,1,0:T(8,128)} %bitcast.19), custom_call_target="tpu_custom_call" | custom-call | bytes 25165824 | tf_op jit(solution)/shard_map/slots/pallas_call | solution.py:86
  33.0 3.5 %coeff.6 = (f32[321,32,128]{2,1,0:T(8,128)S(1)}, f32[320,32,256]{2,1,0:T(8,128)S(1)}) custom-call(s32[16,32]{1,0:T(8,128)S(1)} %get-tuple-element.15.refs_0_, f32[320,32,256]{2,1,0:T(8,128)S(1)} %get-tuple-element.16.refs_1_, f32[2,256,128]{2,1,0:T(8,128)S(1)} %get-tuple-element.29.refs_2_, ...), custom_call_target="tpu_custom_call", output_to_operand_aliasing={{1}: (6, {})} | custom-call | bytes 1572864 | tf_op jit(solution)/shard_map/coeff/pallas_call | solution.py:159
  36.6 3.5 %coeff.7 = (f32[321,32,128]{2,1,0:T(8,128)S(1)}, f32[320,32,256]{2,1,0:T(8,128)S(1)}) custom-call(s32[16,32]{1,0:T(8,128)S(1)} %get-tuple-element.15.refs_0_, f32[320,32,256]{2,1,0:T(8,128)S(1)} %get-tuple-element.16.refs_1_, f32[2,256,128]{2,1,0:T(8,128)S(1)} %collective-permute-done.refs_2_, ...), custom_call_target="tpu_custom_call", output_to_operand_aliasing={{0}: (7, {}), {1}: (8, {})} | custom-call | bytes 1572864 | tf_op jit(solution)/shard_map/coeff/pallas_call | solution.py:159
  46.2 1.6 %collective-permute-start.14 = (f32[128,256]{1,0:T(8,128)S(1)}, f32[128,256]{1,0:T(8,128)S(1)}, u32[]{:S(2)}, u32[]{:S(2)}) collective-permute-start(f32[128,256]{1,0:T(8,128)S(1)} %sketch.7), channel_id=1, source_target_pairs={{0,8},{8,0},{16,24},{24,16},{1,9},{9,1},{17,25},{25,17},{2,10},{10... | collective-permute-start | bytes 393224 | tf_op jit(solution)/shard_map/ppermute | solution.py:19
  50.2 2.5 %collective-permute-done.14 = f32[128,256]{1,0:T(8,128)S(1)} collective-permute-done((f32[128,256]{1,0:T(8,128)S(1)}, f32[128,256]{1,0:T(8,128)S(1)}, u32[]{:S(2)}, u32[]{:S(2)}) %collective-permute-start.14) | collective-permute-done | bytes 131104 | tf_op jit(solution)/shard_map/ppermute | solution.py:19
  52.7 2.6 %collective-permute-start.15 = (f32[128,256]{1,0:T(8,128)S(1)}, f32[128,256]{1,0:T(8,128)S(1)}, u32[]{:S(2)}, u32[]{:S(2)}) collective-permute-start(f32[128,256]{1,0:T(8,128)S(1)} %add.21), channel_id=1, source_target_pairs={{0,16},{8,24},{16,0},{24,8},{1,17},{9,25},{17,1},{25,9},{2,18},{10... | collective-permute-start | bytes 393224 | tf_op jit(solution)/shard_map/ppermute | solution.py:19
  56.2 4.9 %collective-permute-done.15.refs_2_ = f32[128,256]{1,0:T(8,128)S(1)} collective-permute-done((f32[128,256]{1,0:T(8,128)S(1)}, f32[128,256]{1,0:T(8,128)S(1)}, u32[]{:S(2)}, u32[]{:S(2)}) %collective-permute-start.15) | collective-permute-done | bytes 131104 | tf_op jit(solution)/shard_map/ppermute | solution.py:19
  62.2 1.4 %collective-permute-start.23 = (f32[128,128]{1,0:T(8,128)S(1)}, f32[128,128]{1,0:T(8,128)S(1)}, u32[]{:S(2)}, u32[]{:S(2)}) collective-permute-start(f32[128,128]{1,0:T(8,128)S(1)} %get-tuple-element.25), channel_id=1, source_target_pairs={{0,8},{8,0},{16,24},{24,16},{1,9},{9,1},{17,25},{25,17},{2,10},{10... | collective-permute-start | bytes 196616 | tf_op jit(solution)/shard_map/ppermute | solution.py:19
  63.6 2.0 %collective-permute-start.17 = (f32[80,128]{1,0:T(8,128)S(1)}, f32[80,128]{1,0:T(8,128)S(1)}, u32[]{:S(2)}, u32[]{:S(2)}) collective-permute-start(f32[80,128]{1,0:T(8,128)S(1)} %get-tuple-element.22.refs_0_), channel_id=1, source_target_pairs={{0,16},{8,24},{16,0},{24,8},{1,17},{9,25},{17,1},{25,9},{2,18},{10... | collective-permute-start | bytes 122888 | tf_op jit(solution)/shard_map/ppermute | solution.py:19
  65.7 1.9 %collective-permute-start.18 = (f32[80,128]{1,0:T(8,128)S(1)}, f32[80,128]{1,0:T(8,128)S(1)}, u32[]{:S(2)}, u32[]{:S(2)}) collective-permute-start(f32[80,128]{1,0:T(8,128)S(1)} %collective-permute-done.16.refs_1_), channel_id=1, source_target_pairs={{0,16},{8,24},{16,0},{24,8},{1,17},{9,25},{17,1},{25,9},{2,18},{10... | collective-permute-start | bytes 122888 | tf_op jit(solution)/shard_map/ppermute | solution.py:19
  69.0 1.6 %collective-permute-done.18.refs_3_ = f32[80,128]{1,0:T(8,128)S(1)} collective-permute-done((f32[80,128]{1,0:T(8,128)S(1)}, f32[80,128]{1,0:T(8,128)S(1)}, u32[]{:S(2)}, u32[]{:S(2)}) %collective-permute-start.18) | collective-permute-done | bytes 40992 | tf_op jit(solution)/shard_map/ppermute | solution.py:19
  70.7 1.9 %collective-permute-start.24 = (f32[128,128]{1,0:T(8,128)S(1)}, f32[128,128]{1,0:T(8,128)S(1)}, u32[]{:S(2)}, u32[]{:S(2)}) collective-permute-start(f32[128,128]{1,0:T(8,128)S(1)} %pad_maximum_fusion), channel_id=1, source_target_pairs={{0,16},{8,24},{16,0},{24,8},{1,17},{9,25},{17,1},{25,9},{2,18},{10... | collective-permute-start | bytes 196616 | tf_op jit(solution)/shard_map/ppermute | solution.py:19
  73.2 1.5 %collective-permute-start.21 = (f32[80,128]{1,0:T(8,128)S(1)}, f32[80,128]{1,0:T(8,128)S(1)}, u32[]{:S(2)}, u32[]{:S(2)}) collective-permute-start(f32[80,128]{1,0:T(8,128)S(1)} %add.25.refs_5_), channel_id=1, source_target_pairs={{0,4},{1,5},{2,6},{3,7},{4,0},{5,1},{6,2},{7,3},{8,12},{9,13},{10,... | collective-permute-start | bytes 122888 | tf_op jit(solution)/shard_map/ppermute | solution.py:19
  74.8 1.4 %collective-permute-start.22 = (f32[80,128]{1,0:T(8,128)S(1)}, f32[80,128]{1,0:T(8,128)S(1)}, u32[]{:S(2)}, u32[]{:S(2)}) collective-permute-start(f32[80,128]{1,0:T(8,128)S(1)} %add.25.refs_5_), channel_id=1, source_target_pairs={{0,6},{1,7},{2,4},{3,5},{4,2},{5,3},{6,0},{7,1},{8,14},{9,15},{10,... | collective-permute-start | bytes 122888 | tf_op jit(solution)/shard_map/ppermute | solution.py:19
  77.2 2.4 %collective-permute-done.22 = f32[80,128]{1,0:T(8,128)S(1)} collective-permute-done((f32[80,128]{1,0:T(8,128)S(1)}, f32[80,128]{1,0:T(8,128)S(1)}, u32[]{:S(2)}, u32[]{:S(2)}) %collective-permute-start.22) | collective-permute-done | bytes 40992 | tf_op jit(solution)/shard_map/ppermute | solution.py:19
  79.7 8.3 %tree.1 = (bf16[4,256,128]{2,1,0:T(8,128)(2,1)S(1)}, f32[4,256,128]{2,1,0:T(8,128)}) custom-call(f32[80,128]{1,0:T(8,128)S(1)} %get-tuple-element.22.refs_0_, f32[80,128]{1,0:T(8,128)S(1)} %collective-permute-done.16.refs_1_, f32[80,128]{1,0:T(8,128)S(1)} %collective-permute-done.17.refs_2_, f32[80,128]{1,0:T(8,128)S(1)} %collective-permute-done.18.refs_3_, ...), custom_call_target="tpu_custom_call" | custom-call | bytes 25165824 | tf_op jit(solution)/shard_map/tree/pallas_call | solution.py:383
  (52 shorter events, 18.7 us)
Async XLA Ops:
  0.6 19.1 %collective-permute-start.12 = (f32[4,256,128]{2,1,0:T(8,128)}, f32[4,256,128]{2,1,0:T(8,128)S(1)}, u32[]{:S(2)}, u32[]{:S(2)}) collective-permute-start(f32[4,256,128]{2,1,0:T(8,128)} %bitcast.23), channel_id=1, source_target_pairs={{0,1},{1,0},{2,3},{3,2},{4,5},{5,4},{6,7},{7,6},{8,9},{9,8},{10,11... | collective-permute-start | bytes 1572872 | tf_op jit(solution)/shard_map/ppermute | solution.py:19
  2.3 9.7 %collective-permute-start = (f32[2,256,128]{2,1,0:T(8,128)S(1)}, f32[2,256,128]{2,1,0:T(8,128)S(1)}, u32[]{:S(2)}, u32[]{:S(2)}) collective-permute-start(f32[2,256,128]{2,1,0:T(8,128)S(1)} %get-tuple-element.29.refs_2_), channel_id=1, source_target_pairs={{0,2},{1,3},{2,0},{3,1},{4,6},{5,7},{6,4},{7,5},{8,10},{9,11},{10,... | collective-permute-start | bytes 786440 | tf_op jit(solution)/shard_map/ppermute | solution.py:19
  4.8 9.2 %collective-permute-start.3 = (f32[2,256,128]{2,1,0:T(8,128)S(1)}, f32[2,256,128]{2,1,0:T(8,128)S(1)}, u32[]{:S(2)}, u32[]{:S(2)}) collective-permute-start(f32[2,256,128]{2,1,0:T(8,128)S(1)} %get-tuple-element.28.refs_3_), channel_id=1, source_target_pairs={{0,4},{1,5},{2,6},{3,7},{4,0},{5,1},{6,2},{7,3},{8,12},{9,13},{10,... | collective-permute-start | bytes 786440 | tf_op jit(solution)/shard_map/ppermute | solution.py:19
  6.3 13.3 %collective-permute-start.6 = (f32[2,256,128]{2,1,0:T(8,128)S(1)}, f32[2,256,128]{2,1,0:T(8,128)S(1)}, u32[]{:S(2)}, u32[]{:S(2)}) collective-permute-start(f32[2,256,128]{2,1,0:T(8,128)S(1)} %get-tuple-element.29.refs_2_), channel_id=1, source_target_pairs={{0,4},{1,5},{2,6},{3,7},{4,0},{5,1},{6,2},{7,3},{8,12},{9,13},{10,... | collective-permute-start | bytes 786440 | tf_op jit(solution)/shard_map/ppermute | solution.py:19
  6.8 12.9 %collective-permute-start.8 = (f32[2,256,128]{2,1,0:T(8,128)S(1)}, f32[2,256,128]{2,1,0:T(8,128)S(1)}, u32[]{:S(2)}, u32[]{:S(2)}) collective-permute-start(f32[2,256,128]{2,1,0:T(8,128)S(1)} %get-tuple-element.28.refs_3_), channel_id=1, source_target_pairs={{0,2},{1,3},{2,0},{3,1},{4,6},{5,7},{6,4},{7,5},{8,10},{9,11},{10,... | collective-permute-start | bytes 786440 | tf_op jit(solution)/shard_map/ppermute | solution.py:19
  12.0 8.2 %collective-permute-start.10 = (f32[2,256,128]{2,1,0:T(8,128)S(1)}, f32[2,256,128]{2,1,0:T(8,128)S(1)}, u32[]{:S(2)}, u32[]{:S(2)}) collective-permute-start(f32[2,256,128]{2,1,0:T(8,128)S(1)} %collective-permute-done.refs_2_), channel_id=1, source_target_pairs={{0,1},{1,0},{2,3},{3,2},{4,5},{5,4},{6,7},{7,6},{8,9},{9,8},{10,11... | collective-permute-start | bytes 786440 | tf_op jit(solution)/shard_map/ppermute | solution.py:19
  14.0 10.5 %collective-permute-start.1 = (f32[2,256,128]{2,1,0:T(8,128)S(1)}, f32[2,256,128]{2,1,0:T(8,128)S(1)}, u32[]{:S(2)}, u32[]{:S(2)}) collective-permute-start(f32[2,256,128]{2,1,0:T(8,128)S(1)} %collective-permute-done.refs_2_), channel_id=1, source_target_pairs={{0,4},{1,5},{2,6},{3,7},{4,0},{5,1},{6,2},{7,3},{8,12},{9,13},{10,... | collective-permute-start | bytes 786440 | tf_op jit(solution)/shard_map/ppermute | solution.py:19
  19.6 6.8 %collective-permute-start.4 = (f32[2,256,128]{2,1,0:T(8,128)S(1)}, f32[2,256,128]{2,1,0:T(8,128)S(1)}, u32[]{:S(2)}, u32[]{:S(2)}) collective-permute-start(f32[2,256,128]{2,1,0:T(8,128)S(1)} %collective-permute-done.3.refs_3_), channel_id=1, source_target_pairs={{0,2},{1,3},{2,0},{3,1},{4,6},{5,7},{6,4},{7,5},{8,10},{9,11},{10,... | collective-permute-start | bytes 786440 | tf_op jit(solution)/shard_map/ppermute | solution.py:19
  19.7 16.9 %collective-permute-start.11 = (f32[2,256,128]{2,1,0:T(8,128)S(1)}, f32[2,256,128]{2,1,0:T(8,128)S(1)}, u32[]{:S(2)}, u32[]{:S(2)}) collective-permute-start(f32[2,256,128]{2,1,0:T(8,128)S(1)} %collective-permute-done.3.refs_3_), channel_id=1, source_target_pairs={{0,1},{1,0},{2,3},{3,2},{4,5},{5,4},{6,7},{7,6},{8,9},{9,8},{10,11... | collective-permute-start | bytes 786440 | tf_op jit(solution)/shard_map/ppermute | solution.py:19
  19.7 21.7 %collective-permute-start.7 = (f32[2,256,128]{2,1,0:T(8,128)S(1)}, f32[2,256,128]{2,1,0:T(8,128)S(1)}, u32[]{:S(2)}, u32[]{:S(2)}) collective-permute-start(f32[2,256,128]{2,1,0:T(8,128)S(1)} %collective-permute-done.6.refs_2_), channel_id=1, source_target_pairs={{0,1},{1,0},{2,3},{3,2},{4,5},{5,4},{6,7},{7,6},{8,9},{9,8},{10,11... | collective-permute-start | bytes 786440 | tf_op jit(solution)/shard_map/ppermute | solution.py:19
  20.2 21.2 %collective-permute-start.9 = (f32[2,256,128]{2,1,0:T(8,128)S(1)}, f32[2,256,128]{2,1,0:T(8,128)S(1)}, u32[]{:S(2)}, u32[]{:S(2)}) collective-permute-start(f32[2,256,128]{2,1,0:T(8,128)S(1)} %collective-permute-done.8.refs_3_), channel_id=1, source_target_pairs={{0,1},{1,0},{2,3},{3,2},{4,5},{5,4},{6,7},{7,6},{8,9},{9,8},{10,11... | collective-permute-start | bytes 786440 | tf_op jit(solution)/shard_map/ppermute | solution.py:19
  24.5 19.5 %collective-permute-start.2 = (f32[2,256,128]{2,1,0:T(8,128)S(1)}, f32[2,256,128]{2,1,0:T(8,128)S(1)}, u32[]{:S(2)}, u32[]{:S(2)}) collective-permute-start(f32[2,256,128]{2,1,0:T(8,128)S(1)} %collective-permute-done.1.refs_2_), channel_id=1, source_target_pairs={{0,1},{1,0},{2,3},{3,2},{4,5},{5,4},{6,7},{7,6},{8,9},{9,8},{10,11... | collective-permute-start | bytes 786440 | tf_op jit(solution)/shard_map/ppermute | solution.py:19
  26.4 17.6 %collective-permute-start.5 = (f32[2,256,128]{2,1,0:T(8,128)S(1)}, f32[2,256,128]{2,1,0:T(8,128)S(1)}, u32[]{:S(2)}, u32[]{:S(2)}) collective-permute-start(f32[2,256,128]{2,1,0:T(8,128)S(1)} %collective-permute-done.4.refs_3_), channel_id=1, source_target_pairs={{0,1},{1,0},{2,3},{3,2},{4,5},{5,4},{6,7},{7,6},{8,9},{9,8},{10,11... | collective-permute-start | bytes 786440 | tf_op jit(solution)/shard_map/ppermute | solution.py:19
  46.2 6.4 %collective-permute-start.14 = (f32[128,256]{1,0:T(8,128)S(1)}, f32[128,256]{1,0:T(8,128)S(1)}, u32[]{:S(2)}, u32[]{:S(2)}) collective-permute-start(f32[128,256]{1,0:T(8,128)S(1)} %sketch.7), channel_id=1, source_target_pairs={{0,8},{8,0},{16,24},{24,16},{1,9},{9,1},{17,25},{25,17},{2,10},{10... | collective-permute-start | bytes 393224 | tf_op jit(solution)/shard_map/ppermute | solution.py:19
  48.8 7.5 %collective-permute-start.13 = (f32[128,256]{1,0:T(8,128)S(1)}, f32[128,256]{1,0:T(8,128)S(1)}, u32[]{:S(2)}, u32[]{:S(2)}) collective-permute-start(f32[128,256]{1,0:T(8,128)S(1)} %sketch.5), channel_id=1, source_target_pairs={{0,8},{8,0},{16,24},{24,16},{1,9},{9,1},{17,25},{25,17},{2,10},{10... | collective-permute-start | bytes 393224 | tf_op jit(solution)/shard_map/ppermute | solution.py:19
  52.7 8.4 %collective-permute-start.15 = (f32[128,256]{1,0:T(8,128)S(1)}, f32[128,256]{1,0:T(8,128)S(1)}, u32[]{:S(2)}, u32[]{:S(2)}) collective-permute-start(f32[128,256]{1,0:T(8,128)S(1)} %add.21), channel_id=1, source_target_pairs={{0,16},{8,24},{16,0},{24,8},{1,17},{9,25},{17,1},{25,9},{2,18},{10... | collective-permute-start | bytes 393224 | tf_op jit(solution)/shard_map/ppermute | solution.py:19
  61.5 4.1 %collective-permute-start.16 = (f32[80,128]{1,0:T(8,128)S(1)}, f32[80,128]{1,0:T(8,128)S(1)}, u32[]{:S(2)}, u32[]{:S(2)}) collective-permute-start(f32[80,128]{1,0:T(8,128)S(1)} %get-tuple-element.22.refs_0_), channel_id=1, source_target_pairs={{0,8},{8,0},{16,24},{24,16},{1,9},{9,1},{17,25},{25,17},{2,10},{10... | collective-permute-start | bytes 122888 | tf_op jit(solution)/shard_map/ppermute | solution.py:19
  62.2 5.4 %collective-permute-start.23 = (f32[128,128]{1,0:T(8,128)S(1)}, f32[128,128]{1,0:T(8,128)S(1)}, u32[]{:S(2)}, u32[]{:S(2)}) collective-permute-start(f32[128,128]{1,0:T(8,128)S(1)} %get-tuple-element.25), channel_id=1, source_target_pairs={{0,8},{8,0},{16,24},{24,16},{1,9},{9,1},{17,25},{25,17},{2,10},{10... | collective-permute-start | bytes 196616 | tf_op jit(solution)/shard_map/ppermute | solution.py:19
  63.6 5.4 %collective-permute-start.17 = (f32[80,128]{1,0:T(8,128)S(1)}, f32[80,128]{1,0:T(8,128)S(1)}, u32[]{:S(2)}, u32[]{:S(2)}) collective-permute-start(f32[80,128]{1,0:T(8,128)S(1)} %get-tuple-element.22.refs_0_), channel_id=1, source_target_pairs={{0,16},{8,24},{16,0},{24,8},{1,17},{9,25},{17,1},{25,9},{2,18},{10... | collective-permute-start | bytes 122888 | tf_op jit(solution)/shard_map/ppermute | solution.py:19
  65.7 4.9 %collective-permute-start.18 = (f32[80,128]{1,0:T(8,128)S(1)}, f32[80,128]{1,0:T(8,128)S(1)}, u32[]{:S(2)}, u32[]{:S(2)}) collective-permute-start(f32[80,128]{1,0:T(8,128)S(1)} %collective-permute-done.16.refs_1_), channel_id=1, source_target_pairs={{0,16},{8,24},{16,0},{24,8},{1,17},{9,25},{17,1},{25,9},{2,18},{10... | collective-permute-start | bytes 122888 | tf_op jit(solution)/shard_map/ppermute | solution.py:19
  70.7 17.3 %collective-permute-start.24 = (f32[128,128]{1,0:T(8,128)S(1)}, f32[128,128]{1,0:T(8,128)S(1)}, u32[]{:S(2)}, u32[]{:S(2)}) collective-permute-start(f32[128,128]{1,0:T(8,128)S(1)} %pad_maximum_fusion), channel_id=1, source_target_pairs={{0,16},{8,24},{16,0},{24,8},{1,17},{9,25},{17,1},{25,9},{2,18},{10... | collective-permute-start | bytes 196616 | tf_op jit(solution)/shard_map/ppermute | solution.py:19
  72.6 4.1 %collective-permute-start.20 = (f32[80,128]{1,0:T(8,128)S(1)}, f32[80,128]{1,0:T(8,128)S(1)}, u32[]{:S(2)}, u32[]{:S(2)}) collective-permute-start(f32[80,128]{1,0:T(8,128)S(1)} %add.25.refs_5_), channel_id=1, source_target_pairs={{0,2},{1,3},{2,0},{3,1},{4,6},{5,7},{6,4},{7,5},{8,10},{9,11},{10,... | collective-permute-start | bytes 122888 | tf_op jit(solution)/shard_map/ppermute | solution.py:19
  73.2 4.0 %collective-permute-start.21 = (f32[80,128]{1,0:T(8,128)S(1)}, f32[80,128]{1,0:T(8,128)S(1)}, u32[]{:S(2)}, u32[]{:S(2)}) collective-permute-start(f32[80,128]{1,0:T(8,128)S(1)} %add.25.refs_5_), channel_id=1, source_target_pairs={{0,4},{1,5},{2,6},{3,7},{4,0},{5,1},{6,2},{7,3},{8,12},{9,13},{10,... | collective-permute-start | bytes 122888 | tf_op jit(solution)/shard_map/ppermute | solution.py:19
  74.8 4.9 %collective-permute-start.22 = (f32[80,128]{1,0:T(8,128)S(1)}, f32[80,128]{1,0:T(8,128)S(1)}, u32[]{:S(2)}, u32[]{:S(2)}) collective-permute-start(f32[80,128]{1,0:T(8,128)S(1)} %add.25.refs_5_), channel_id=1, source_target_pairs={{0,6},{1,7},{2,4},{3,5},{4,2},{5,3},{6,0},{7,1},{8,14},{9,15},{10,... | collective-permute-start | bytes 122888 | tf_op jit(solution)/shard_map/ppermute | solution.py:19
  (3 other events, 3.4 us)

commit v6 on v4

--- a/solution.py
+++ b/solution.py
@@ -29,6 +29,10 @@
     return lax.dot_general(
         x, y, (dims, ((), ())), precision=lax.Precision.HIGHEST, preferred_element_type=f32
     )
+
+
+def in_hbm(x):
+    return pltpu.with_memory_space_constraint(x, pltpu.HBM)
 
 
 def table_kernel(order, unit, n_local, cols_ref, ranks_ref, v_ref, slot_ref, held_ref, sem):
@@ -83,24 +87,16 @@
         in_specs=[VM, VM, pl.BlockSpec(memory_space=pltpu.HBM)],
         out_specs=(VM, VM),
         scratch_shapes=[pltpu.SemaphoreType.DMA],
-        compiler_params=pltpu.CompilerParams(vmem_limit_bytes=38 << 20),
+        compiler_params=pltpu.CompilerParams(vmem_limit_bytes=4 << 20),
         cost_estimate=pl.CostEstimate(flops=0, bytes_accessed=24 << 20, transcendentals=0),
         name="slots",
-    )(cols, ranks, v)
-
-
-def coeff_kernel(most, start, unit, n_pieces, part, parts, *refs):
+    )(cols, ranks, in_hbm(v))
+
+
+def coeff_kernel(most, start, unit, n_pieces, *refs):
     slot_ref, v_ref = refs[:2]
     pieces = refs[2 : 2 + n_pieces]
-    if part is None:
-        c_ref, w_ref = refs[-2:]
-    else:
-        u_ref = refs[2 + n_pieces]
-        c_ref, held_ref, w_ref, sem = refs[-4:]
-        length = u_ref.shape[0] // parts
-        stretch = pl.ds(part * length, length)
-        copy = pltpu.make_async_copy(u_ref.at[stretch], held_ref.at[stretch], sem)
-        copy.start()
+    c_ref, w_ref = refs[-2:]
     p = pieces[0].shape[2]
     n_all, k, _ = v_ref.shape
     at = 0
@@ -131,44 +127,26 @@
         return 0
 
     lax.fori_loop(0, at, body, 0, unroll=4)
-    if part is not None:
-        copy.wait()
-
-
-def coefficients(slots, v, pieces, start, most, unit, before, u=None, held_u=None, part=None, parts=1):
+
+
+def coefficients(slots, v, pieces, start, most, unit, before, ahead):
     n_all, k, rows = v.shape
     p = pieces[0].shape[2]
     held = sum(piece.shape[0] for piece in pieces)
-    args = [slots, v, *pieces]
-    specs = [SM] + [VM] * (1 + len(pieces))
-    shapes = [jax.ShapeDtypeStruct((n_all + 1, k, p), f32)]
-    scratch = [pltpu.VMEM((held, rows, 2 * p), bf16)]
-    copying = part is not None
-    if copying:
-        args.append(u)
-        specs.append(pl.BlockSpec(memory_space=pltpu.HBM))
-        shapes.append(jax.ShapeDtypeStruct(u.shape, f32))
-        scratch.append(pltpu.SemaphoreType.DMA)
-    aliases = {}
-    for output, value in enumerate((before, held_u)):
-        if value is not None:
-            aliases[len(args)] = output
-            args.append(value)
-            specs.append(VM)
-    out = pl.pallas_call(
-        functools.partial(coeff_kernel, most, start, unit, len(pieces), part, parts),
-        out_shape=tuple(shapes),
-        in_specs=specs,
-        out_specs=(VM,) * len(shapes),
-        scratch_shapes=scratch,
-        input_output_aliases=aliases,
-        compiler_params=pltpu.CompilerParams(vmem_limit_bytes=(20 if copying else 12) << 20),
+    args = [slots, v, *pieces] + [value for value in (ahead, before) if value is not None]
+    return pl.pallas_call(
+        functools.partial(coeff_kernel, most, start, unit, len(pieces)),
+        out_shape=jax.ShapeDtypeStruct((n_all + 1, k, p), f32),
+        in_specs=[SM] + [VM] * (len(args) - 1),
+        out_specs=VM,
+        scratch_shapes=[pltpu.VMEM((held, rows, 2 * p), bf16)],
+        input_output_aliases={} if before is None else {len(args) - 1: 0},
+        compiler_params=pltpu.CompilerParams(vmem_limit_bytes=12 << 20),
         cost_estimate=pl.CostEstimate(
             flops=0, bytes_accessed=held * 192 << 10, transcendentals=0
         ),
         name="coeff",
     )(*args)
-    return out if copying else (out[0], None)
 
 
 def sketch_kernel(m, n_blocks, c_ref, u_ref, o_ref):
@@ -465,18 +443,15 @@
     unit = 2 * width
     columns = jnp.swapaxes(columns[0], 1, 2)
     slots, v = slot_table(tuple(order), columns, ranks[0], v, depth, unit, n_local)
-    coeff = held_u = None
+    coeff = None
     start = 0
     for index, pieces in enumerate(groups):
-        if index < 2:
-            copied = (u, held_u, index, 2)
-            coeff, held_u = coefficients(slots, v, pieces, start, most, unit, coeff, *copied)
-        else:
-            coeff, _ = coefficients(slots, v, pieces, start, most, unit, coeff)
+        ahead = u if index == len(groups) - 4 else None
+        coeff = coefficients(slots, v, pieces, start, most, unit, coeff, ahead)
         start += sum(piece.shape[0] for piece in pieces)
     made = {}
     for m in (3, 2, 1, 0):
-        made[m] = sketch(coeff, held_u, m, n_blocks)
+        made[m] = sketch(coeff, u, m, n_blocks)
     across = swapped(made[3], "grp", 1)
     across = swapped(made[2] + across, "grp", 2)
     beside = swapped(made[1], "grp", 1)

time: 87.5 us -> 85.4 us (0.976)
  Pallas kernels: 28.9 us -> 26.9 us
    pallas_call x6, Pallas kernels: 11.6 us -> 9.58 us  [coefficients(): pl.pallas_call(functools.partial(coeff_kernel, most, start, unit, len(pie...]
  transfers between devices with their start and end apart: 25 -> 25, of which waited for: 12 -> 12; matrix products, arithmetic and copies ran while one was open for 1% -> 1% of each run, Pallas kernels for 29% -> 27%
where the time goes in v6:
time: 85.4 us; the launch traced here: 85.2 us
  waiting for transfers between devices  31.2 us (37%)
  Pallas kernels  26.9 us (31%)
  starting transfers between devices  23.8 us (28%)
  local copies, waits for them, and re-layouts  2.45 us (3%)
  between operations  0.88 us (1%)
    ppermute x25, waiting for transfers between devices, swapped(): return lax.ppermute(value, axis, pairs)  31.2 us
    ppermute x25, starting transfers between devices, swapped(): return lax.ppermute(value, axis, pairs)  23.8 us
    pallas_call x6, Pallas kernels, coefficients(): pl.pallas_call(functools.partial(coeff_kernel, most, start, unit, len(pie...  9.58 us
    pallas_call x1, Pallas kernels, tree(): pl.pallas_call(functools.partial(tree_kernel, panel, group, n_leaf, len(l...  8.33 us
    pallas_call x1, Pallas kernels, slot_table(): pl.pallas_call(functools.partial(table_kernel, order, unit, n_local), out...  3.99 us
    pallas_call x4, Pallas kernels, sketch(): pl.pallas_call(functools.partial(sketch_kernel, m, n_blocks), out_shape=j...  3.59 us
  transfers between devices with their start and end apart: 25, of which 12 were waited for; matrix products, arithmetic and copies ran while one was open for 1% of the time, Pallas kernels for 27%

profile of v6, /device:TPU:0, one launch (start us, length us, event | category | flops | bytes accessed | tf_op | source)
XLA Modules:
  0.0 85.2 jit_solution(5147214840367818546)
XLA Ops:
  2.3 2.6 %collective-permute-start = (f32[2,256,128]{2,1,0:T(8,128)S(1)}, f32[2,256,128]{2,1,0:T(8,128)S(1)}, u32[]{:S(2)}, u32[]{:S(2)}) collective-permute-start(f32[2,256,128]{2,1,0:T(8,128)S(1)} %get-tuple-element.19.refs_2_), channel_id=1, source_target_pairs={{0,2},{1,3},{2,0},{3,1},{4,6},{5,7},{6,4},{7,5},{8,10},{9,11},{10,... | collective-permute-start | bytes 786440 | tf_op jit(solution)/shard_map/ppermute | solution.py:19
  4.8 1.5 %collective-permute-start.3 = (f32[2,256,128]{2,1,0:T(8,128)S(1)}, f32[2,256,128]{2,1,0:T(8,128)S(1)}, u32[]{:S(2)}, u32[]{:S(2)}) collective-permute-start(f32[2,256,128]{2,1,0:T(8,128)S(1)} %get-tuple-element.18.refs_3_), channel_id=1, source_target_pairs={{0,4},{1,5},{2,6},{3,7},{4,0},{5,1},{6,2},{7,3},{8,12},{9,13},{10,... | collective-permute-start | bytes 786440 | tf_op jit(solution)/shard_map/ppermute | solution.py:19
  6.9 5.1 %collective-permute-done.refs_2_ = f32[2,256,128]{2,1,0:T(8,128)S(1)} collective-permute-done((f32[2,256,128]{2,1,0:T(8,128)S(1)}, f32[2,256,128]{2,1,0:T(8,128)S(1)}, u32[]{:S(2)}, u32[]{:S(2)}) %collective-permute-start) | collective-permute-done | bytes 262176 | tf_op jit(solution)/shard_map/ppermute | solution.py:19
  12.0 2.0 %collective-permute-done.3.refs_3_ = f32[2,256,128]{2,1,0:T(8,128)S(1)} collective-permute-done((f32[2,256,128]{2,1,0:T(8,128)S(1)}, f32[2,256,128]{2,1,0:T(8,128)S(1)}, u32[]{:S(2)}, u32[]{:S(2)}) %collective-permute-start.3) | collective-permute-done | bytes 262176 | tf_op jit(solution)/shard_map/ppermute | solution.py:19
  14.0 1.5 %collective-permute-start.1 = (f32[2,256,128]{2,1,0:T(8,128)S(1)}, f32[2,256,128]{2,1,0:T(8,128)S(1)}, u32[]{:S(2)}, u32[]{:S(2)}) collective-permute-start(f32[2,256,128]{2,1,0:T(8,128)S(1)} %collective-permute-done.refs_2_), channel_id=1, source_target_pairs={{0,4},{1,5},{2,6},{3,7},{4,0},{5,1},{6,2},{7,3},{8,12},{9,13},{10,... | collective-permute-start | bytes 786440 | tf_op jit(solution)/shard_map/ppermute | solution.py:19
  15.5 4.1 %collective-permute-done.6.refs_2_ = f32[2,256,128]{2,1,0:T(8,128)S(1)} collective-permute-done((f32[2,256,128]{2,1,0:T(8,128)S(1)}, f32[2,256,128]{2,1,0:T(8,128)S(1)}, u32[]{:S(2)}, u32[]{:S(2)}) %collective-permute-start.6) | collective-permute-done | bytes 262176 | tf_op jit(solution)/shard_map/ppermute | solution.py:19
  20.3 4.2 %collective-permute-done.1.refs_2_ = f32[2,256,128]{2,1,0:T(8,128)S(1)} collective-permute-done((f32[2,256,128]{2,1,0:T(8,128)S(1)}, f32[2,256,128]{2,1,0:T(8,128)S(1)}, u32[]{:S(2)}, u32[]{:S(2)}) %collective-permute-start.1) | collective-permute-done | bytes 262176 | tf_op jit(solution)/shard_map/ppermute | solution.py:19
  24.5 1.9 %collective-permute-done.4.refs_3_ = f32[2,256,128]{2,1,0:T(8,128)S(1)} collective-permute-done((f32[2,256,128]{2,1,0:T(8,128)S(1)}, f32[2,256,128]{2,1,0:T(8,128)S(1)}, u32[]{:S(2)}, u32[]{:S(2)}) %collective-permute-start.4) | collective-permute-done | bytes 262176 | tf_op jit(solution)/shard_map/ppermute | solution.py:19
  27.8 4.0 %slots.1 = (s32[16,32]{1,0:T(8,128)S(1)}, f32[320,32,256]{2,1,0:T(8,128)S(1)}) custom-call(s32[4,1,80]{2,1,0:T(1,128)S(1)} %bitcast.24, s32[4,80]{1,0:T(4,128)S(1)} %bitcast.25, f32[320,32,256]{2,1,0:T(8,128)} %bitcast.26), custom_call_target="tpu_custom_call" | custom-call | bytes 25165824 | tf_op jit(solution)/shard_map/slots/pallas_call | solution.py:81
  31.8 2.1 %coeff.6.refs_6_ = f32[321,32,128]{2,1,0:T(8,128)S(1)} custom-call(s32[16,32]{1,0:T(8,128)S(1)} %get-tuple-element.10.refs_0_, f32[320,32,256]{2,1,0:T(8,128)S(1)} %get-tuple-element.11.refs_1_, f32[2,256,128]{2,1,0:T(8,128)S(1)} %get-tuple-element.19.refs_2_, f32[2,256,128]{2,1,0:T(8,128)S(1)} %get-tuple-element.18.refs_3_, ...), custom_call_target="tpu_custom_call" | custom-call | bytes 1572864 | tf_op jit(solution)/shard_map/coeff/pallas_call | solution.py:137
  34.0 2.1 %coeff.7.refs_5_ = f32[321,32,128]{2,1,0:T(8,128)S(1)} custom-call(s32[16,32]{1,0:T(8,128)S(1)} %get-tuple-element.10.refs_0_, f32[320,32,256]{2,1,0:T(8,128)S(1)} %get-tuple-element.11.refs_1_, f32[2,256,128]{2,1,0:T(8,128)S(1)} %collective-permute-done.refs_2_, f32[2,256,128]{2,1,0:T(8,128)S(1)} %collective-permute-done.3.refs_3_, ...), custom_call_target="tpu_custom_call", output_to_operand_aliasing={{}: (6, {})} | custom-call | bytes 1572864 | tf_op jit(solution)/shard_map/coeff/pallas_call | solution.py:137
  42.5 1.6 %collective-permute-start.14 = (f32[128,256]{1,0:T(8,128)S(1)}, f32[128,256]{1,0:T(8,128)S(1)}, u32[]{:S(2)}, u32[]{:S(2)}) collective-permute-start(f32[128,256]{1,0:T(8,128)S(1)} %sketch.7), channel_id=1, source_target_pairs={{0,8},{8,0},{16,24},{24,16},{1,9},{9,1},{17,25},{25,17},{2,10},{10... | collective-permute-start | bytes 393224 | tf_op jit(solution)/shard_map/ppermute | solution.py:19
  46.4 2.5 %collective-permute-done.14 = f32[128,256]{1,0:T(8,128)S(1)} collective-permute-done((f32[128,256]{1,0:T(8,128)S(1)}, f32[128,256]{1,0:T(8,128)S(1)}, u32[]{:S(2)}, u32[]{:S(2)}) %collective-permute-start.14) | collective-permute-done | bytes 131104 | tf_op jit(solution)/shard_map/ppermute | solution.py:19
  48.9 2.7 %collective-permute-start.15 = (f32[128,256]{1,0:T(8,128)S(1)}, f32[128,256]{1,0:T(8,128)S(1)}, u32[]{:S(2)}, u32[]{:S(2)}) collective-permute-start(f32[128,256]{1,0:T(8,128)S(1)} %add.21), channel_id=1, source_target_pairs={{0,16},{8,24},{16,0},{24,8},{1,17},{9,25},{17,1},{25,9},{2,18},{10... | collective-permute-start | bytes 393224 | tf_op jit(solution)/shard_map/ppermute | solution.py:19
  52.5 4.9 %collective-permute-done.15.refs_2_ = f32[128,256]{1,0:T(8,128)S(1)} collective-permute-done((f32[128,256]{1,0:T(8,128)S(1)}, f32[128,256]{1,0:T(8,128)S(1)}, u32[]{:S(2)}, u32[]{:S(2)}) %collective-permute-start.15) | collective-permute-done | bytes 131104 | tf_op jit(solution)/shard_map/ppermute | solution.py:19
  58.4 1.4 %collective-permute-start.23 = (f32[128,128]{1,0:T(8,128)S(1)}, f32[128,128]{1,0:T(8,128)S(1)}, u32[]{:S(2)}, u32[]{:S(2)}) collective-permute-start(f32[128,128]{1,0:T(8,128)S(1)} %get-tuple-element.15), channel_id=1, source_target_pairs={{0,8},{8,0},{16,24},{24,16},{1,9},{9,1},{17,25},{25,17},{2,10},{10... | collective-permute-start | bytes 196616 | tf_op jit(solution)/shard_map/ppermute | solution.py:19
  59.8 2.1 %collective-permute-start.17 = (f32[80,128]{1,0:T(8,128)S(1)}, f32[80,128]{1,0:T(8,128)S(1)}, u32[]{:S(2)}, u32[]{:S(2)}) collective-permute-start(f32[80,128]{1,0:T(8,128)S(1)} %get-tuple-element.12.refs_0_), channel_id=1, source_target_pairs={{0,16},{8,24},{16,0},{24,8},{1,17},{9,25},{17,1},{25,9},{2,18},{10... | collective-permute-start | bytes 122888 | tf_op jit(solution)/shard_map/ppermute | solution.py:19
  61.9 1.9 %collective-permute-start.18 = (f32[80,128]{1,0:T(8,128)S(1)}, f32[80,128]{1,0:T(8,128)S(1)}, u32[]{:S(2)}, u32[]{:S(2)}) collective-permute-start(f32[80,128]{1,0:T(8,128)S(1)} %collective-permute-done.16.refs_1_), channel_id=1, source_target_pairs={{0,16},{8,24},{16,0},{24,8},{1,17},{9,25},{17,1},{25,9},{2,18},{10... | collective-permute-start | bytes 122888 | tf_op jit(solution)/shard_map/ppermute | solution.py:19
  65.2 1.6 %collective-permute-done.18.refs_3_ = f32[80,128]{1,0:T(8,128)S(1)} collective-permute-done((f32[80,128]{1,0:T(8,128)S(1)}, f32[80,128]{1,0:T(8,128)S(1)}, u32[]{:S(2)}, u32[]{:S(2)}) %collective-permute-start.18) | collective-permute-done | bytes 40992 | tf_op jit(solution)/shard_map/ppermute | solution.py:19
  66.9 1.9 %collective-permute-start.24 = (f32[128,128]{1,0:T(8,128)S(1)}, f32[128,128]{1,0:T(8,128)S(1)}, u32[]{:S(2)}, u32[]{:S(2)}) collective-permute-start(f32[128,128]{1,0:T(8,128)S(1)} %pad_maximum_fusion), channel_id=1, source_target_pairs={{0,16},{8,24},{16,0},{24,8},{1,17},{9,25},{17,1},{25,9},{2,18},{10... | collective-permute-start | bytes 196616 | tf_op jit(solution)/shard_map/ppermute | solution.py:19
  69.5 1.5 %collective-permute-start.21 = (f32[80,128]{1,0:T(8,128)S(1)}, f32[80,128]{1,0:T(8,128)S(1)}, u32[]{:S(2)}, u32[]{:S(2)}) collective-permute-start(f32[80,128]{1,0:T(8,128)S(1)} %add.25.refs_5_), channel_id=1, source_target_pairs={{0,4},{1,5},{2,6},{3,7},{4,0},{5,1},{6,2},{7,3},{8,12},{9,13},{10,... | collective-permute-start | bytes 122888 | tf_op jit(solution)/shard_map/ppermute | solution.py:19
  71.0 1.4 %collective-permute-start.22 = (f32[80,128]{1,0:T(8,128)S(1)}, f32[80,128]{1,0:T(8,128)S(1)}, u32[]{:S(2)}, u32[]{:S(2)}) collective-permute-start(f32[80,128]{1,0:T(8,128)S(1)} %add.25.refs_5_), channel_id=1, source_target_pairs={{0,6},{1,7},{2,4},{3,5},{4,2},{5,3},{6,0},{7,1},{8,14},{9,15},{10,... | collective-permute-start | bytes 122888 | tf_op jit(solution)/shard_map/ppermute | solution.py:19
  73.5 2.4 %collective-permute-done.22 = f32[80,128]{1,0:T(8,128)S(1)} collective-permute-done((f32[80,128]{1,0:T(8,128)S(1)}, f32[80,128]{1,0:T(8,128)S(1)}, u32[]{:S(2)}, u32[]{:S(2)}) %collective-permute-start.22) | collective-permute-done | bytes 40992 | tf_op jit(solution)/shard_map/ppermute | solution.py:19
  75.9 8.3 %tree.1 = (bf16[4,256,128]{2,1,0:T(8,128)(2,1)S(1)}, f32[4,256,128]{2,1,0:T(8,128)}) custom-call(f32[80,128]{1,0:T(8,128)S(1)} %get-tuple-element.12.refs_0_, f32[80,128]{1,0:T(8,128)S(1)} %collective-permute-done.16.refs_1_, f32[80,128]{1,0:T(8,128)S(1)} %collective-permute-done.17.refs_2_, f32[80,128]{1,0:T(8,128)S(1)} %collective-permute-done.18.refs_3_, ...), custom_call_target="tpu_custom_call" | custom-call | bytes 25165824 | tf_op jit(solution)/shard_map/tree/pallas_call | solution.py:360
  (59 shorter events, 18.9 us)
Async XLA Ops:
  0.6 19.1 %collective-permute-start.12 = (f32[4,256,128]{2,1,0:T(8,128)}, f32[4,256,128]{2,1,0:T(8,128)S(1)}, u32[]{:S(2)}, u32[]{:S(2)}) collective-permute-start(f32[4,256,128]{2,1,0:T(8,128)} %bitcast.27), channel_id=1, source_target_pairs={{0,1},{1,0},{2,3},{3,2},{4,5},{5,4},{6,7},{7,6},{8,9},{9,8},{10,11... | collective-permute-start | bytes 1572872 | tf_op jit(solution)/shard_map/ppermute | solution.py:19
  2.3 9.7 %collective-permute-start = (f32[2,256,128]{2,1,0:T(8,128)S(1)}, f32[2,256,128]{2,1,0:T(8,128)S(1)}, u32[]{:S(2)}, u32[]{:S(2)}) collective-permute-start(f32[2,256,128]{2,1,0:T(8,128)S(1)} %get-tuple-element.19.refs_2_), channel_id=1, source_target_pairs={{0,2},{1,3},{2,0},{3,1},{4,6},{5,7},{6,4},{7,5},{8,10},{9,11},{10,... | collective-permute-start | bytes 786440 | tf_op jit(solution)/shard_map/ppermute | solution.py:19
  4.8 9.2 %collective-permute-start.3 = (f32[2,256,128]{2,1,0:T(8,128)S(1)}, f32[2,256,128]{2,1,0:T(8,128)S(1)}, u32[]{:S(2)}, u32[]{:S(2)}) collective-permute-start(f32[2,256,128]{2,1,0:T(8,128)S(1)} %get-tuple-element.18.refs_3_), channel_id=1, source_target_pairs={{0,4},{1,5},{2,6},{3,7},{4,0},{5,1},{6,2},{7,3},{8,12},{9,13},{10,... | collective-permute-start | bytes 786440 | tf_op jit(solution)/shard_map/ppermute | solution.py:19
  6.3 13.3 %collective-permute-start.6 = (f32[2,256,128]{2,1,0:T(8,128)S(1)}, f32[2,256,128]{2,1,0:T(8,128)S(1)}, u32[]{:S(2)}, u32[]{:S(2)}) collective-permute-start(f32[2,256,128]{2,1,0:T(8,128)S(1)} %get-tuple-element.19.refs_2_), channel_id=1, source_target_pairs={{0,4},{1,5},{2,6},{3,7},{4,0},{5,1},{6,2},{7,3},{8,12},{9,13},{10,... | collective-permute-start | bytes 786440 | tf_op jit(solution)/shard_map/ppermute | solution.py:19
  6.8 12.9 %collective-permute-start.8 = (f32[2,256,128]{2,1,0:T(8,128)S(1)}, f32[2,256,128]{2,1,0:T(8,128)S(1)}, u32[]{:S(2)}, u32[]{:S(2)}) collective-permute-start(f32[2,256,128]{2,1,0:T(8,128)S(1)} %get-tuple-element.18.refs_3_), channel_id=1, source_target_pairs={{0,2},{1,3},{2,0},{3,1},{4,6},{5,7},{6,4},{7,5},{8,10},{9,11},{10,... | collective-permute-start | bytes 786440 | tf_op jit(solution)/shard_map/ppermute | solution.py:19
  12.0 8.2 %collective-permute-start.10 = (f32[2,256,128]{2,1,0:T(8,128)S(1)}, f32[2,256,128]{2,1,0:T(8,128)S(1)}, u32[]{:S(2)}, u32[]{:S(2)}) collective-permute-start(f32[2,256,128]{2,1,0:T(8,128)S(1)} %collective-permute-done.refs_2_), channel_id=1, source_target_pairs={{0,1},{1,0},{2,3},{3,2},{4,5},{5,4},{6,7},{7,6},{8,9},{9,8},{10,11... | collective-permute-start | bytes 786440 | tf_op jit(solution)/shard_map/ppermute | solution.py:19
  14.0 10.5 %collective-permute-start.1 = (f32[2,256,128]{2,1,0:T(8,128)S(1)}, f32[2,256,128]{2,1,0:T(8,128)S(1)}, u32[]{:S(2)}, u32[]{:S(2)}) collective-permute-start(f32[2,256,128]{2,1,0:T(8,128)S(1)} %collective-permute-done.refs_2_), channel_id=1, source_target_pairs={{0,4},{1,5},{2,6},{3,7},{4,0},{5,1},{6,2},{7,3},{8,12},{9,13},{10,... | collective-permute-start | bytes 786440 | tf_op jit(solution)/shard_map/ppermute | solution.py:19
  19.6 6.8 %collective-permute-start.4 = (f32[2,256,128]{2,1,0:T(8,128)S(1)}, f32[2,256,128]{2,1,0:T(8,128)S(1)}, u32[]{:S(2)}, u32[]{:S(2)}) collective-permute-start(f32[2,256,128]{2,1,0:T(8,128)S(1)} %collective-permute-done.3.refs_3_), channel_id=1, source_target_pairs={{0,2},{1,3},{2,0},{3,1},{4,6},{5,7},{6,4},{7,5},{8,10},{9,11},{10,... | collective-permute-start | bytes 786440 | tf_op jit(solution)/shard_map/ppermute | solution.py:19
  19.7 14.3 %collective-permute-start.11 = (f32[2,256,128]{2,1,0:T(8,128)S(1)}, f32[2,256,128]{2,1,0:T(8,128)S(1)}, u32[]{:S(2)}, u32[]{:S(2)}) collective-permute-start(f32[2,256,128]{2,1,0:T(8,128)S(1)} %collective-permute-done.3.refs_3_), channel_id=1, source_target_pairs={{0,1},{1,0},{2,3},{3,2},{4,5},{5,4},{6,7},{7,6},{8,9},{9,8},{10,11... | collective-permute-start | bytes 786440 | tf_op jit(solution)/shard_map/ppermute | solution.py:19
  19.7 17.8 %collective-permute-start.7 = (f32[2,256,128]{2,1,0:T(8,128)S(1)}, f32[2,256,128]{2,1,0:T(8,128)S(1)}, u32[]{:S(2)}, u32[]{:S(2)}) collective-permute-start(f32[2,256,128]{2,1,0:T(8,128)S(1)} %collective-permute-done.6.refs_2_), channel_id=1, source_target_pairs={{0,1},{1,0},{2,3},{3,2},{4,5},{5,4},{6,7},{7,6},{8,9},{9,8},{10,11... | collective-permute-start | bytes 786440 | tf_op jit(solution)/shard_map/ppermute | solution.py:19
  20.2 17.3 %collective-permute-start.9 = (f32[2,256,128]{2,1,0:T(8,128)S(1)}, f32[2,256,128]{2,1,0:T(8,128)S(1)}, u32[]{:S(2)}, u32[]{:S(2)}) collective-permute-start(f32[2,256,128]{2,1,0:T(8,128)S(1)} %collective-permute-done.8.refs_3_), channel_id=1, source_target_pairs={{0,1},{1,0},{2,3},{3,2},{4,5},{5,4},{6,7},{7,6},{8,9},{9,8},{10,11... | collective-permute-start | bytes 786440 | tf_op jit(solution)/shard_map/ppermute | solution.py:19
  24.5 15.7 %collective-permute-start.2 = (f32[2,256,128]{2,1,0:T(8,128)S(1)}, f32[2,256,128]{2,1,0:T(8,128)S(1)}, u32[]{:S(2)}, u32[]{:S(2)}) collective-permute-start(f32[2,256,128]{2,1,0:T(8,128)S(1)} %collective-permute-done.1.refs_2_), channel_id=1, source_target_pairs={{0,1},{1,0},{2,3},{3,2},{4,5},{5,4},{6,7},{7,6},{8,9},{9,8},{10,11... | collective-permute-start | bytes 786440 | tf_op jit(solution)/shard_map/ppermute | solution.py:19
  26.4 13.8 %collective-permute-start.5 = (f32[2,256,128]{2,1,0:T(8,128)S(1)}, f32[2,256,128]{2,1,0:T(8,128)S(1)}, u32[]{:S(2)}, u32[]{:S(2)}) collective-permute-start(f32[2,256,128]{2,1,0:T(8,128)S(1)} %collective-permute-done.4.refs_3_), channel_id=1, source_target_pairs={{0,1},{1,0},{2,3},{3,2},{4,5},{5,4},{6,7},{7,6},{8,9},{9,8},{10,11... | collective-permute-start | bytes 786440 | tf_op jit(solution)/shard_map/ppermute | solution.py:19
  42.5 6.4 %collective-permute-start.14 = (f32[128,256]{1,0:T(8,128)S(1)}, f32[128,256]{1,0:T(8,128)S(1)}, u32[]{:S(2)}, u32[]{:S(2)}) collective-permute-start(f32[128,256]{1,0:T(8,128)S(1)} %sketch.7), channel_id=1, source_target_pairs={{0,8},{8,0},{16,24},{24,16},{1,9},{9,1},{17,25},{25,17},{2,10},{10... | collective-permute-start | bytes 393224 | tf_op jit(solution)/shard_map/ppermute | solution.py:19
  45.0 7.5 %collective-permute-start.13 = (f32[128,256]{1,0:T(8,128)S(1)}, f32[128,256]{1,0:T(8,128)S(1)}, u32[]{:S(2)}, u32[]{:S(2)}) collective-permute-start(f32[128,256]{1,0:T(8,128)S(1)} %sketch.5), channel_id=1, source_target_pairs={{0,8},{8,0},{16,24},{24,16},{1,9},{9,1},{17,25},{25,17},{2,10},{10... | collective-permute-start | bytes 393224 | tf_op jit(solution)/shard_map/ppermute | solution.py:19
  48.9 8.4 %collective-permute-start.15 = (f32[128,256]{1,0:T(8,128)S(1)}, f32[128,256]{1,0:T(8,128)S(1)}, u32[]{:S(2)}, u32[]{:S(2)}) collective-permute-start(f32[128,256]{1,0:T(8,128)S(1)} %add.21), channel_id=1, source_target_pairs={{0,16},{8,24},{16,0},{24,8},{1,17},{9,25},{17,1},{25,9},{2,18},{10... | collective-permute-start | bytes 393224 | tf_op jit(solution)/shard_map/ppermute | solution.py:19
  57.8 4.1 %collective-permute-start.16 = (f32[80,128]{1,0:T(8,128)S(1)}, f32[80,128]{1,0:T(8,128)S(1)}, u32[]{:S(2)}, u32[]{:S(2)}) collective-permute-start(f32[80,128]{1,0:T(8,128)S(1)} %get-tuple-element.12.refs_0_), channel_id=1, source_target_pairs={{0,8},{8,0},{16,24},{24,16},{1,9},{9,1},{17,25},{25,17},{2,10},{10... | collective-permute-start | bytes 122888 | tf_op jit(solution)/shard_map/ppermute | solution.py:19
  58.4 5.4 %collective-permute-start.23 = (f32[128,128]{1,0:T(8,128)S(1)}, f32[128,128]{1,0:T(8,128)S(1)}, u32[]{:S(2)}, u32[]{:S(2)}) collective-permute-start(f32[128,128]{1,0:T(8,128)S(1)} %get-tuple-element.15), channel_id=1, source_target_pairs={{0,8},{8,0},{16,24},{24,16},{1,9},{9,1},{17,25},{25,17},{2,10},{10... | collective-permute-start | bytes 196616 | tf_op jit(solution)/shard_map/ppermute | solution.py:19
  59.8 5.4 %collective-permute-start.17 = (f32[80,128]{1,0:T(8,128)S(1)}, f32[80,128]{1,0:T(8,128)S(1)}, u32[]{:S(2)}, u32[]{:S(2)}) collective-permute-start(f32[80,128]{1,0:T(8,128)S(1)} %get-tuple-element.12.refs_0_), channel_id=1, source_target_pairs={{0,16},{8,24},{16,0},{24,8},{1,17},{9,25},{17,1},{25,9},{2,18},{10... | collective-permute-start | bytes 122888 | tf_op jit(solution)/shard_map/ppermute | solution.py:19
  61.9 4.9 %collective-permute-start.18 = (f32[80,128]{1,0:T(8,128)S(1)}, f32[80,128]{1,0:T(8,128)S(1)}, u32[]{:S(2)}, u32[]{:S(2)}) collective-permute-start(f32[80,128]{1,0:T(8,128)S(1)} %collective-permute-done.16.refs_1_), channel_id=1, source_target_pairs={{0,16},{8,24},{16,0},{24,8},{1,17},{9,25},{17,1},{25,9},{2,18},{10... | collective-permute-start | bytes 122888 | tf_op jit(solution)/shard_map/ppermute | solution.py:19
  66.9 17.3 %collective-permute-start.24 = (f32[128,128]{1,0:T(8,128)S(1)}, f32[128,128]{1,0:T(8,128)S(1)}, u32[]{:S(2)}, u32[]{:S(2)}) collective-permute-start(f32[128,128]{1,0:T(8,128)S(1)} %pad_maximum_fusion), channel_id=1, source_target_pairs={{0,16},{8,24},{16,0},{24,8},{1,17},{9,25},{17,1},{25,9},{2,18},{10... | collective-permute-start | bytes 196616 | tf_op jit(solution)/shard_map/ppermute | solution.py:19
  68.9 4.1 %collective-permute-start.20 = (f32[80,128]{1,0:T(8,128)S(1)}, f32[80,128]{1,0:T(8,128)S(1)}, u32[]{:S(2)}, u32[]{:S(2)}) collective-permute-start(f32[80,128]{1,0:T(8,128)S(1)} %add.25.refs_5_), channel_id=1, source_target_pairs={{0,2},{1,3},{2,0},{3,1},{4,6},{5,7},{6,4},{7,5},{8,10},{9,11},{10,... | collective-permute-start | bytes 122888 | tf_op jit(solution)/shard_map/ppermute | solution.py:19
  69.5 4.0 %collective-permute-start.21 = (f32[80,128]{1,0:T(8,128)S(1)}, f32[80,128]{1,0:T(8,128)S(1)}, u32[]{:S(2)}, u32[]{:S(2)}) collective-permute-start(f32[80,128]{1,0:T(8,128)S(1)} %add.25.refs_5_), channel_id=1, source_target_pairs={{0,4},{1,5},{2,6},{3,7},{4,0},{5,1},{6,2},{7,3},{8,12},{9,13},{10,... | collective-permute-start | bytes 122888 | tf_op jit(solution)/shard_map/ppermute | solution.py:19
  71.0 4.9 %collective-permute-start.22 = (f32[80,128]{1,0:T(8,128)S(1)}, f32[80,128]{1,0:T(8,128)S(1)}, u32[]{:S(2)}, u32[]{:S(2)}) collective-permute-start(f32[80,128]{1,0:T(8,128)S(1)} %add.25.refs_5_), channel_id=1, source_target_pairs={{0,6},{1,7},{2,4},{3,5},{4,2},{5,3},{6,0},{7,1},{8,14},{9,15},{10,... | collective-permute-start | bytes 122888 | tf_op jit(solution)/shard_map/ppermute | solution.py:19
  (6 other events, 14.2 us)

commit v7 on v6

--- a/solution.py
+++ b/solution.py
@@ -119,8 +119,8 @@
             highs.append(high)
             lows.append(low)
         w = w_ref[j]
-        both = jnp.dot(jnp.concatenate(highs, 0), w, preferred_element_type=f32)
-        both = both + jnp.dot(jnp.concatenate(lows, 0), w, preferred_element_type=f32)
+        both = jnp.dot(jnp.concatenate(highs + lows, 0), w, preferred_element_type=f32)
+        both = both[: most * k] + both[most * k :]
         total = both[:, :p] + both[:, p:]
         for n in range(most):
             c_ref[ids[n]] = jnp.where(kept[n], total[n * k : (n + 1) * k], 0.0)
@@ -154,15 +154,16 @@
     k = u_ref.shape[1]
     step = rows // k
     leaf = jnp.bitwise_xor(lax.axis_index("grp"), m)
+    both = jnp.zeros((2 * p, rows), f32)
     total = jnp.zeros((p, rows), f32)
     for q in range(n_blocks // step):
         at = pl.ds(leaf * n_blocks + q * step, step)
         high, low = split(c_ref[at].reshape(rows, p).T)
         u_high, u_low = split(u_ref[at].reshape(rows, rows))
-        total = total + jnp.dot(high, u_high, preferred_element_type=f32)
-        total = total + jnp.dot(low, u_high, preferred_element_type=f32)
+        pair = jnp.concatenate([high, low], axis=0)
+        both = both + jnp.dot(pair, u_high, preferred_element_type=f32)
         total = total + jnp.dot(high, u_low, preferred_element_type=f32)
-    o_ref[...] = total
+    o_ref[...] = total + both[:p] + both[p:]
 
 
 def sketch(coeff, u, m, n_blocks):
@@ -303,8 +304,9 @@
     p = x.shape[1]
     high, low = split(x)
     dims = (((1,), (1,)), ((), ()))
-    both = lax.dot_general(high, solve, dims, preferred_element_type=f32)
-    both = both + lax.dot_general(low, solve, dims, preferred_element_type=f32)
+    both = jnp.concatenate([high, low], axis=0)
+    both = lax.dot_general(both, solve, dims, preferred_element_type=f32)
+    both = both[: x.shape[0]] + both[x.shape[0] :]
     return both[:, :p] + both[:, p:]
 
 

time: 85.4 us -> 85.5 us (level)
  no operation moved by 1% of the time
where the time goes in v7:
time: 85.5 us; the launch traced here: 85.3 us
  waiting for transfers between devices  31.4 us (37%)
  Pallas kernels  26.7 us (31%)
  starting transfers between devices  23.8 us (28%)
  local copies, waits for them, and re-layouts  2.45 us (3%)
  between operations  0.88 us (1%)
    ppermute x25, waiting for transfers between devices, swapped(): return lax.ppermute(value, axis, pairs)  31.4 us
    ppermute x25, starting transfers between devices, swapped(): return lax.ppermute(value, axis, pairs)  23.8 us
    pallas_call x6, Pallas kernels, coefficients(): pl.pallas_call(functools.partial(coeff_kernel, most, start, unit, len(pie...  9.66 us
    pallas_call x1, Pallas kernels, tree(): pl.pallas_call(functools.partial(tree_kernel, panel, group, n_leaf, len(l...  8.43 us
    pallas_call x1, Pallas kernels, slot_table(): pl.pallas_call(functools.partial(table_kernel, order, unit, n_local), out...  3.99 us
    pallas_call x4, Pallas kernels, sketch(): pl.pallas_call(functools.partial(sketch_kernel, m, n_blocks), out_shape=j...  3.3 us
  transfers between devices with their start and end apart: 25, of which 12 were waited for; matrix products, arithmetic and copies ran while one was open for 1% of the time, Pallas kernels for 27%

profile of v7, /device:TPU:0, one launch (start us, length us, event | category | flops | bytes accessed | tf_op | source)
XLA Modules:
  0.0 85.3 jit_solution(9076089987426676708)
XLA Ops:
  2.3 2.6 %collective-permute-start = (f32[2,256,128]{2,1,0:T(8,128)S(1)}, f32[2,256,128]{2,1,0:T(8,128)S(1)}, u32[]{:S(2)}, u32[]{:S(2)}) collective-permute-start(f32[2,256,128]{2,1,0:T(8,128)S(1)} %get-tuple-element.19.refs_2_), channel_id=1, source_target_pairs={{0,2},{1,3},{2,0},{3,1},{4,6},{5,7},{6,4},{7,5},{8,10},{9,11},{10,... | collective-permute-start | bytes 786440 | tf_op jit(solution)/shard_map/ppermute | solution.py:19
  4.8 1.5 %collective-permute-start.3 = (f32[2,256,128]{2,1,0:T(8,128)S(1)}, f32[2,256,128]{2,1,0:T(8,128)S(1)}, u32[]{:S(2)}, u32[]{:S(2)}) collective-permute-start(f32[2,256,128]{2,1,0:T(8,128)S(1)} %get-tuple-element.18.refs_3_), channel_id=1, source_target_pairs={{0,4},{1,5},{2,6},{3,7},{4,0},{5,1},{6,2},{7,3},{8,12},{9,13},{10,... | collective-permute-start | bytes 786440 | tf_op jit(solution)/shard_map/ppermute | solution.py:19
  6.9 5.1 %collective-permute-done.refs_2_ = f32[2,256,128]{2,1,0:T(8,128)S(1)} collective-permute-done((f32[2,256,128]{2,1,0:T(8,128)S(1)}, f32[2,256,128]{2,1,0:T(8,128)S(1)}, u32[]{:S(2)}, u32[]{:S(2)}) %collective-permute-start) | collective-permute-done | bytes 262176 | tf_op jit(solution)/shard_map/ppermute | solution.py:19
  12.0 2.0 %collective-permute-done.3.refs_3_ = f32[2,256,128]{2,1,0:T(8,128)S(1)} collective-permute-done((f32[2,256,128]{2,1,0:T(8,128)S(1)}, f32[2,256,128]{2,1,0:T(8,128)S(1)}, u32[]{:S(2)}, u32[]{:S(2)}) %collective-permute-start.3) | collective-permute-done | bytes 262176 | tf_op jit(solution)/shard_map/ppermute | solution.py:19
  14.0 1.5 %collective-permute-start.1 = (f32[2,256,128]{2,1,0:T(8,128)S(1)}, f32[2,256,128]{2,1,0:T(8,128)S(1)}, u32[]{:S(2)}, u32[]{:S(2)}) collective-permute-start(f32[2,256,128]{2,1,0:T(8,128)S(1)} %collective-permute-done.refs_2_), channel_id=1, source_target_pairs={{0,4},{1,5},{2,6},{3,7},{4,0},{5,1},{6,2},{7,3},{8,12},{9,13},{10,... | collective-permute-start | bytes 786440 | tf_op jit(solution)/shard_map/ppermute | solution.py:19
  15.5 4.1 %collective-permute-done.6.refs_2_ = f32[2,256,128]{2,1,0:T(8,128)S(1)} collective-permute-done((f32[2,256,128]{2,1,0:T(8,128)S(1)}, f32[2,256,128]{2,1,0:T(8,128)S(1)}, u32[]{:S(2)}, u32[]{:S(2)}) %collective-permute-start.6) | collective-permute-done | bytes 262176 | tf_op jit(solution)/shard_map/ppermute | solution.py:19
  20.3 4.2 %collective-permute-done.1.refs_2_ = f32[2,256,128]{2,1,0:T(8,128)S(1)} collective-permute-done((f32[2,256,128]{2,1,0:T(8,128)S(1)}, f32[2,256,128]{2,1,0:T(8,128)S(1)}, u32[]{:S(2)}, u32[]{:S(2)}) %collective-permute-start.1) | collective-permute-done | bytes 262176 | tf_op jit(solution)/shard_map/ppermute | solution.py:19
  24.5 1.9 %collective-permute-done.4.refs_3_ = f32[2,256,128]{2,1,0:T(8,128)S(1)} collective-permute-done((f32[2,256,128]{2,1,0:T(8,128)S(1)}, f32[2,256,128]{2,1,0:T(8,128)S(1)}, u32[]{:S(2)}, u32[]{:S(2)}) %collective-permute-start.4) | collective-permute-done | bytes 262176 | tf_op jit(solution)/shard_map/ppermute | solution.py:19
  27.8 4.0 %slots.1 = (s32[16,32]{1,0:T(8,128)S(1)}, f32[320,32,256]{2,1,0:T(8,128)S(1)}) custom-call(s32[4,1,80]{2,1,0:T(1,128)S(1)} %bitcast.24, s32[4,80]{1,0:T(4,128)S(1)} %bitcast.25, f32[320,32,256]{2,1,0:T(8,128)} %bitcast.26), custom_call_target="tpu_custom_call" | custom-call | bytes 25165824 | tf_op jit(solution)/shard_map/slots/pallas_call | solution.py:81
  31.8 2.1 %coeff.6.refs_6_ = f32[321,32,128]{2,1,0:T(8,128)S(1)} custom-call(s32[16,32]{1,0:T(8,128)S(1)} %get-tuple-element.10.refs_0_, f32[320,32,256]{2,1,0:T(8,128)S(1)} %get-tuple-element.11.refs_1_, f32[2,256,128]{2,1,0:T(8,128)S(1)} %get-tuple-element.19.refs_2_, f32[2,256,128]{2,1,0:T(8,128)S(1)} %get-tuple-element.18.refs_3_, ...), custom_call_target="tpu_custom_call" | custom-call | bytes 1572864 | tf_op jit(solution)/shard_map/coeff/pallas_call | solution.py:137
  34.0 2.1 %coeff.7.refs_5_ = f32[321,32,128]{2,1,0:T(8,128)S(1)} custom-call(s32[16,32]{1,0:T(8,128)S(1)} %get-tuple-element.10.refs_0_, f32[320,32,256]{2,1,0:T(8,128)S(1)} %get-tuple-element.11.refs_1_, f32[2,256,128]{2,1,0:T(8,128)S(1)} %collective-permute-done.refs_2_, f32[2,256,128]{2,1,0:T(8,128)S(1)} %collective-permute-done.3.refs_3_, ...), custom_call_target="tpu_custom_call", output_to_operand_aliasing={{}: (6, {})} | custom-call | bytes 1572864 | tf_op jit(solution)/shard_map/coeff/pallas_call | solution.py:137
  42.5 1.6 %collective-permute-start.14 = (f32[128,256]{1,0:T(8,128)S(1)}, f32[128,256]{1,0:T(8,128)S(1)}, u32[]{:S(2)}, u32[]{:S(2)}) collective-permute-start(f32[128,256]{1,0:T(8,128)S(1)} %sketch.7), channel_id=1, source_target_pairs={{0,8},{8,0},{16,24},{24,16},{1,9},{9,1},{17,25},{25,17},{2,10},{10... | collective-permute-start | bytes 393224 | tf_op jit(solution)/shard_map/ppermute | solution.py:19
  46.3 2.6 %collective-permute-done.14 = f32[128,256]{1,0:T(8,128)S(1)} collective-permute-done((f32[128,256]{1,0:T(8,128)S(1)}, f32[128,256]{1,0:T(8,128)S(1)}, u32[]{:S(2)}, u32[]{:S(2)}) %collective-permute-start.14) | collective-permute-done | bytes 131104 | tf_op jit(solution)/shard_map/ppermute | solution.py:19
  48.9 2.7 %collective-permute-start.15 = (f32[128,256]{1,0:T(8,128)S(1)}, f32[128,256]{1,0:T(8,128)S(1)}, u32[]{:S(2)}, u32[]{:S(2)}) collective-permute-start(f32[128,256]{1,0:T(8,128)S(1)} %add.21), channel_id=1, source_target_pairs={{0,16},{8,24},{16,0},{24,8},{1,17},{9,25},{17,1},{25,9},{2,18},{10... | collective-permute-start | bytes 393224 | tf_op jit(solution)/shard_map/ppermute | solution.py:19
  52.4 4.9 %collective-permute-done.15.refs_2_ = f32[128,256]{1,0:T(8,128)S(1)} collective-permute-done((f32[128,256]{1,0:T(8,128)S(1)}, f32[128,256]{1,0:T(8,128)S(1)}, u32[]{:S(2)}, u32[]{:S(2)}) %collective-permute-start.15) | collective-permute-done | bytes 131104 | tf_op jit(solution)/shard_map/ppermute | solution.py:19
  58.4 1.4 %collective-permute-start.23 = (f32[128,128]{1,0:T(8,128)S(1)}, f32[128,128]{1,0:T(8,128)S(1)}, u32[]{:S(2)}, u32[]{:S(2)}) collective-permute-start(f32[128,128]{1,0:T(8,128)S(1)} %get-tuple-element.15), channel_id=1, source_target_pairs={{0,8},{8,0},{16,24},{24,16},{1,9},{9,1},{17,25},{25,17},{2,10},{10... | collective-permute-start | bytes 196616 | tf_op jit(solution)/shard_map/ppermute | solution.py:19
  59.9 2.0 %collective-permute-start.17 = (f32[80,128]{1,0:T(8,128)S(1)}, f32[80,128]{1,0:T(8,128)S(1)}, u32[]{:S(2)}, u32[]{:S(2)}) collective-permute-start(f32[80,128]{1,0:T(8,128)S(1)} %get-tuple-element.12.refs_0_), channel_id=1, source_target_pairs={{0,16},{8,24},{16,0},{24,8},{1,17},{9,25},{17,1},{25,9},{2,18},{10... | collective-permute-start | bytes 122888 | tf_op jit(solution)/shard_map/ppermute | solution.py:19
  61.9 1.9 %collective-permute-start.18 = (f32[80,128]{1,0:T(8,128)S(1)}, f32[80,128]{1,0:T(8,128)S(1)}, u32[]{:S(2)}, u32[]{:S(2)}) collective-permute-start(f32[80,128]{1,0:T(8,128)S(1)} %collective-permute-done.16.refs_1_), channel_id=1, source_target_pairs={{0,16},{8,24},{16,0},{24,8},{1,17},{9,25},{17,1},{25,9},{2,18},{10... | collective-permute-start | bytes 122888 | tf_op jit(solution)/shard_map/ppermute | solution.py:19
  65.2 1.6 %collective-permute-done.18.refs_3_ = f32[80,128]{1,0:T(8,128)S(1)} collective-permute-done((f32[80,128]{1,0:T(8,128)S(1)}, f32[80,128]{1,0:T(8,128)S(1)}, u32[]{:S(2)}, u32[]{:S(2)}) %collective-permute-start.18) | collective-permute-done | bytes 40992 | tf_op jit(solution)/shard_map/ppermute | solution.py:19
  67.0 1.9 %collective-permute-start.24 = (f32[128,128]{1,0:T(8,128)S(1)}, f32[128,128]{1,0:T(8,128)S(1)}, u32[]{:S(2)}, u32[]{:S(2)}) collective-permute-start(f32[128,128]{1,0:T(8,128)S(1)} %pad_maximum_fusion), channel_id=1, source_target_pairs={{0,16},{8,24},{16,0},{24,8},{1,17},{9,25},{17,1},{25,9},{2,18},{10... | collective-permute-start | bytes 196616 | tf_op jit(solution)/shard_map/ppermute | solution.py:19
  69.5 1.5 %collective-permute-start.21 = (f32[80,128]{1,0:T(8,128)S(1)}, f32[80,128]{1,0:T(8,128)S(1)}, u32[]{:S(2)}, u32[]{:S(2)}) collective-permute-start(f32[80,128]{1,0:T(8,128)S(1)} %add.25.refs_5_), channel_id=1, source_target_pairs={{0,4},{1,5},{2,6},{3,7},{4,0},{5,1},{6,2},{7,3},{8,12},{9,13},{10,... | collective-permute-start | bytes 122888 | tf_op jit(solution)/shard_map/ppermute | solution.py:19
  71.0 1.4 %collective-permute-start.22 = (f32[80,128]{1,0:T(8,128)S(1)}, f32[80,128]{1,0:T(8,128)S(1)}, u32[]{:S(2)}, u32[]{:S(2)}) collective-permute-start(f32[80,128]{1,0:T(8,128)S(1)} %add.25.refs_5_), channel_id=1, source_target_pairs={{0,6},{1,7},{2,4},{3,5},{4,2},{5,3},{6,0},{7,1},{8,14},{9,15},{10,... | collective-permute-start | bytes 122888 | tf_op jit(solution)/shard_map/ppermute | solution.py:19
  73.5 2.4 %collective-permute-done.22 = f32[80,128]{1,0:T(8,128)S(1)} collective-permute-done((f32[80,128]{1,0:T(8,128)S(1)}, f32[80,128]{1,0:T(8,128)S(1)}, u32[]{:S(2)}, u32[]{:S(2)}) %collective-permute-start.22) | collective-permute-done | bytes 40992 | tf_op jit(solution)/shard_map/ppermute | solution.py:19
  75.9 8.4 %tree.1 = (bf16[4,256,128]{2,1,0:T(8,128)(2,1)S(1)}, f32[4,256,128]{2,1,0:T(8,128)}) custom-call(f32[80,128]{1,0:T(8,128)S(1)} %get-tuple-element.12.refs_0_, f32[80,128]{1,0:T(8,128)S(1)} %collective-permute-done.16.refs_1_, f32[80,128]{1,0:T(8,128)S(1)} %collective-permute-done.17.refs_2_, f32[80,128]{1,0:T(8,128)S(1)} %collective-permute-done.18.refs_3_, ...), custom_call_target="tpu_custom_call" | custom-call | bytes 25165824 | tf_op jit(solution)/shard_map/tree/pallas_call | solution.py:362
  (59 shorter events, 18.6 us)
Async XLA Ops:
  0.6 19.1 %collective-permute-start.12 = (f32[4,256,128]{2,1,0:T(8,128)}, f32[4,256,128]{2,1,0:T(8,128)S(1)}, u32[]{:S(2)}, u32[]{:S(2)}) collective-permute-start(f32[4,256,128]{2,1,0:T(8,128)} %bitcast.27), channel_id=1, source_target_pairs={{0,1},{1,0},{2,3},{3,2},{4,5},{5,4},{6,7},{7,6},{8,9},{9,8},{10,11... | collective-permute-start | bytes 1572872 | tf_op jit(solution)/shard_map/ppermute | solution.py:19
  2.3 9.7 %collective-permute-start = (f32[2,256,128]{2,1,0:T(8,128)S(1)}, f32[2,256,128]{2,1,0:T(8,128)S(1)}, u32[]{:S(2)}, u32[]{:S(2)}) collective-permute-start(f32[2,256,128]{2,1,0:T(8,128)S(1)} %get-tuple-element.19.refs_2_), channel_id=1, source_target_pairs={{0,2},{1,3},{2,0},{3,1},{4,6},{5,7},{6,4},{7,5},{8,10},{9,11},{10,... | collective-permute-start | bytes 786440 | tf_op jit(solution)/shard_map/ppermute | solution.py:19
  4.8 9.2 %collective-permute-start.3 = (f32[2,256,128]{2,1,0:T(8,128)S(1)}, f32[2,256,128]{2,1,0:T(8,128)S(1)}, u32[]{:S(2)}, u32[]{:S(2)}) collective-permute-start(f32[2,256,128]{2,1,0:T(8,128)S(1)} %get-tuple-element.18.refs_3_), channel_id=1, source_target_pairs={{0,4},{1,5},{2,6},{3,7},{4,0},{5,1},{6,2},{7,3},{8,12},{9,13},{10,... | collective-permute-start | bytes 786440 | tf_op jit(solution)/shard_map/ppermute | solution.py:19
  6.3 13.3 %collective-permute-start.6 = (f32[2,256,128]{2,1,0:T(8,128)S(1)}, f32[2,256,128]{2,1,0:T(8,128)S(1)}, u32[]{:S(2)}, u32[]{:S(2)}) collective-permute-start(f32[2,256,128]{2,1,0:T(8,128)S(1)} %get-tuple-element.19.refs_2_), channel_id=1, source_target_pairs={{0,4},{1,5},{2,6},{3,7},{4,0},{5,1},{6,2},{7,3},{8,12},{9,13},{10,... | collective-permute-start | bytes 786440 | tf_op jit(solution)/shard_map/ppermute | solution.py:19
  6.8 12.9 %collective-permute-start.8 = (f32[2,256,128]{2,1,0:T(8,128)S(1)}, f32[2,256,128]{2,1,0:T(8,128)S(1)}, u32[]{:S(2)}, u32[]{:S(2)}) collective-permute-start(f32[2,256,128]{2,1,0:T(8,128)S(1)} %get-tuple-element.18.refs_3_), channel_id=1, source_target_pairs={{0,2},{1,3},{2,0},{3,1},{4,6},{5,7},{6,4},{7,5},{8,10},{9,11},{10,... | collective-permute-start | bytes 786440 | tf_op jit(solution)/shard_map/ppermute | solution.py:19
  12.0 8.2 %collective-permute-start.10 = (f32[2,256,128]{2,1,0:T(8,128)S(1)}, f32[2,256,128]{2,1,0:T(8,128)S(1)}, u32[]{:S(2)}, u32[]{:S(2)}) collective-permute-start(f32[2,256,128]{2,1,0:T(8,128)S(1)} %collective-permute-done.refs_2_), channel_id=1, source_target_pairs={{0,1},{1,0},{2,3},{3,2},{4,5},{5,4},{6,7},{7,6},{8,9},{9,8},{10,11... | collective-permute-start | bytes 786440 | tf_op jit(solution)/shard_map/ppermute | solution.py:19
  14.0 10.5 %collective-permute-start.1 = (f32[2,256,128]{2,1,0:T(8,128)S(1)}, f32[2,256,128]{2,1,0:T(8,128)S(1)}, u32[]{:S(2)}, u32[]{:S(2)}) collective-permute-start(f32[2,256,128]{2,1,0:T(8,128)S(1)} %collective-permute-done.refs_2_), channel_id=1, source_target_pairs={{0,4},{1,5},{2,6},{3,7},{4,0},{5,1},{6,2},{7,3},{8,12},{9,13},{10,... | collective-permute-start | bytes 786440 | tf_op jit(solution)/shard_map/ppermute | solution.py:19
  19.6 6.8 %collective-permute-start.4 = (f32[2,256,128]{2,1,0:T(8,128)S(1)}, f32[2,256,128]{2,1,0:T(8,128)S(1)}, u32[]{:S(2)}, u32[]{:S(2)}) collective-permute-start(f32[2,256,128]{2,1,0:T(8,128)S(1)} %collective-permute-done.3.refs_3_), channel_id=1, source_target_pairs={{0,2},{1,3},{2,0},{3,1},{4,6},{5,7},{6,4},{7,5},{8,10},{9,11},{10,... | collective-permute-start | bytes 786440 | tf_op jit(solution)/shard_map/ppermute | solution.py:19
  19.7 14.3 %collective-permute-start.11 = (f32[2,256,128]{2,1,0:T(8,128)S(1)}, f32[2,256,128]{2,1,0:T(8,128)S(1)}, u32[]{:S(2)}, u32[]{:S(2)}) collective-permute-start(f32[2,256,128]{2,1,0:T(8,128)S(1)} %collective-permute-done.3.refs_3_), channel_id=1, source_target_pairs={{0,1},{1,0},{2,3},{3,2},{4,5},{5,4},{6,7},{7,6},{8,9},{9,8},{10,11... | collective-permute-start | bytes 786440 | tf_op jit(solution)/shard_map/ppermute | solution.py:19
  19.7 17.8 %collective-permute-start.7 = (f32[2,256,128]{2,1,0:T(8,128)S(1)}, f32[2,256,128]{2,1,0:T(8,128)S(1)}, u32[]{:S(2)}, u32[]{:S(2)}) collective-permute-start(f32[2,256,128]{2,1,0:T(8,128)S(1)} %collective-permute-done.6.refs_2_), channel_id=1, source_target_pairs={{0,1},{1,0},{2,3},{3,2},{4,5},{5,4},{6,7},{7,6},{8,9},{9,8},{10,11... | collective-permute-start | bytes 786440 | tf_op jit(solution)/shard_map/ppermute | solution.py:19
  20.2 17.3 %collective-permute-start.9 = (f32[2,256,128]{2,1,0:T(8,128)S(1)}, f32[2,256,128]{2,1,0:T(8,128)S(1)}, u32[]{:S(2)}, u32[]{:S(2)}) collective-permute-start(f32[2,256,128]{2,1,0:T(8,128)S(1)} %collective-permute-done.8.refs_3_), channel_id=1, source_target_pairs={{0,1},{1,0},{2,3},{3,2},{4,5},{5,4},{6,7},{7,6},{8,9},{9,8},{10,11... | collective-permute-start | bytes 786440 | tf_op jit(solution)/shard_map/ppermute | solution.py:19
  24.5 15.8 %collective-permute-start.2 = (f32[2,256,128]{2,1,0:T(8,128)S(1)}, f32[2,256,128]{2,1,0:T(8,128)S(1)}, u32[]{:S(2)}, u32[]{:S(2)}) collective-permute-start(f32[2,256,128]{2,1,0:T(8,128)S(1)} %collective-permute-done.1.refs_2_), channel_id=1, source_target_pairs={{0,1},{1,0},{2,3},{3,2},{4,5},{5,4},{6,7},{7,6},{8,9},{9,8},{10,11... | collective-permute-start | bytes 786440 | tf_op jit(solution)/shard_map/ppermute | solution.py:19
  26.4 13.8 %collective-permute-start.5 = (f32[2,256,128]{2,1,0:T(8,128)S(1)}, f32[2,256,128]{2,1,0:T(8,128)S(1)}, u32[]{:S(2)}, u32[]{:S(2)}) collective-permute-start(f32[2,256,128]{2,1,0:T(8,128)S(1)} %collective-permute-done.4.refs_3_), channel_id=1, source_target_pairs={{0,1},{1,0},{2,3},{3,2},{4,5},{5,4},{6,7},{7,6},{8,9},{9,8},{10,11... | collective-permute-start | bytes 786440 | tf_op jit(solution)/shard_map/ppermute | solution.py:19
  42.5 6.4 %collective-permute-start.14 = (f32[128,256]{1,0:T(8,128)S(1)}, f32[128,256]{1,0:T(8,128)S(1)}, u32[]{:S(2)}, u32[]{:S(2)}) collective-permute-start(f32[128,256]{1,0:T(8,128)S(1)} %sketch.7), channel_id=1, source_target_pairs={{0,8},{8,0},{16,24},{24,16},{1,9},{9,1},{17,25},{25,17},{2,10},{10... | collective-permute-start | bytes 393224 | tf_op jit(solution)/shard_map/ppermute | solution.py:19
  44.9 7.5 %collective-permute-start.13 = (f32[128,256]{1,0:T(8,128)S(1)}, f32[128,256]{1,0:T(8,128)S(1)}, u32[]{:S(2)}, u32[]{:S(2)}) collective-permute-start(f32[128,256]{1,0:T(8,128)S(1)} %sketch.5), channel_id=1, source_target_pairs={{0,8},{8,0},{16,24},{24,16},{1,9},{9,1},{17,25},{25,17},{2,10},{10... | collective-permute-start | bytes 393224 | tf_op jit(solution)/shard_map/ppermute | solution.py:19
  48.9 8.4 %collective-permute-start.15 = (f32[128,256]{1,0:T(8,128)S(1)}, f32[128,256]{1,0:T(8,128)S(1)}, u32[]{:S(2)}, u32[]{:S(2)}) collective-permute-start(f32[128,256]{1,0:T(8,128)S(1)} %add.21), channel_id=1, source_target_pairs={{0,16},{8,24},{16,0},{24,8},{1,17},{9,25},{17,1},{25,9},{2,18},{10... | collective-permute-start | bytes 393224 | tf_op jit(solution)/shard_map/ppermute | solution.py:19
  57.8 4.1 %collective-permute-start.16 = (f32[80,128]{1,0:T(8,128)S(1)}, f32[80,128]{1,0:T(8,128)S(1)}, u32[]{:S(2)}, u32[]{:S(2)}) collective-permute-start(f32[80,128]{1,0:T(8,128)S(1)} %get-tuple-element.12.refs_0_), channel_id=1, source_target_pairs={{0,8},{8,0},{16,24},{24,16},{1,9},{9,1},{17,25},{25,17},{2,10},{10... | collective-permute-start | bytes 122888 | tf_op jit(solution)/shard_map/ppermute | solution.py:19
  58.4 5.4 %collective-permute-start.23 = (f32[128,128]{1,0:T(8,128)S(1)}, f32[128,128]{1,0:T(8,128)S(1)}, u32[]{:S(2)}, u32[]{:S(2)}) collective-permute-start(f32[128,128]{1,0:T(8,128)S(1)} %get-tuple-element.15), channel_id=1, source_target_pairs={{0,8},{8,0},{16,24},{24,16},{1,9},{9,1},{17,25},{25,17},{2,10},{10... | collective-permute-start | bytes 196616 | tf_op jit(solution)/shard_map/ppermute | solution.py:19
  59.9 5.3 %collective-permute-start.17 = (f32[80,128]{1,0:T(8,128)S(1)}, f32[80,128]{1,0:T(8,128)S(1)}, u32[]{:S(2)}, u32[]{:S(2)}) collective-permute-start(f32[80,128]{1,0:T(8,128)S(1)} %get-tuple-element.12.refs_0_), channel_id=1, source_target_pairs={{0,16},{8,24},{16,0},{24,8},{1,17},{9,25},{17,1},{25,9},{2,18},{10... | collective-permute-start | bytes 122888 | tf_op jit(solution)/shard_map/ppermute | solution.py:19
  61.9 4.9 %collective-permute-start.18 = (f32[80,128]{1,0:T(8,128)S(1)}, f32[80,128]{1,0:T(8,128)S(1)}, u32[]{:S(2)}, u32[]{:S(2)}) collective-permute-start(f32[80,128]{1,0:T(8,128)S(1)} %collective-permute-done.16.refs_1_), channel_id=1, source_target_pairs={{0,16},{8,24},{16,0},{24,8},{1,17},{9,25},{17,1},{25,9},{2,18},{10... | collective-permute-start | bytes 122888 | tf_op jit(solution)/shard_map/ppermute | solution.py:19
  67.0 17.4 %collective-permute-start.24 = (f32[128,128]{1,0:T(8,128)S(1)}, f32[128,128]{1,0:T(8,128)S(1)}, u32[]{:S(2)}, u32[]{:S(2)}) collective-permute-start(f32[128,128]{1,0:T(8,128)S(1)} %pad_maximum_fusion), channel_id=1, source_target_pairs={{0,16},{8,24},{16,0},{24,8},{1,17},{9,25},{17,1},{25,9},{2,18},{10... | collective-permute-start | bytes 196616 | tf_op jit(solution)/shard_map/ppermute | solution.py:19
  68.9 4.1 %collective-permute-start.20 = (f32[80,128]{1,0:T(8,128)S(1)}, f32[80,128]{1,0:T(8,128)S(1)}, u32[]{:S(2)}, u32[]{:S(2)}) collective-permute-start(f32[80,128]{1,0:T(8,128)S(1)} %add.25.refs_5_), channel_id=1, source_target_pairs={{0,2},{1,3},{2,0},{3,1},{4,6},{5,7},{6,4},{7,5},{8,10},{9,11},{10,... | collective-permute-start | bytes 122888 | tf_op jit(solution)/shard_map/ppermute | solution.py:19
  69.5 4.0 %collective-permute-start.21 = (f32[80,128]{1,0:T(8,128)S(1)}, f32[80,128]{1,0:T(8,128)S(1)}, u32[]{:S(2)}, u32[]{:S(2)}) collective-permute-start(f32[80,128]{1,0:T(8,128)S(1)} %add.25.refs_5_), channel_id=1, source_target_pairs={{0,4},{1,5},{2,6},{3,7},{4,0},{5,1},{6,2},{7,3},{8,12},{9,13},{10,... | collective-permute-start | bytes 122888 | tf_op jit(solution)/shard_map/ppermute | solution.py:19
  71.0 4.9 %collective-permute-start.22 = (f32[80,128]{1,0:T(8,128)S(1)}, f32[80,128]{1,0:T(8,128)S(1)}, u32[]{:S(2)}, u32[]{:S(2)}) collective-permute-start(f32[80,128]{1,0:T(8,128)S(1)} %add.25.refs_5_), channel_id=1, source_target_pairs={{0,6},{1,7},{2,4},{3,5},{4,2},{5,3},{6,0},{7,1},{8,14},{9,15},{10,... | collective-permute-start | bytes 122888 | tf_op jit(solution)/shard_map/ppermute | solution.py:19
  (6 other events, 14.2 us)

commit v8 on v6

--- a/solution.py
+++ b/solution.py
@@ -126,7 +126,7 @@
             c_ref[ids[n]] = jnp.where(kept[n], total[n * k : (n + 1) * k], 0.0)
         return 0
 
-    lax.fori_loop(0, at, body, 0, unroll=4)
+    lax.fori_loop(0, at, body, 0, unroll=8)
 
 
 def coefficients(slots, v, pieces, start, most, unit, before, ahead):
@@ -154,15 +154,16 @@
     k = u_ref.shape[1]
     step = rows // k
     leaf = jnp.bitwise_xor(lax.axis_index("grp"), m)
+    both = jnp.zeros((2 * p, rows), f32)
     total = jnp.zeros((p, rows), f32)
     for q in range(n_blocks // step):
         at = pl.ds(leaf * n_blocks + q * step, step)
         high, low = split(c_ref[at].reshape(rows, p).T)
         u_high, u_low = split(u_ref[at].reshape(rows, rows))
-        total = total + jnp.dot(high, u_high, preferred_element_type=f32)
-        total = total + jnp.dot(low, u_high, preferred_element_type=f32)
+        pair = jnp.concatenate([high, low], axis=0)
+        both = both + jnp.dot(pair, u_high, preferred_element_type=f32)
         total = total + jnp.dot(high, u_low, preferred_element_type=f32)
-    o_ref[...] = total
+    o_ref[...] = total + both[:p] + both[p:]
 
 
 def sketch(coeff, u, m, n_blocks):
@@ -378,7 +379,11 @@
     rows = (own_ref[...], near_ref[:quarter], far_ref[:quarter], far_ref[quarter:])
     for m, value in enumerate(rows):
         leaf = jnp.bitwise_xor(own, m)
-        basis_ref[leaf] = applied(value, solve_ref[leaf])
+        pair = jnp.concatenate(split(value), axis=0)
+        dims = (((1,), (1,)), ((), ()))
+        both = lax.dot_general(pair, solve_ref[leaf], dims, preferred_element_type=f32)
+        both = both[:quarter] + both[quarter:]
+        basis_ref[leaf] = both[:, : value.shape[1]] + both[:, value.shape[1] :]
 
 
 def basis(solves, own, near, far):

time: 85.4 us -> 87.2 us (1.021)
  Pallas kernels: 26.9 us -> 27.9 us
    pallas_call x6, Pallas kernels: 9.58 us -> 11 us  [coefficients(): pl.pallas_call(functools.partial(coeff_kernel, most, start, unit, len(pie...]
  transfers between devices with their start and end apart: 25 -> 25, of which waited for: 12 -> 12; matrix products, arithmetic and copies ran while one was open for 1% -> 1% of each run, Pallas kernels for 27% -> 28%
where the time goes in v8:
time: 87.2 us; the launch traced here: 87 us
  waiting for transfers between devices  31.4 us (36%)
  Pallas kernels  27.9 us (32%)
  starting transfers between devices  23.8 us (27%)
  local copies, waits for them, and re-layouts  2.94 us (3%)
    ppermute x25, waiting for transfers between devices, swapped(): return lax.ppermute(value, axis, pairs)  31.4 us
    ppermute x25, starting transfers between devices, swapped(): return lax.ppermute(value, axis, pairs)  23.8 us
    pallas_call x6, Pallas kernels, coefficients(): pl.pallas_call(functools.partial(coeff_kernel, most, start, unit, len(pie...  11 us
    pallas_call x1, Pallas kernels, tree(): pl.pallas_call(functools.partial(tree_kernel, panel, group, n_leaf, len(l...  8.33 us
    pallas_call x1, Pallas kernels, slot_table(): pl.pallas_call(functools.partial(table_kernel, order, unit, n_local), out...  3.99 us
    pallas_call x4, Pallas kernels, sketch(): pl.pallas_call(functools.partial(sketch_kernel, m, n_blocks), out_shape=j...  3.3 us
    unnamed x10, local copies, waits for them, and re-layouts  1.88 us
  transfers between devices with their start and end apart: 25, of which 12 were waited for; matrix products, arithmetic and copies ran while one was open for 1% of the time, Pallas kernels for 28%

profile of v8, /device:TPU:0, one launch (start us, length us, event | category | flops | bytes accessed | tf_op | source)
XLA Modules:
  0.0 87.0 jit_solution(10085468641573337654)
XLA Ops:
  2.3 2.6 %collective-permute-start = (f32[2,256,128]{2,1,0:T(8,128)S(1)}, f32[2,256,128]{2,1,0:T(8,128)S(1)}, u32[]{:S(2)}, u32[]{:S(2)}) collective-permute-start(f32[2,256,128]{2,1,0:T(8,128)S(1)} %get-tuple-element.19.refs_2_), channel_id=1, source_target_pairs={{0,2},{1,3},{2,0},{3,1},{4,6},{5,7},{6,4},{7,5},{8,10},{9,11},{10,... | collective-permute-start | bytes 786440 | tf_op jit(solution)/shard_map/ppermute | solution.py:19
  4.8 1.5 %collective-permute-start.3 = (f32[2,256,128]{2,1,0:T(8,128)S(1)}, f32[2,256,128]{2,1,0:T(8,128)S(1)}, u32[]{:S(2)}, u32[]{:S(2)}) collective-permute-start(f32[2,256,128]{2,1,0:T(8,128)S(1)} %get-tuple-element.18.refs_3_), channel_id=1, source_target_pairs={{0,4},{1,5},{2,6},{3,7},{4,0},{5,1},{6,2},{7,3},{8,12},{9,13},{10,... | collective-permute-start | bytes 786440 | tf_op jit(solution)/shard_map/ppermute | solution.py:19
  6.9 5.1 %collective-permute-done.refs_2_ = f32[2,256,128]{2,1,0:T(8,128)S(1)} collective-permute-done((f32[2,256,128]{2,1,0:T(8,128)S(1)}, f32[2,256,128]{2,1,0:T(8,128)S(1)}, u32[]{:S(2)}, u32[]{:S(2)}) %collective-permute-start) | collective-permute-done | bytes 262176 | tf_op jit(solution)/shard_map/ppermute | solution.py:19
  12.0 2.0 %collective-permute-done.3.refs_3_ = f32[2,256,128]{2,1,0:T(8,128)S(1)} collective-permute-done((f32[2,256,128]{2,1,0:T(8,128)S(1)}, f32[2,256,128]{2,1,0:T(8,128)S(1)}, u32[]{:S(2)}, u32[]{:S(2)}) %collective-permute-start.3) | collective-permute-done | bytes 262176 | tf_op jit(solution)/shard_map/ppermute | solution.py:19
  15.5 4.1 %collective-permute-done.6.refs_2_ = f32[2,256,128]{2,1,0:T(8,128)S(1)} collective-permute-done((f32[2,256,128]{2,1,0:T(8,128)S(1)}, f32[2,256,128]{2,1,0:T(8,128)S(1)}, u32[]{:S(2)}, u32[]{:S(2)}) %collective-permute-start.6) | collective-permute-done | bytes 262176 | tf_op jit(solution)/shard_map/ppermute | solution.py:19
  20.3 4.2 %collective-permute-done.1.refs_2_ = f32[2,256,128]{2,1,0:T(8,128)S(1)} collective-permute-done((f32[2,256,128]{2,1,0:T(8,128)S(1)}, f32[2,256,128]{2,1,0:T(8,128)S(1)}, u32[]{:S(2)}, u32[]{:S(2)}) %collective-permute-start.1) | collective-permute-done | bytes 262176 | tf_op jit(solution)/shard_map/ppermute | solution.py:19
  24.5 1.9 %collective-permute-done.4.refs_3_ = f32[2,256,128]{2,1,0:T(8,128)S(1)} collective-permute-done((f32[2,256,128]{2,1,0:T(8,128)S(1)}, f32[2,256,128]{2,1,0:T(8,128)S(1)}, u32[]{:S(2)}, u32[]{:S(2)}) %collective-permute-start.4) | collective-permute-done | bytes 262176 | tf_op jit(solution)/shard_map/ppermute | solution.py:19
  27.8 4.0 %slots.1 = (s32[16,32]{1,0:T(8,128)S(1)}, f32[320,32,256]{2,1,0:T(8,128)S(1)}) custom-call(s32[4,1,80]{2,1,0:T(1,128)S(1)} %bitcast.24, s32[4,80]{1,0:T(4,128)S(1)} %bitcast.25, f32[320,32,256]{2,1,0:T(8,128)} %bitcast.26), custom_call_target="tpu_custom_call" | custom-call | bytes 25165824 | tf_op jit(solution)/shard_map/slots/pallas_call | solution.py:81
  31.8 1.9 %coeff.6.refs_6_ = f32[321,32,128]{2,1,0:T(8,128)S(1)} custom-call(s32[16,32]{1,0:T(8,128)S(1)} %get-tuple-element.10.refs_0_, f32[320,32,256]{2,1,0:T(8,128)S(1)} %get-tuple-element.11.refs_1_, f32[2,256,128]{2,1,0:T(8,128)S(1)} %get-tuple-element.19.refs_2_, f32[2,256,128]{2,1,0:T(8,128)S(1)} %get-tuple-element.18.refs_3_, ...), custom_call_target="tpu_custom_call" | custom-call | bytes 1572864 | tf_op jit(solution)/shard_map/coeff/pallas_call | solution.py:137
  33.7 1.8 %coeff.7.refs_5_ = f32[321,32,128]{2,1,0:T(8,128)S(1)} custom-call(s32[16,32]{1,0:T(8,128)S(1)} %get-tuple-element.10.refs_0_, f32[320,32,256]{2,1,0:T(8,128)S(1)} %get-tuple-element.11.refs_1_, f32[2,256,128]{2,1,0:T(8,128)S(1)} %collective-permute-done.refs_2_, f32[2,256,128]{2,1,0:T(8,128)S(1)} %collective-permute-done.3.refs_3_, ...), custom_call_target="tpu_custom_call", output_to_operand_aliasing={{}: (6, {})} | custom-call | bytes 1572864 | tf_op jit(solution)/shard_map/coeff/pallas_call | solution.py:137
  36.1 1.8 %coeff.8.refs_4_ = f32[321,32,128]{2,1,0:T(8,128)S(1)} custom-call(s32[16,32]{1,0:T(8,128)S(1)} %get-tuple-element.10.refs_0_, f32[320,32,256]{2,1,0:T(8,128)S(1)} %get-tuple-element.11.refs_1_, f32[2,256,128]{2,1,0:T(8,128)S(1)} %collective-permute-done.6.refs_2_, ...), custom_call_target="tpu_custom_call", output_to_operand_aliasing={{}: (5, {})} | custom-call | bytes 786432 | tf_op jit(solution)/shard_map/coeff/pallas_call | solution.py:137
  37.9 1.8 %coeff.9.refs_4_ = f32[321,32,128]{2,1,0:T(8,128)S(1)} custom-call(s32[16,32]{1,0:T(8,128)S(1)} %get-tuple-element.10.refs_0_, f32[320,32,256]{2,1,0:T(8,128)S(1)} %get-tuple-element.11.refs_1_, f32[2,256,128]{2,1,0:T(8,128)S(1)} %collective-permute-done.7.refs_2_, ...), custom_call_target="tpu_custom_call", output_to_operand_aliasing={{}: (4, {})} | custom-call | bytes 786432 | tf_op jit(solution)/shard_map/coeff/pallas_call | solution.py:137
  39.8 1.8 %coeff.10.refs_4_ = f32[321,32,128]{2,1,0:T(8,128)S(1)} custom-call(s32[16,32]{1,0:T(8,128)S(1)} %get-tuple-element.10.refs_0_, f32[320,32,256]{2,1,0:T(8,128)S(1)} %get-tuple-element.11.refs_1_, f32[2,256,128]{2,1,0:T(8,128)S(1)} %collective-permute-done.1.refs_2_, ...), custom_call_target="tpu_custom_call", output_to_operand_aliasing={{}: (4, {})} | custom-call | bytes 786432 | tf_op jit(solution)/shard_map/coeff/pallas_call | solution.py:137
  41.6 1.8 %coeff.11.c_ref = f32[321,32,128]{2,1,0:T(8,128)S(1)} custom-call(s32[16,32]{1,0:T(8,128)S(1)} %get-tuple-element.10.refs_0_, f32[320,32,256]{2,1,0:T(8,128)S(1)} %get-tuple-element.11.refs_1_, f32[2,256,128]{2,1,0:T(8,128)S(1)} %collective-permute-done.2.refs_2_, f32[2,256,128]{2,1,0:T(8,128)S(1)} %collective-permute-done.5.refs_3_, ...), custom_call_target="tpu_custom_call", output_to_operand_aliasing={{}: (4, {})} | custom-call | bytes 786432 | tf_op jit(solution)/shard_map/coeff/pallas_call | solution.py:137
  44.3 1.6 %collective-permute-start.14 = (f32[128,256]{1,0:T(8,128)S(1)}, f32[128,256]{1,0:T(8,128)S(1)}, u32[]{:S(2)}, u32[]{:S(2)}) collective-permute-start(f32[128,256]{1,0:T(8,128)S(1)} %sketch.7), channel_id=1, source_target_pairs={{0,8},{8,0},{16,24},{24,16},{1,9},{9,1},{17,25},{25,17},{2,10},{10... | collective-permute-start | bytes 393224 | tf_op jit(solution)/shard_map/ppermute | solution.py:19
  48.1 2.6 %collective-permute-done.14 = f32[128,256]{1,0:T(8,128)S(1)} collective-permute-done((f32[128,256]{1,0:T(8,128)S(1)}, f32[128,256]{1,0:T(8,128)S(1)}, u32[]{:S(2)}, u32[]{:S(2)}) %collective-permute-start.14) | collective-permute-done | bytes 131104 | tf_op jit(solution)/shard_map/ppermute | solution.py:19
  50.7 2.7 %collective-permute-start.15 = (f32[128,256]{1,0:T(8,128)S(1)}, f32[128,256]{1,0:T(8,128)S(1)}, u32[]{:S(2)}, u32[]{:S(2)}) collective-permute-start(f32[128,256]{1,0:T(8,128)S(1)} %add.21), channel_id=1, source_target_pairs={{0,16},{8,24},{16,0},{24,8},{1,17},{9,25},{17,1},{25,9},{2,18},{10... | collective-permute-start | bytes 393224 | tf_op jit(solution)/shard_map/ppermute | solution.py:19
  54.2 4.9 %collective-permute-done.15.refs_2_ = f32[128,256]{1,0:T(8,128)S(1)} collective-permute-done((f32[128,256]{1,0:T(8,128)S(1)}, f32[128,256]{1,0:T(8,128)S(1)}, u32[]{:S(2)}, u32[]{:S(2)}) %collective-permute-start.15) | collective-permute-done | bytes 131104 | tf_op jit(solution)/shard_map/ppermute | solution.py:19
  61.7 2.0 %collective-permute-start.17 = (f32[80,128]{1,0:T(8,128)S(1)}, f32[80,128]{1,0:T(8,128)S(1)}, u32[]{:S(2)}, u32[]{:S(2)}) collective-permute-start(f32[80,128]{1,0:T(8,128)S(1)} %get-tuple-element.12.refs_0_), channel_id=1, source_target_pairs={{0,16},{8,24},{16,0},{24,8},{1,17},{9,25},{17,1},{25,9},{2,18},{10... | collective-permute-start | bytes 122888 | tf_op jit(solution)/shard_map/ppermute | solution.py:19
  63.7 1.9 %collective-permute-start.18 = (f32[80,128]{1,0:T(8,128)S(1)}, f32[80,128]{1,0:T(8,128)S(1)}, u32[]{:S(2)}, u32[]{:S(2)}) collective-permute-start(f32[80,128]{1,0:T(8,128)S(1)} %collective-permute-done.16.refs_1_), channel_id=1, source_target_pairs={{0,16},{8,24},{16,0},{24,8},{1,17},{9,25},{17,1},{25,9},{2,18},{10... | collective-permute-start | bytes 122888 | tf_op jit(solution)/shard_map/ppermute | solution.py:19
  67.0 1.7 %collective-permute-done.18.refs_3_ = f32[80,128]{1,0:T(8,128)S(1)} collective-permute-done((f32[80,128]{1,0:T(8,128)S(1)}, f32[80,128]{1,0:T(8,128)S(1)}, u32[]{:S(2)}, u32[]{:S(2)}) %collective-permute-start.18) | collective-permute-done | bytes 40992 | tf_op jit(solution)/shard_map/ppermute | solution.py:19
  68.8 1.9 %collective-permute-start.24 = (f32[128,128]{1,0:T(8,128)S(1)}, f32[128,128]{1,0:T(8,128)S(1)}, u32[]{:S(2)}, u32[]{:S(2)}) collective-permute-start(f32[128,128]{1,0:T(8,128)S(1)} %pad_maximum_fusion), channel_id=1, source_target_pairs={{0,16},{8,24},{16,0},{24,8},{1,17},{9,25},{17,1},{25,9},{2,18},{10... | collective-permute-start | bytes 196616 | tf_op jit(solution)/shard_map/ppermute | solution.py:19
  75.3 2.4 %collective-permute-done.22 = f32[80,128]{1,0:T(8,128)S(1)} collective-permute-done((f32[80,128]{1,0:T(8,128)S(1)}, f32[80,128]{1,0:T(8,128)S(1)}, u32[]{:S(2)}, u32[]{:S(2)}) %collective-permute-start.22) | collective-permute-done | bytes 40992 | tf_op jit(solution)/shard_map/ppermute | solution.py:19
  77.8 8.3 %tree.1 = (bf16[4,256,128]{2,1,0:T(8,128)(2,1)S(1)}, f32[4,256,128]{2,1,0:T(8,128)}) custom-call(f32[80,128]{1,0:T(8,128)S(1)} %get-tuple-element.12.refs_0_, f32[80,128]{1,0:T(8,128)S(1)} %collective-permute-done.16.refs_1_, f32[80,128]{1,0:T(8,128)S(1)} %collective-permute-done.17.refs_2_, f32[80,128]{1,0:T(8,128)S(1)} %collective-permute-done.18.refs_3_, ...), custom_call_target="tpu_custom_call" | custom-call | bytes 25165824 | tf_op jit(solution)/shard_map/tree/pallas_call | solution.py:361
  (59 shorter events, 19.6 us)
Async XLA Ops:
  0.6 19.1 %collective-permute-start.12 = (f32[4,256,128]{2,1,0:T(8,128)}, f32[4,256,128]{2,1,0:T(8,128)S(1)}, u32[]{:S(2)}, u32[]{:S(2)}) collective-permute-start(f32[4,256,128]{2,1,0:T(8,128)} %bitcast.27), channel_id=1, source_target_pairs={{0,1},{1,0},{2,3},{3,2},{4,5},{5,4},{6,7},{7,6},{8,9},{9,8},{10,11... | collective-permute-start | bytes 1572872 | tf_op jit(solution)/shard_map/ppermute | solution.py:19
  2.3 9.7 %collective-permute-start = (f32[2,256,128]{2,1,0:T(8,128)S(1)}, f32[2,256,128]{2,1,0:T(8,128)S(1)}, u32[]{:S(2)}, u32[]{:S(2)}) collective-permute-start(f32[2,256,128]{2,1,0:T(8,128)S(1)} %get-tuple-element.19.refs_2_), channel_id=1, source_target_pairs={{0,2},{1,3},{2,0},{3,1},{4,6},{5,7},{6,4},{7,5},{8,10},{9,11},{10,... | collective-permute-start | bytes 786440 | tf_op jit(solution)/shard_map/ppermute | solution.py:19
  4.8 9.2 %collective-permute-start.3 = (f32[2,256,128]{2,1,0:T(8,128)S(1)}, f32[2,256,128]{2,1,0:T(8,128)S(1)}, u32[]{:S(2)}, u32[]{:S(2)}) collective-permute-start(f32[2,256,128]{2,1,0:T(8,128)S(1)} %get-tuple-element.18.refs_3_), channel_id=1, source_target_pairs={{0,4},{1,5},{2,6},{3,7},{4,0},{5,1},{6,2},{7,3},{8,12},{9,13},{10,... | collective-permute-start | bytes 786440 | tf_op jit(solution)/shard_map/ppermute | solution.py:19
  6.3 13.3 %collective-permute-start.6 = (f32[2,256,128]{2,1,0:T(8,128)S(1)}, f32[2,256,128]{2,1,0:T(8,128)S(1)}, u32[]{:S(2)}, u32[]{:S(2)}) collective-permute-start(f32[2,256,128]{2,1,0:T(8,128)S(1)} %get-tuple-element.19.refs_2_), channel_id=1, source_target_pairs={{0,4},{1,5},{2,6},{3,7},{4,0},{5,1},{6,2},{7,3},{8,12},{9,13},{10,... | collective-permute-start | bytes 786440 | tf_op jit(solution)/shard_map/ppermute | solution.py:19
  6.8 12.9 %collective-permute-start.8 = (f32[2,256,128]{2,1,0:T(8,128)S(1)}, f32[2,256,128]{2,1,0:T(8,128)S(1)}, u32[]{:S(2)}, u32[]{:S(2)}) collective-permute-start(f32[2,256,128]{2,1,0:T(8,128)S(1)} %get-tuple-element.18.refs_3_), channel_id=1, source_target_pairs={{0,2},{1,3},{2,0},{3,1},{4,6},{5,7},{6,4},{7,5},{8,10},{9,11},{10,... | collective-permute-start | bytes 786440 | tf_op jit(solution)/shard_map/ppermute | solution.py:19
  12.0 8.2 %collective-permute-start.10 = (f32[2,256,128]{2,1,0:T(8,128)S(1)}, f32[2,256,128]{2,1,0:T(8,128)S(1)}, u32[]{:S(2)}, u32[]{:S(2)}) collective-permute-start(f32[2,256,128]{2,1,0:T(8,128)S(1)} %collective-permute-done.refs_2_), channel_id=1, source_target_pairs={{0,1},{1,0},{2,3},{3,2},{4,5},{5,4},{6,7},{7,6},{8,9},{9,8},{10,11... | collective-permute-start | bytes 786440 | tf_op jit(solution)/shard_map/ppermute | solution.py:19
  14.0 10.5 %collective-permute-start.1 = (f32[2,256,128]{2,1,0:T(8,128)S(1)}, f32[2,256,128]{2,1,0:T(8,128)S(1)}, u32[]{:S(2)}, u32[]{:S(2)}) collective-permute-start(f32[2,256,128]{2,1,0:T(8,128)S(1)} %collective-permute-done.refs_2_), channel_id=1, source_target_pairs={{0,4},{1,5},{2,6},{3,7},{4,0},{5,1},{6,2},{7,3},{8,12},{9,13},{10,... | collective-permute-start | bytes 786440 | tf_op jit(solution)/shard_map/ppermute | solution.py:19
  19.6 6.8 %collective-permute-start.4 = (f32[2,256,128]{2,1,0:T(8,128)S(1)}, f32[2,256,128]{2,1,0:T(8,128)S(1)}, u32[]{:S(2)}, u32[]{:S(2)}) collective-permute-start(f32[2,256,128]{2,1,0:T(8,128)S(1)} %collective-permute-done.3.refs_3_), channel_id=1, source_target_pairs={{0,2},{1,3},{2,0},{3,1},{4,6},{5,7},{6,4},{7,5},{8,10},{9,11},{10,... | collective-permute-start | bytes 786440 | tf_op jit(solution)/shard_map/ppermute | solution.py:19
  19.7 14.0 %collective-permute-start.11 = (f32[2,256,128]{2,1,0:T(8,128)S(1)}, f32[2,256,128]{2,1,0:T(8,128)S(1)}, u32[]{:S(2)}, u32[]{:S(2)}) collective-permute-start(f32[2,256,128]{2,1,0:T(8,128)S(1)} %collective-permute-done.3.refs_3_), channel_id=1, source_target_pairs={{0,1},{1,0},{2,3},{3,2},{4,5},{5,4},{6,7},{7,6},{8,9},{9,8},{10,11... | collective-permute-start | bytes 786440 | tf_op jit(solution)/shard_map/ppermute | solution.py:19
  19.7 18.2 %collective-permute-start.7 = (f32[2,256,128]{2,1,0:T(8,128)S(1)}, f32[2,256,128]{2,1,0:T(8,128)S(1)}, u32[]{:S(2)}, u32[]{:S(2)}) collective-permute-start(f32[2,256,128]{2,1,0:T(8,128)S(1)} %collective-permute-done.6.refs_2_), channel_id=1, source_target_pairs={{0,1},{1,0},{2,3},{3,2},{4,5},{5,4},{6,7},{7,6},{8,9},{9,8},{10,11... | collective-permute-start | bytes 786440 | tf_op jit(solution)/shard_map/ppermute | solution.py:19
  20.2 17.7 %collective-permute-start.9 = (f32[2,256,128]{2,1,0:T(8,128)S(1)}, f32[2,256,128]{2,1,0:T(8,128)S(1)}, u32[]{:S(2)}, u32[]{:S(2)}) collective-permute-start(f32[2,256,128]{2,1,0:T(8,128)S(1)} %collective-permute-done.8.refs_3_), channel_id=1, source_target_pairs={{0,1},{1,0},{2,3},{3,2},{4,5},{5,4},{6,7},{7,6},{8,9},{9,8},{10,11... | collective-permute-start | bytes 786440 | tf_op jit(solution)/shard_map/ppermute | solution.py:19
  24.5 17.1 %collective-permute-start.2 = (f32[2,256,128]{2,1,0:T(8,128)S(1)}, f32[2,256,128]{2,1,0:T(8,128)S(1)}, u32[]{:S(2)}, u32[]{:S(2)}) collective-permute-start(f32[2,256,128]{2,1,0:T(8,128)S(1)} %collective-permute-done.1.refs_2_), channel_id=1, source_target_pairs={{0,1},{1,0},{2,3},{3,2},{4,5},{5,4},{6,7},{7,6},{8,9},{9,8},{10,11... | collective-permute-start | bytes 786440 | tf_op jit(solution)/shard_map/ppermute | solution.py:19
  26.4 15.2 %collective-permute-start.5 = (f32[2,256,128]{2,1,0:T(8,128)S(1)}, f32[2,256,128]{2,1,0:T(8,128)S(1)}, u32[]{:S(2)}, u32[]{:S(2)}) collective-permute-start(f32[2,256,128]{2,1,0:T(8,128)S(1)} %collective-permute-done.4.refs_3_), channel_id=1, source_target_pairs={{0,1},{1,0},{2,3},{3,2},{4,5},{5,4},{6,7},{7,6},{8,9},{9,8},{10,11... | collective-permute-start | bytes 786440 | tf_op jit(solution)/shard_map/ppermute | solution.py:19
  44.3 6.4 %collective-permute-start.14 = (f32[128,256]{1,0:T(8,128)S(1)}, f32[128,256]{1,0:T(8,128)S(1)}, u32[]{:S(2)}, u32[]{:S(2)}) collective-permute-start(f32[128,256]{1,0:T(8,128)S(1)} %sketch.7), channel_id=1, source_target_pairs={{0,8},{8,0},{16,24},{24,16},{1,9},{9,1},{17,25},{25,17},{2,10},{10... | collective-permute-start | bytes 393224 | tf_op jit(solution)/shard_map/ppermute | solution.py:19
  46.8 7.5 %collective-permute-start.13 = (f32[128,256]{1,0:T(8,128)S(1)}, f32[128,256]{1,0:T(8,128)S(1)}, u32[]{:S(2)}, u32[]{:S(2)}) collective-permute-start(f32[128,256]{1,0:T(8,128)S(1)} %sketch.5), channel_id=1, source_target_pairs={{0,8},{8,0},{16,24},{24,16},{1,9},{9,1},{17,25},{25,17},{2,10},{10... | collective-permute-start | bytes 393224 | tf_op jit(solution)/shard_map/ppermute | solution.py:19
  50.7 8.4 %collective-permute-start.15 = (f32[128,256]{1,0:T(8,128)S(1)}, f32[128,256]{1,0:T(8,128)S(1)}, u32[]{:S(2)}, u32[]{:S(2)}) collective-permute-start(f32[128,256]{1,0:T(8,128)S(1)} %add.21), channel_id=1, source_target_pairs={{0,16},{8,24},{16,0},{24,8},{1,17},{9,25},{17,1},{25,9},{2,18},{10... | collective-permute-start | bytes 393224 | tf_op jit(solution)/shard_map/ppermute | solution.py:19
  59.6 4.1 %collective-permute-start.16 = (f32[80,128]{1,0:T(8,128)S(1)}, f32[80,128]{1,0:T(8,128)S(1)}, u32[]{:S(2)}, u32[]{:S(2)}) collective-permute-start(f32[80,128]{1,0:T(8,128)S(1)} %get-tuple-element.12.refs_0_), channel_id=1, source_target_pairs={{0,8},{8,0},{16,24},{24,16},{1,9},{9,1},{17,25},{25,17},{2,10},{10... | collective-permute-start | bytes 122888 | tf_op jit(solution)/shard_map/ppermute | solution.py:19
  60.3 5.4 %collective-permute-start.23 = (f32[128,128]{1,0:T(8,128)S(1)}, f32[128,128]{1,0:T(8,128)S(1)}, u32[]{:S(2)}, u32[]{:S(2)}) collective-permute-start(f32[128,128]{1,0:T(8,128)S(1)} %get-tuple-element.15), channel_id=1, source_target_pairs={{0,8},{8,0},{16,24},{24,16},{1,9},{9,1},{17,25},{25,17},{2,10},{10... | collective-permute-start | bytes 196616 | tf_op jit(solution)/shard_map/ppermute | solution.py:19
  61.7 5.3 %collective-permute-start.17 = (f32[80,128]{1,0:T(8,128)S(1)}, f32[80,128]{1,0:T(8,128)S(1)}, u32[]{:S(2)}, u32[]{:S(2)}) collective-permute-start(f32[80,128]{1,0:T(8,128)S(1)} %get-tuple-element.12.refs_0_), channel_id=1, source_target_pairs={{0,16},{8,24},{16,0},{24,8},{1,17},{9,25},{17,1},{25,9},{2,18},{10... | collective-permute-start | bytes 122888 | tf_op jit(solution)/shard_map/ppermute | solution.py:19
  63.7 4.9 %collective-permute-start.18 = (f32[80,128]{1,0:T(8,128)S(1)}, f32[80,128]{1,0:T(8,128)S(1)}, u32[]{:S(2)}, u32[]{:S(2)}) collective-permute-start(f32[80,128]{1,0:T(8,128)S(1)} %collective-permute-done.16.refs_1_), channel_id=1, source_target_pairs={{0,16},{8,24},{16,0},{24,8},{1,17},{9,25},{17,1},{25,9},{2,18},{10... | collective-permute-start | bytes 122888 | tf_op jit(solution)/shard_map/ppermute | solution.py:19
  68.8 17.3 %collective-permute-start.24 = (f32[128,128]{1,0:T(8,128)S(1)}, f32[128,128]{1,0:T(8,128)S(1)}, u32[]{:S(2)}, u32[]{:S(2)}) collective-permute-start(f32[128,128]{1,0:T(8,128)S(1)} %pad_maximum_fusion), channel_id=1, source_target_pairs={{0,16},{8,24},{16,0},{24,8},{1,17},{9,25},{17,1},{25,9},{2,18},{10... | collective-permute-start | bytes 196616 | tf_op jit(solution)/shard_map/ppermute | solution.py:19
  70.7 4.1 %collective-permute-start.20 = (f32[80,128]{1,0:T(8,128)S(1)}, f32[80,128]{1,0:T(8,128)S(1)}, u32[]{:S(2)}, u32[]{:S(2)}) collective-permute-start(f32[80,128]{1,0:T(8,128)S(1)} %add.25.refs_5_), channel_id=1, source_target_pairs={{0,2},{1,3},{2,0},{3,1},{4,6},{5,7},{6,4},{7,5},{8,10},{9,11},{10,... | collective-permute-start | bytes 122888 | tf_op jit(solution)/shard_map/ppermute | solution.py:19
  71.3 4.0 %collective-permute-start.21 = (f32[80,128]{1,0:T(8,128)S(1)}, f32[80,128]{1,0:T(8,128)S(1)}, u32[]{:S(2)}, u32[]{:S(2)}) collective-permute-start(f32[80,128]{1,0:T(8,128)S(1)} %add.25.refs_5_), channel_id=1, source_target_pairs={{0,4},{1,5},{2,6},{3,7},{4,0},{5,1},{6,2},{7,3},{8,12},{9,13},{10,... | collective-permute-start | bytes 122888 | tf_op jit(solution)/shard_map/ppermute | solution.py:19
  72.8 4.9 %collective-permute-start.22 = (f32[80,128]{1,0:T(8,128)S(1)}, f32[80,128]{1,0:T(8,128)S(1)}, u32[]{:S(2)}, u32[]{:S(2)}) collective-permute-start(f32[80,128]{1,0:T(8,128)S(1)} %add.25.refs_5_), channel_id=1, source_target_pairs={{0,6},{1,7},{2,4},{3,5},{4,2},{5,3},{6,0},{7,1},{8,14},{9,15},{10,... | collective-permute-start | bytes 122888 | tf_op jit(solution)/shard_map/ppermute | solution.py:19
  (6 other events, 13.3 us)
